TPU v7x, 512 devices: a whole 4x8x8 slice. The times are simulated.
512 devices in a mesh: tm: 64 (over x, y, core), row: 8 (over z).
Axes of the slice: x: 4, y: 8, z: 8, core: 2. Of those that a mesh axis runs over, the one named last changes fastest.
Arguments:
- trans: bfloat16 [128, 1024, 1024], P('tm', 'row'), may hold values from -0.3 to 0.9
- offset: bfloat16 [128, 1024], P('tm', 'row'), may hold values from -6 to 6
- spread: bfloat16 [128, 1024, 1024], P('tm', 'row'), may hold values from -0.3 to 2.3, as said below
Outputs:
- trans_out: bfloat16 [128, 1024, 1024], P('tm', 'row')
- offset_out: bfloat16 [128, 1024], P('tm', 'row')
- spread_out: bfloat16 [128, 1024, 1024], P('tm', 'row')
Inputs may be any that keep to these rules, and one draw needn't show every extreme that they name: `spread`: each block's matrix is symmetric.
All inputs are finite; a program needn't handle non-finite values.
Results may differ from a plain program's by a relative error of at most 0.0056.
Values may be sent and summed in bfloat16 or wider, within the bound.
No kernel may reach another device: no remote copies, remote signals or barrier semaphores. Data moves between devices by JAX's collectives and lax.ppermute only.
A program may use at most 64 MiB of HBM per device.

v0:
```python
import jax
import jax.numpy as jnp
from jax import lax
from jax.experimental import pallas as pl
from jax.experimental.pallas import tpu as pltpu
from jax.sharding import PartitionSpec as P


BF16, F32 = jnp.bfloat16, jnp.float32
HBM = pl.BlockSpec(memory_space=pl.ANY)
VMEM = pl.BlockSpec(memory_space=pltpu.VMEM)
GRANT = 12 * 2**20
TAIL = 16


def hop(block, axis, distance):
    size = lax.axis_size(axis)
    return lax.ppermute(block, axis, [(i, (i + distance) % size) for i in range(size)])


def nn(a, b):
    return lax.dot_general(a, b, (((1,), (0,)), ((), ())), preferred_element_type=F32)


def nt(a, b):
    return lax.dot_general(a, b, (((1,), (1,)), ((), ())), preferred_element_type=F32)


def kept(shape, kind):
    return pltpu.VMEM(shape, kind)


def near(array):
    return pltpu.with_memory_space_constraint(array, pltpu.VMEM)


def call(body, ins, outs, flops, after=()):
    count = len(ins)

    def run(*refs):
        body(*refs[:count], *refs[count + len(after) :])

    return pl.pallas_call(
        run,
        in_specs=[VMEM] * count + [HBM] * len(after),
        out_specs=tuple(VMEM for _ in outs),
        out_shape=tuple(outs),
        cost_estimate=pl.CostEstimate(flops=flops, bytes_accessed=2**20, transcendentals=0),
        compiler_params=pltpu.CompilerParams(vmem_limit_bytes=GRANT),
    )(*[near(array) for array in ins], *after)


def part(array, picked, shape):
    def copy(ref, out):
        out[...] = ref[picked]

    return call(copy, [array], [kept(shape, BF16)], 1000)[0]


def slot(offset, count):
    return lax.rem(lax.axis_index("row") + (offset + count), count)


def join(pieces, whole, count):
    rows = whole.shape[0] // count
    for offset, panel in pieces:
        start = pl.multiple_of(slot(offset, count) * rows, rows)
        whole[pl.ds(start, rows), :] = panel


def unpack(pieces, whole, count):
    size = whole.shape[0] // count
    half = count // 2
    whole[...] = jnp.zeros(whole.shape, BF16)
    for offset, (ref, base) in pieces:
        s = slot(offset, count)
        row = pl.multiple_of(s * size, size)
        for k in range(half):
            column = pl.multiple_of(lax.rem(s + k, count) * size, size)
            whole[pl.ds(row, size), pl.ds(column, size)] = ref[base + k * size : base + (k + 1) * size, :]
        a = lax.rem(s, half)
        row = pl.multiple_of(a * size + lax.div(s, half) * (size // 2), size // 2)
        column = pl.multiple_of((a + half) * size, size)
        start = base + half * size
        whole[pl.ds(row, size // 2), pl.ds(column, size)] = ref[start : start + size // 2, :]


def by_symmetric(a, whole):
    return nn(a, whole) + nt(a, whole)


def two_rows(row):
    high = row.astype(BF16).astype(F32)
    index = lax.broadcasted_iota(jnp.int32, (TAIL, row.shape[1]), 0)
    return jnp.where(index == 0, high, jnp.where(index == 1, row - high, 0.0)).astype(BF16)


def one_row(tile):
    return tile[0:1].astype(F32) + tile[1:2].astype(F32)


def on_device(trans, offset, spread):
    count = lax.axis_size("row")
    _, rows, size = trans.shape
    half = count // 2
    packed = half * rows + rows // 2
    product = 2 * rows * size * size
    panel = kept((rows, size), BF16)
    wide = kept((rows, size), F32)
    pair = kept((2 * rows, size), BF16)
    whole = kept((size, size), BF16)
    short = kept((rows + TAIL, size), BF16)
    long = kept((2 * rows + TAIL, size), BF16)
    line = kept((8, rows), F32)

    def gather(block, parts):
        fore, back = [block], [block]
        for _ in range(half - 1):
            fore.append(hop(fore[-1], "row", 1))
            back.append(hop(back[-1], "row", -1))
        halves = parts[0](fore[-1]), parts[1](back[-1])
        even = hop(halves[0], "row", 1)
        odd = hop(halves[1], "row", -1)
        arrays = [block] + fore[1:] + back[1:]
        offsets = [0] + [-k for k in range(1, half)] + list(range(1, half))
        return arrays, offsets, even, odd, halves

    e_arrays, offsets, e_even_last, e_odd_last, _ = gather(
        trans, (lambda x: part(x, 0, (rows, size)), lambda x: part(x, 1, (rows, size)))
    )
    b1_in = hop(part(trans, 1, (rows, size)), "tm", 1)
    n = len(e_arrays)

    def first(*refs):
        last, out, joined = refs[n], refs[n + 1], refs[n + 2]
        join([(way, ref[1]) for way, ref in zip(offsets, refs)] + [(half, last[...])], joined, count)
        out[...] = nn(refs[0][0], joined[...]).astype(BF16)

    x1, e_odd = call(first, e_arrays + [e_odd_last], [panel, whole], product)
    x1_in = hop(x1, "tm", 1)

    def evens(*refs):
        last, joined = refs[n], refs[n + 1]
        join([(way, ref[0]) for way, ref in zip(offsets, refs)] + [(half, last[...])], joined, count)

    (e_even,) = call(evens, e_arrays + [e_even_last], [whole], 1000)

    def pack(l_ref, g_ref, out):
        z = lax.axis_index("row")
        for b in range(2):
            base = b * (packed + TAIL)
            for k in range(half):
                c = lax.rem(z + k, count)
                tile = l_ref[b, :, pl.ds(pl.multiple_of(c * rows, rows), rows)]
                out[base + k * rows : base + (k + 1) * rows, :] = tile * jnp.asarray(0.5, BF16) if k == 0 else tile
            c = lax.rem(z + half, count)
            tile = l_ref[b, :, pl.ds(pl.multiple_of(c * rows, rows), rows)].astype(F32)
            lower = tile.T[rows // 2 :]
            out[base + half * rows : base + packed, :] = jnp.where(z < half, tile[: rows // 2], lower).astype(BF16)
        g = g_ref[...].astype(F32)
        index = lax.broadcasted_iota(jnp.int32, (TAIL, rows), 0)
        tile = jnp.where(index == 0, g[0:1], jnp.where(index == 1, g[1:2], 0.0))
        out[packed : packed + TAIL, :] = tile.astype(BF16)

    (sent,) = call(
        pack, [spread, offset], [kept((2 * packed + TAIL, rows), BF16)], 1000
    )
    l_arrays, _, l_even_last, l_odd_last, _ = gather(
        sent, (
            lambda x: part(x, slice(0, packed + TAIL), (packed + TAIL, rows)),
            lambda x: part(x, slice(packed + TAIL, 2 * packed + TAIL), (packed, rows)),
        ),
    )

    def second(x1_ref, b1_ref, even, odd, x3_ref, b3_ref, x2_ref):
        past = lax.axis_index("tm") < 1
        one = jnp.concatenate([x1_ref[...], b1_ref[...]], axis=0)
        two = nn(one, even[...]).astype(BF16)
        three = nn(two, odd[...])
        three = jnp.where(past, one.astype(F32), three).astype(BF16)
        x3_ref[...] = three[:rows]
        b3_ref[...] = three[rows:]
        x2_ref[...] = two

    x3, b3, x2 = call(second, [x1_in, b1_in, e_even, e_odd], [panel, panel, pair], 4 * product)
    b3_in = hop(b3, "tm", 1)

    def third(b3_ref, even, b4_ref):
        own = b3_ref[...]
        past = lax.axis_index("tm") < 2
        b4_ref[...] = jnp.where(past, own.astype(F32), nn(own, even[...])).astype(BF16)


    def fourth(*refs):
        last, b3_ref, m_ref, joined, g_ref = refs[n : n + 5]
        unpack([(way, (ref, 0)) for way, ref in zip(offsets, refs)] + [(half, (last, 0))], joined, count)
        for way, ref in list(zip(offsets, refs)) + [(half, last)]:
            column = pl.multiple_of(slot(way, count) * rows, rows)
            g_ref[:, pl.ds(column, rows)] = ref[packed : packed + TAIL, :]
        past = lax.axis_index("tm") < 2
        own = b3_ref[...]
        m_ref[:rows, :] = jnp.where(past, 0.0, by_symmetric(own, joined[...])).astype(BF16)
        m_ref[rows:, :] = jnp.zeros((TAIL, size), BF16)
        m_ref[rows:, :rows] = two_rows(jnp.where(past, 0.0, nt(g_ref[...], own)[0:1]))

    v, l_even, g_all = call(
        fourth, l_arrays + [l_even_last, b3_in], [short, whole, kept((TAIL, size), BF16)], 2 * product
    )
    v_in = hop(v, "tm", -1)
    (b4,) = call(third, [b3_in, e_even], [panel], product, after=(v,))
    b4_in = hop(b4, "tm", -2)

    def fifth(*refs):
        last, x1_ref, b1_ref, x2_ref, x3_ref, even, l_ev, g_ref, own = refs[n : n + 9]
        m_ref, near_ref, far_ref, head_ref, row_ref, l_od = refs[n + 9 :]
        unpack([(way, (ref, packed + TAIL)) for way, ref in zip(offsets, refs)] + [(half, (last, 0))], l_od, count)
        past = lax.axis_index("tm") < 1
        one = jnp.concatenate([x1_ref[...], b1_ref[...]], axis=0)
        two = x2_ref[...]
        close = by_symmetric(one, l_ev[...])
        far = by_symmetric(jnp.concatenate([two, own[0]], axis=0), l_od[...])
        w = close[:rows] + nt(far[:rows].astype(BF16), even[...])
        near_ref[...] = close[rows:]
        far_ref[...] = far[rows : 2 * rows]
        head_ref[...] = far[2 * rows :]
        g = g_ref[...]
        row = nt(g, one)[0:1] + nt(g, two)[1:2]
        index = lax.broadcasted_iota(jnp.int32, (8, rows), 0)
        row_ref[...] = jnp.where(index == 0, row[:, rows:], nt(g, own[0])[1:2])
        m_ref[:rows, :] = jnp.where(past, 0.0, w).astype(BF16)
        m_ref[rows : 2 * rows, :] = x3_ref[...]
        m_ref[2 * rows :, :] = jnp.zeros((TAIL, size), BF16)
        m_ref[2 * rows :, :rows] = two_rows(jnp.where(past, 0.0, row[:, :rows]))

    w, close, far, head, line_, _ = call(
        fifth,
        l_arrays + [l_odd_last, x1_in, b1_in, x2, x3, e_even, l_even, g_all, trans],
        [long, wide, wide, wide, line, whole],
        11 * product,
        after=(v, b4),
    )
    w_in = hop(w, "tm", -1)

    def sixth(v_ref, close_ref, far_ref, line_ref, even, odd, m_ref):
        past = lax.axis_index("tm") < 1
        behind = far_ref[...] + nt(v_ref[:rows, :], odd[...])
        u = close_ref[...] + nt(behind.astype(BF16), even[...])
        row = line_ref[0:1] + one_row(v_ref[rows:, :rows])
        m_ref[:rows, :] = jnp.where(past, 0.0, u).astype(BF16)
        m_ref[rows:, :] = jnp.zeros((TAIL, size), BF16)
        m_ref[rows:, :rows] = two_rows(jnp.where(past, 0.0, row))

    (u,) = call(sixth, [v_in, close, far, line_, e_even, e_odd], [short], 2 * product)
    u_in = hop(u, "tm", -1)

    def seventh(w_ref, head_ref, even, odd, l_own, out):
        inner = head_ref[...] + nt(w_ref[:rows, :], odd[...])
        out[...] = (nt(inner.astype(BF16), even[...]) + l_own[0].astype(F32)).astype(BF16)

    (l_first,) = call(seventh, [w_in, head, e_even, e_odd, spread], [panel], 2 * product, after=(u,))

    def eighth(w_ref, u_ref, b4_ref, line_ref, odd, l_ref, l_own, g_own, e_out, g_out, l_out):
        l_out[1] = (nt(u_ref[:rows, :], odd[...]) + l_own[1].astype(F32)).astype(BF16)
        l_out[0] = l_ref[...]
        e_out[0] = w_ref[rows : 2 * rows, :]
        e_out[1] = b4_ref[...]
        g = g_own[...].astype(F32)
        g_out[0:1, :] = (g[0:1] + line_ref[1:2] + one_row(w_ref[2 * rows :, :rows])).astype(BF16)
        g_out[1:2, :] = (g[1:2] + one_row(u_ref[rows:, :rows])).astype(BF16)

    return call(
        eighth,
        [w_in, u_in, b4_in, line_, e_odd, l_first, spread, offset],
        [jax.ShapeDtypeStruct(x.shape, BF16) for x in (trans, offset, spread)],
        product,
    )


def solution(mesh):
    placed = (P("tm", "row", None), P("tm", "row"), P("tm", "row", None))
    return jax.shard_map(on_device, mesh=mesh, in_specs=placed, out_specs=placed, check_vma=False)
```

profile of v0, /device:TPU:56, one launch (start us, length us, event | category | flops | bytes accessed | tf_op | source)
XLA Modules:
  0.0 135.7 jit_solution(13394367587959700407)
XLA Ops:
  0.6 0.0 copy-start.1
  0.6 11.1 %collective-permute-start.10 = (bf16[2,128,1024]{2,1,0:T(8,128)(2,1)}, bf16[2,128,1024]{2,1,0:T(8,128)(2,1)S(1)}, u32[]{:S(2)}, u32[]{:S(2)}) collective-permute-start(bf16[2,128,1024]{2,1,0:T(8,128)(2,1)} %refs_15_.1), channel_id=1, source_target_pairs={{0,7},{1,0},{2,1},{3,2},{4,3},{5,4},{6,5},{7,6},{8,15},{9,8},{10,9... | collective-permute-start | bytes 1572872 | tf_op jit(solution)/shard_map/ppermute | solution.py:18
  11.7 1.9 %collective-permute-start.7 = (bf16[2,128,1024]{2,1,0:T(8,128)(2,1)}, bf16[2,128,1024]{2,1,0:T(8,128)(2,1)S(1)}, u32[]{:S(2)}, u32[]{:S(2)}) collective-permute-start(bf16[2,128,1024]{2,1,0:T(8,128)(2,1)} %refs_15_.1), channel_id=1, source_target_pairs={{0,1},{1,2},{2,3},{3,4},{4,5},{5,6},{6,7},{7,0},{8,9},{9,10},{10,1... | collective-permute-start | bytes 1572872 | tf_op jit(solution)/shard_map/ppermute | solution.py:18
  13.7 9.5 %collective-permute-done.10.refs_4_ = bf16[2,128,1024]{2,1,0:T(8,128)(2,1)S(1)} collective-permute-done((bf16[2,128,1024]{2,1,0:T(8,128)(2,1)}, bf16[2,128,1024]{2,1,0:T(8,128)(2,1)S(1)}, u32[]{:S(2)}, u32[]{:S(2)}) %collective-permute-start.10) | collective-permute-done | bytes 524320 | tf_op jit(solution)/shard_map/ppermute | solution.py:18
  23.2 5.5 %collective-permute-start.11 = (bf16[2,128,1024]{2,1,0:T(8,128)(2,1)S(1)}, bf16[2,128,1024]{2,1,0:T(8,128)(2,1)S(1)}, u32[]{:S(2)}, u32[]{:S(2)}) collective-permute-start(bf16[2,128,1024]{2,1,0:T(8,128)(2,1)S(1)} %collective-permute-done.10.refs_4_), channel_id=1, source_target_pairs={{0,7},{1,0},{2,1},{3,2},{4,3},{5,4},{6,5},{7,6},{8,15},{9,8},{10,9... | collective-permute-start | bytes 1572872 | tf_op jit(solution)/shard_map/ppermute | solution.py:18
  28.7 0.0 collective-permute-done.7.refs_1_
  28.7 1.9 %collective-permute-start.8 = (bf16[2,128,1024]{2,1,0:T(8,128)(2,1)S(1)}, bf16[2,128,1024]{2,1,0:T(8,128)(2,1)S(1)}, u32[]{:S(2)}, u32[]{:S(2)}) collective-permute-start(bf16[2,128,1024]{2,1,0:T(8,128)(2,1)S(1)} %collective-permute-done.7.refs_1_), channel_id=1, source_target_pairs={{0,1},{1,2},{2,3},{3,4},{4,5},{5,6},{6,7},{7,0},{8,9},{9,10},{10,1... | collective-permute-start | bytes 1572872 | tf_op jit(solution)/shard_map/ppermute | solution.py:18
  30.6 8.4 %collective-permute-done.11.refs_5_ = bf16[2,128,1024]{2,1,0:T(8,128)(2,1)S(1)} collective-permute-done((bf16[2,128,1024]{2,1,0:T(8,128)(2,1)S(1)}, bf16[2,128,1024]{2,1,0:T(8,128)(2,1)S(1)}, u32[]{:S(2)}, u32[]{:S(2)}) %collective-permute-start.11) | collective-permute-done | bytes 524320 | tf_op jit(solution)/shard_map/ppermute | solution.py:18
  39.0 5.6 %collective-permute-start.12 = (bf16[2,128,1024]{2,1,0:T(8,128)(2,1)S(1)}, bf16[2,128,1024]{2,1,0:T(8,128)(2,1)S(1)}, u32[]{:S(2)}, u32[]{:S(2)}) collective-permute-start(bf16[2,128,1024]{2,1,0:T(8,128)(2,1)S(1)} %collective-permute-done.11.refs_5_), channel_id=1, source_target_pairs={{0,7},{1,0},{2,1},{3,2},{4,3},{5,4},{6,5},{7,6},{8,15},{9,8},{10,9... | collective-permute-start | bytes 1572872 | tf_op jit(solution)/shard_map/ppermute | solution.py:18
  44.6 1.9 %collective-permute-start.9 = (bf16[2,128,1024]{2,1,0:T(8,128)(2,1)S(1)}, bf16[2,128,1024]{2,1,0:T(8,128)(2,1)S(1)}, u32[]{:S(2)}, u32[]{:S(2)}) collective-permute-start(bf16[2,128,1024]{2,1,0:T(8,128)(2,1)S(1)} %collective-permute-done.8.refs_2_), channel_id=1, source_target_pairs={{0,1},{1,2},{2,3},{3,4},{4,5},{5,6},{6,7},{7,0},{8,9},{9,10},{10,1... | collective-permute-start | bytes 1572872 | tf_op jit(solution)/shard_map/ppermute | solution.py:18
  46.5 0.0 copy-start.2
  46.6 1.0 copy-done.2
  47.6 0.7 copy-done.4
  48.2 0.2 shard_map.58.refs_0_
  48.4 1.9 %collective-permute-start = (bf16[1168,128]{1,0:T(8,128)(2,1)S(1)}, bf16[1168,128]{1,0:T(8,128)(2,1)S(1)}, u32[]{:S(2)}, u32[]{:S(2)}) collective-permute-start(bf16[1168,128]{1,0:T(8,128)(2,1)S(1)} %shard_map.58.refs_0_), channel_id=1, source_target_pairs={{0,1},{1,2},{2,3},{3,4},{4,5},{5,6},{6,7},{7,0},{8,9},{9,10},{10,1... | collective-permute-start | bytes 897032 | tf_op jit(solution)/shard_map/ppermute | solution.py:18
  50.3 5.1 %collective-permute-start.3 = (bf16[1168,128]{1,0:T(8,128)(2,1)S(1)}, bf16[1168,128]{1,0:T(8,128)(2,1)S(1)}, u32[]{:S(2)}, u32[]{:S(2)}) collective-permute-start(bf16[1168,128]{1,0:T(8,128)(2,1)S(1)} %shard_map.58.refs_0_), channel_id=1, source_target_pairs={{0,7},{1,0},{2,1},{3,2},{4,3},{5,4},{6,5},{7,6},{8,15},{9,8},{10,9... | collective-permute-start | bytes 897032 | tf_op jit(solution)/shard_map/ppermute | solution.py:18
  55.5 5.1 %collective-permute-start.13 = (bf16[128,1024]{1,0:T(8,128)(2,1)S(1)}, bf16[128,1024]{1,0:T(8,128)(2,1)S(1)}, u32[]{:S(2)}, u32[]{:S(2)}) collective-permute-start(bf16[128,1024]{1,0:T(8,128)(2,1)S(1)} %shard_map.60), channel_id=1, source_target_pairs={{0,7},{1,0},{2,1},{3,2},{4,3},{5,4},{6,5},{7,6},{8,15},{9,8},{10,9... | collective-permute-start | bytes 786440 | tf_op jit(solution)/shard_map/ppermute | solution.py:18
  60.6 5.2 %collective-permute-done.refs_1_ = bf16[1168,128]{1,0:T(8,128)(2,1)S(1)} collective-permute-done((bf16[1168,128]{1,0:T(8,128)(2,1)S(1)}, bf16[1168,128]{1,0:T(8,128)(2,1)S(1)}, u32[]{:S(2)}, u32[]{:S(2)}) %collective-permute-start) | collective-permute-done | bytes 299040 | tf_op jit(solution)/shard_map/ppermute | solution.py:18
  65.8 1.9 %collective-permute-start.1 = (bf16[1168,128]{1,0:T(8,128)(2,1)S(1)}, bf16[1168,128]{1,0:T(8,128)(2,1)S(1)}, u32[]{:S(2)}, u32[]{:S(2)}) collective-permute-start(bf16[1168,128]{1,0:T(8,128)(2,1)S(1)} %collective-permute-done.refs_1_), channel_id=1, source_target_pairs={{0,1},{1,2},{2,3},{3,4},{4,5},{5,6},{6,7},{7,0},{8,9},{9,10},{10,1... | collective-permute-start | bytes 897032 | tf_op jit(solution)/shard_map/ppermute | solution.py:18
  67.7 5.1 %collective-permute-start.4 = (bf16[1168,128]{1,0:T(8,128)(2,1)S(1)}, bf16[1168,128]{1,0:T(8,128)(2,1)S(1)}, u32[]{:S(2)}, u32[]{:S(2)}) collective-permute-start(bf16[1168,128]{1,0:T(8,128)(2,1)S(1)} %collective-permute-done.3.refs_4_), channel_id=1, source_target_pairs={{0,7},{1,0},{2,1},{3,2},{4,3},{5,4},{6,5},{7,6},{8,15},{9,8},{10,9... | collective-permute-start | bytes 897032 | tf_op jit(solution)/shard_map/ppermute | solution.py:18
  72.9 0.0 copy-start
  72.9 1.0 copy-done
  73.9 1.9 %collective-permute-start.15 = (bf16[128,1024]{1,0:T(8,128)(2,1)S(1)}, bf16[128,1024]{1,0:T(8,128)(2,1)S(1)}, u32[]{:S(2)}, u32[]{:S(2)}) collective-permute-start(bf16[128,1024]{1,0:T(8,128)(2,1)S(1)} %shard_map.62), channel_id=1, source_target_pairs={{0,8},{8,16},{16,24},{24,32},{32,40},{40,48},{48,56},{56,64},{64,7... | collective-permute-start | bytes 786440 | tf_op jit(solution)/shard_map/ppermute | solution.py:18
  75.9 1.9 %collective-permute-start.16 = (bf16[128,1024]{1,0:T(8,128)(2,1)S(1)}, bf16[128,1024]{1,0:T(8,128)(2,1)S(1)}, u32[]{:S(2)}, u32[]{:S(2)}) collective-permute-start(bf16[128,1024]{1,0:T(8,128)(2,1)S(1)} %shard_map.63), channel_id=1, source_target_pairs={{0,1},{1,2},{2,3},{3,4},{4,5},{5,6},{6,7},{7,0},{8,9},{9,10},{10,1... | collective-permute-start | bytes 786440 | tf_op jit(solution)/shard_map/ppermute | solution.py:18
  77.8 0.6 shard_map.61
  78.4 2.7 %collective-permute-start.14 = (bf16[128,1024]{1,0:T(8,128)(2,1)S(1)}, bf16[128,1024]{1,0:T(8,128)(2,1)S(1)}, u32[]{:S(2)}, u32[]{:S(2)}) collective-permute-start(bf16[128,1024]{1,0:T(8,128)(2,1)S(1)} %get-tuple-element.16), channel_id=1, source_target_pairs={{0,8},{8,16},{16,24},{24,32},{32,40},{40,48},{48,56},{56,64},{64,7... | collective-permute-start | bytes 786440 | tf_op jit(solution)/shard_map/ppermute | solution.py:18
  81.2 1.9 %collective-permute-start.2 = (bf16[1168,128]{1,0:T(8,128)(2,1)S(1)}, bf16[1168,128]{1,0:T(8,128)(2,1)S(1)}, u32[]{:S(2)}, u32[]{:S(2)}) collective-permute-start(bf16[1168,128]{1,0:T(8,128)(2,1)S(1)} %collective-permute-done.1.refs_2_), channel_id=1, source_target_pairs={{0,1},{1,2},{2,3},{3,4},{4,5},{5,6},{6,7},{7,0},{8,9},{9,10},{10,1... | collective-permute-start | bytes 897032 | tf_op jit(solution)/shard_map/ppermute | solution.py:18
  83.1 5.1 %collective-permute-start.5 = (bf16[1168,128]{1,0:T(8,128)(2,1)S(1)}, bf16[1168,128]{1,0:T(8,128)(2,1)S(1)}, u32[]{:S(2)}, u32[]{:S(2)}) collective-permute-start(bf16[1168,128]{1,0:T(8,128)(2,1)S(1)} %collective-permute-done.4.refs_5_), channel_id=1, source_target_pairs={{0,7},{1,0},{2,1},{3,2},{4,3},{5,4},{6,5},{7,6},{8,15},{9,8},{10,9... | collective-permute-start | bytes 897032 | tf_op jit(solution)/shard_map/ppermute | solution.py:18
  88.3 0.2 shard_map.64.refs_2_.refs_1_.refs_12_.refs_4_
  88.4 1.3 shard_map.65
  89.7 1.9 %collective-permute-start.18 = (bf16[128,1024]{1,0:T(8,128)(2,1)S(1)}, bf16[128,1024]{1,0:T(8,128)(2,1)S(1)}, u32[]{:S(2)}, u32[]{:S(2)}) collective-permute-start(bf16[128,1024]{1,0:T(8,128)(2,1)S(1)} %get-tuple-element.20), channel_id=1, source_target_pairs={{0,8},{8,16},{16,24},{24,32},{32,40},{40,48},{48,56},{56,64},{64,7... | collective-permute-start | bytes 786440 | tf_op jit(solution)/shard_map/ppermute | solution.py:18
  91.6 2.8 %collective-permute-done.2.refs_0_.refs_3_ = bf16[1168,128]{1,0:T(8,128)(2,1)S(1)} collective-permute-done((bf16[1168,128]{1,0:T(8,128)(2,1)S(1)}, bf16[1168,128]{1,0:T(8,128)(2,1)S(1)}, u32[]{:S(2)}, u32[]{:S(2)}) %collective-permute-start.2) | collective-permute-done | bytes 299040 | tf_op jit(solution)/shard_map/ppermute | solution.py:18
  94.4 1.9 %collective-permute-start.17 = (bf16[592,128]{1,0:T(8,128)(2,1)S(1)}, bf16[592,128]{1,0:T(8,128)(2,1)S(1)}, u32[]{:S(2)}, u32[]{:S(2)}) collective-permute-start(bf16[592,128]{1,0:T(8,128)(2,1)S(1)} %shard_map.66), channel_id=1, source_target_pairs={{0,1},{1,2},{2,3},{3,4},{4,5},{5,6},{6,7},{7,0},{8,9},{9,10},{10,1... | collective-permute-start | bytes 454664 | tf_op jit(solution)/shard_map/ppermute | solution.py:18
  96.4 5.1 %collective-permute-start.6 = (bf16[576,128]{1,0:T(8,128)(2,1)S(1)}, bf16[576,128]{1,0:T(8,128)(2,1)S(1)}, u32[]{:S(2)}, u32[]{:S(2)}) collective-permute-start(bf16[576,128]{1,0:T(8,128)(2,1)S(1)} %shard_map.59), channel_id=1, source_target_pairs={{0,7},{1,0},{2,1},{3,2},{4,3},{5,4},{6,5},{7,6},{8,15},{9,8},{10,9... | collective-permute-start | bytes 442376 | tf_op jit(solution)/shard_map/ppermute | solution.py:18
  101.5 1.8 %collective-permute-done.17.refs_7_ = bf16[592,128]{1,0:T(8,128)(2,1)S(1)} collective-permute-done((bf16[592,128]{1,0:T(8,128)(2,1)S(1)}, bf16[592,128]{1,0:T(8,128)(2,1)S(1)}, u32[]{:S(2)}, u32[]{:S(2)}) %collective-permute-start.17) | collective-permute-done | bytes 151584 | tf_op jit(solution)/shard_map/ppermute | solution.py:18
  103.3 1.6 %shard_map.67 = (bf16[144,1024]{1,0:T(8,128)(2,1)S(1)}, bf16[1024,1024]{1,0:T(8,128)(2,1)S(1)}, bf16[16,1024]{1,0:T(8,128)(2,1)S(1)}) custom-call(bf16[1168,128]{1,0:T(8,128)(2,1)S(1)} %shard_map.58.refs_0_, bf16[1168,128]{1,0:T(8,128)(2,1)S(1)} %collective-permute-done.refs_1_, bf16[1168,128]{1,0:T(8,128)(2,1)S(1)} %collective-permute-done.1.refs_2_, ...), custom_call_target="tpu_custom_call" | custom-call | flops 536870912 | bytes 1048576 | tf_op jit(solution)/shard_map/pallas_call | solution.py:43
  104.9 1.9 %collective-permute-start.20 = (bf16[144,1024]{1,0:T(8,128)(2,1)S(1)}, bf16[144,1024]{1,0:T(8,128)(2,1)S(1)}, u32[]{:S(2)}, u32[]{:S(2)}) collective-permute-start(bf16[144,1024]{1,0:T(8,128)(2,1)S(1)} %get-tuple-element.23.refs_2_.refs_16_), channel_id=1, source_target_pairs={{0,504},{8,0},{16,8},{24,16},{32,24},{40,32},{48,40},{56,48},{64,5... | collective-permute-start | bytes 884744 | tf_op jit(solution)/shard_map/ppermute | solution.py:18
  106.8 0.5 shard_map.68.refs_17_
  107.3 4.3 %shard_map.69 = (bf16[272,1024]{1,0:T(8,128)(2,1)S(1)}, f32[128,1024]{1,0:T(8,128)S(1)}, f32[128,1024]{1,0:T(8,128)S(1)}, f32[128,1024]{1,0:T(8,128)S(1)}, f32[8...) custom-call(bf16[1168,128]{1,0:T(8,128)(2,1)S(1)} %shard_map.58.refs_0_, bf16[1168,128]{1,0:T(8,128)(2,1)S(1)} %collective-permute-done.refs_1_, ...), custom_call_target="tpu_custom_call" | custom-call | flops 2952790016 | bytes 1048576 | tf_op jit(solution)/shard_map/pallas_call | solution.py:43
  111.6 3.3 %collective-permute-start.19 = (bf16[272,1024]{1,0:T(8,128)(2,1)S(1)}, bf16[272,1024]{1,0:T(8,128)(2,1)S(1)}, u32[]{:S(2)}, u32[]{:S(2)}) collective-permute-start(bf16[272,1024]{1,0:T(8,128)(2,1)S(1)} %get-tuple-element.24), channel_id=1, source_target_pairs={{0,504},{8,0},{16,8},{24,16},{32,24},{40,32},{48,40},{56,48},{64,5... | collective-permute-start | bytes 1671176 | tf_op jit(solution)/shard_map/ppermute | solution.py:18
  114.9 0.0 copy-start.3
  115.0 1.5 %shard_map.70.refs_5_ = bf16[144,1024]{1,0:T(8,128)(2,1)S(1)} custom-call(bf16[144,1024]{1,0:T(8,128)(2,1)S(1)} %collective-permute-done.20.refs_0_, f32[128,1024]{1,0:T(8,128)S(1)} %get-tuple-element.25.refs_1_, f32[128,1024]{1,0:T(8,128)S(1)} %get-tuple-element.26.refs_2_, f32[8,128]{1,0:T(8,128)S(1)} %get-tuple-element.27.refs_3_, ...), custom_call_target="tpu_custom_call" | custom-call | flops 536870912 | bytes 1048576 | tf_op jit(solution)/shard_map/pallas_call | solution.py:43
  116.5 1.9 %collective-permute-start.21 = (bf16[144,1024]{1,0:T(8,128)(2,1)S(1)}, bf16[144,1024]{1,0:T(8,128)(2,1)S(1)}, u32[]{:S(2)}, u32[]{:S(2)}) collective-permute-start(bf16[144,1024]{1,0:T(8,128)(2,1)S(1)} %shard_map.70.refs_5_), channel_id=1, source_target_pairs={{0,504},{8,0},{16,8},{24,16},{32,24},{40,32},{48,40},{56,48},{64,5... | collective-permute-start | bytes 884744 | tf_op jit(solution)/shard_map/ppermute | solution.py:18
  118.4 3.2 %collective-permute-start.22 = (bf16[128,1024]{1,0:T(8,128)(2,1)S(1)}, bf16[128,1024]{1,0:T(8,128)(2,1)S(1)}, u32[]{:S(2)}, u32[]{:S(2)}) collective-permute-start(bf16[128,1024]{1,0:T(8,128)(2,1)S(1)} %shard_map.68.refs_17_), channel_id=1, source_target_pairs={{0,496},{8,504},{16,0},{24,8},{32,16},{40,24},{48,32},{56,40},{64,... | collective-permute-start | bytes 786440 | tf_op jit(solution)/shard_map/ppermute | solution.py:18
  121.7 0.3 collective-permute-done.19.refs_0_
  122.0 1.5 %shard_map.71.refs_5_ = bf16[128,1024]{1,0:T(8,128)(2,1)S(1)} custom-call(bf16[272,1024]{1,0:T(8,128)(2,1)S(1)} %collective-permute-done.19.refs_0_, f32[128,1024]{1,0:T(8,128)S(1)} %get-tuple-element.28.refs_1_, bf16[1024,1024]{1,0:T(8,128)(2,1)S(1)} %shard_map.64.refs_2_.refs_1_.refs_12_.refs_4_, ...), custom_call_target="tpu_custom_call" | custom-call | flops 536870912 | bytes 1048576 | tf_op jit(solution)/shard_map/pallas_call | solution.py:43
  123.5 10.5 %collective-permute-done.22.refs_2_ = bf16[128,1024]{1,0:T(8,128)(2,1)S(1)} collective-permute-done((bf16[128,1024]{1,0:T(8,128)(2,1)S(1)}, bf16[128,1024]{1,0:T(8,128)(2,1)S(1)}, u32[]{:S(2)}, u32[]{:S(2)}) %collective-permute-start.22) | collective-permute-done | bytes 262176 | tf_op jit(solution)/shard_map/ppermute | solution.py:18
  134.0 1.7 %shard_map.72 = (bf16[2,128,1024]{2,1,0:T(8,128)(2,1)}, bf16[2,128]{1,0:T(2,128)(2,1)}, bf16[2,128,1024]{2,1,0:T(8,128)(2,1)}) custom-call(bf16[272,1024]{1,0:T(8,128)(2,1)S(1)} %collective-permute-done.19.refs_0_, bf16[144,1024]{1,0:T(8,128)(2,1)S(1)} %collective-permute-done.21.refs_1_, bf16[128,1024]{1,0:T(8,128)(2,1)S(1)} %collective-permute-done.22.refs_2_, ...), custom_call_target="tpu_custom_call" | custom-call | flops 268435456 | bytes 1048576 | tf_op jit(solution)/shard_map/pallas_call | solution.py:43
  (25 shorter events, 0.1 us)
Async XLA Ops:
  0.6 77.2 %copy-start.1 = (bf16[2,128,1024]{2,1,0:T(8,128)(2,1)S(1)}, bf16[2,128,1024]{2,1,0:T(8,128)(2,1)}, u32[]{:S(2)}) copy-start(bf16[2,128,1024]{2,1,0:T(8,128)(2,1)} %refs_15_.1) | copy-start | bytes 1572868
  0.6 22.6 %collective-permute-start.10 = (bf16[2,128,1024]{2,1,0:T(8,128)(2,1)}, bf16[2,128,1024]{2,1,0:T(8,128)(2,1)S(1)}, u32[]{:S(2)}, u32[]{:S(2)}) collective-permute-start(bf16[2,128,1024]{2,1,0:T(8,128)(2,1)} %refs_15_.1), channel_id=1, source_target_pairs={{0,7},{1,0},{2,1},{3,2},{4,3},{5,4},{6,5},{7,6},{8,15},{9,8},{10,9... | collective-permute-start | bytes 1572872 | tf_op jit(solution)/shard_map/ppermute | solution.py:18
  11.7 17.0 %collective-permute-start.7 = (bf16[2,128,1024]{2,1,0:T(8,128)(2,1)}, bf16[2,128,1024]{2,1,0:T(8,128)(2,1)S(1)}, u32[]{:S(2)}, u32[]{:S(2)}) collective-permute-start(bf16[2,128,1024]{2,1,0:T(8,128)(2,1)} %refs_15_.1), channel_id=1, source_target_pairs={{0,1},{1,2},{2,3},{3,4},{4,5},{5,6},{6,7},{7,0},{8,9},{9,10},{10,1... | collective-permute-start | bytes 1572872 | tf_op jit(solution)/shard_map/ppermute | solution.py:18
  23.2 15.8 %collective-permute-start.11 = (bf16[2,128,1024]{2,1,0:T(8,128)(2,1)S(1)}, bf16[2,128,1024]{2,1,0:T(8,128)(2,1)S(1)}, u32[]{:S(2)}, u32[]{:S(2)}) collective-permute-start(bf16[2,128,1024]{2,1,0:T(8,128)(2,1)S(1)} %collective-permute-done.10.refs_4_), channel_id=1, source_target_pairs={{0,7},{1,0},{2,1},{3,2},{4,3},{5,4},{6,5},{7,6},{8,15},{9,8},{10,9... | collective-permute-start | bytes 1572872 | tf_op jit(solution)/shard_map/ppermute | solution.py:18
  28.7 15.9 %collective-permute-start.8 = (bf16[2,128,1024]{2,1,0:T(8,128)(2,1)S(1)}, bf16[2,128,1024]{2,1,0:T(8,128)(2,1)S(1)}, u32[]{:S(2)}, u32[]{:S(2)}) collective-permute-start(bf16[2,128,1024]{2,1,0:T(8,128)(2,1)S(1)} %collective-permute-done.7.refs_1_), channel_id=1, source_target_pairs={{0,1},{1,2},{2,3},{3,4},{4,5},{5,6},{6,7},{7,0},{8,9},{9,10},{10,1... | collective-permute-start | bytes 1572872 | tf_op jit(solution)/shard_map/ppermute | solution.py:18
  39.0 16.5 %collective-permute-start.12 = (bf16[2,128,1024]{2,1,0:T(8,128)(2,1)S(1)}, bf16[2,128,1024]{2,1,0:T(8,128)(2,1)S(1)}, u32[]{:S(2)}, u32[]{:S(2)}) collective-permute-start(bf16[2,128,1024]{2,1,0:T(8,128)(2,1)S(1)} %collective-permute-done.11.refs_5_), channel_id=1, source_target_pairs={{0,7},{1,0},{2,1},{3,2},{4,3},{5,4},{6,5},{7,6},{8,15},{9,8},{10,9... | collective-permute-start | bytes 1572872 | tf_op jit(solution)/shard_map/ppermute | solution.py:18
  44.6 31.2 %collective-permute-start.9 = (bf16[2,128,1024]{2,1,0:T(8,128)(2,1)S(1)}, bf16[2,128,1024]{2,1,0:T(8,128)(2,1)S(1)}, u32[]{:S(2)}, u32[]{:S(2)}) collective-permute-start(bf16[2,128,1024]{2,1,0:T(8,128)(2,1)S(1)} %collective-permute-done.8.refs_2_), channel_id=1, source_target_pairs={{0,1},{1,2},{2,3},{3,4},{4,5},{5,6},{6,7},{7,0},{8,9},{9,10},{10,1... | collective-permute-start | bytes 1572872 | tf_op jit(solution)/shard_map/ppermute | solution.py:18
  46.5 1.0 copy-start.2
  47.6 0.7 copy-start.4
  48.4 17.4 %collective-permute-start = (bf16[1168,128]{1,0:T(8,128)(2,1)S(1)}, bf16[1168,128]{1,0:T(8,128)(2,1)S(1)}, u32[]{:S(2)}, u32[]{:S(2)}) collective-permute-start(bf16[1168,128]{1,0:T(8,128)(2,1)S(1)} %shard_map.58.refs_0_), channel_id=1, source_target_pairs={{0,1},{1,2},{2,3},{3,4},{4,5},{5,6},{6,7},{7,0},{8,9},{9,10},{10,1... | collective-permute-start | bytes 897032 | tf_op jit(solution)/shard_map/ppermute | solution.py:18
  50.3 17.4 %collective-permute-start.3 = (bf16[1168,128]{1,0:T(8,128)(2,1)S(1)}, bf16[1168,128]{1,0:T(8,128)(2,1)S(1)}, u32[]{:S(2)}, u32[]{:S(2)}) collective-permute-start(bf16[1168,128]{1,0:T(8,128)(2,1)S(1)} %shard_map.58.refs_0_), channel_id=1, source_target_pairs={{0,7},{1,0},{2,1},{3,2},{4,3},{5,4},{6,5},{7,6},{8,15},{9,8},{10,9... | collective-permute-start | bytes 897032 | tf_op jit(solution)/shard_map/ppermute | solution.py:18
  55.5 22.3 %collective-permute-start.13 = (bf16[128,1024]{1,0:T(8,128)(2,1)S(1)}, bf16[128,1024]{1,0:T(8,128)(2,1)S(1)}, u32[]{:S(2)}, u32[]{:S(2)}) collective-permute-start(bf16[128,1024]{1,0:T(8,128)(2,1)S(1)} %shard_map.60), channel_id=1, source_target_pairs={{0,7},{1,0},{2,1},{3,2},{4,3},{5,4},{6,5},{7,6},{8,15},{9,8},{10,9... | collective-permute-start | bytes 786440 | tf_op jit(solution)/shard_map/ppermute | solution.py:18
  65.8 15.4 %collective-permute-start.1 = (bf16[1168,128]{1,0:T(8,128)(2,1)S(1)}, bf16[1168,128]{1,0:T(8,128)(2,1)S(1)}, u32[]{:S(2)}, u32[]{:S(2)}) collective-permute-start(bf16[1168,128]{1,0:T(8,128)(2,1)S(1)} %collective-permute-done.refs_1_), channel_id=1, source_target_pairs={{0,1},{1,2},{2,3},{3,4},{4,5},{5,6},{6,7},{7,0},{8,9},{9,10},{10,1... | collective-permute-start | bytes 897032 | tf_op jit(solution)/shard_map/ppermute | solution.py:18
  67.7 15.4 %collective-permute-start.4 = (bf16[1168,128]{1,0:T(8,128)(2,1)S(1)}, bf16[1168,128]{1,0:T(8,128)(2,1)S(1)}, u32[]{:S(2)}, u32[]{:S(2)}) collective-permute-start(bf16[1168,128]{1,0:T(8,128)(2,1)S(1)} %collective-permute-done.3.refs_4_), channel_id=1, source_target_pairs={{0,7},{1,0},{2,1},{3,2},{4,3},{5,4},{6,5},{7,6},{8,15},{9,8},{10,9... | collective-permute-start | bytes 897032 | tf_op jit(solution)/shard_map/ppermute | solution.py:18
  72.9 1.0 copy-start
  73.9 14.5 %collective-permute-start.15 = (bf16[128,1024]{1,0:T(8,128)(2,1)S(1)}, bf16[128,1024]{1,0:T(8,128)(2,1)S(1)}, u32[]{:S(2)}, u32[]{:S(2)}) collective-permute-start(bf16[128,1024]{1,0:T(8,128)(2,1)S(1)} %shard_map.62), channel_id=1, source_target_pairs={{0,8},{8,16},{16,24},{24,32},{32,40},{40,48},{48,56},{56,64},{64,7... | collective-permute-start | bytes 786440 | tf_op jit(solution)/shard_map/ppermute | solution.py:18
  75.9 12.4 %collective-permute-start.16 = (bf16[128,1024]{1,0:T(8,128)(2,1)S(1)}, bf16[128,1024]{1,0:T(8,128)(2,1)S(1)}, u32[]{:S(2)}, u32[]{:S(2)}) collective-permute-start(bf16[128,1024]{1,0:T(8,128)(2,1)S(1)} %shard_map.63), channel_id=1, source_target_pairs={{0,1},{1,2},{2,3},{3,4},{4,5},{5,6},{6,7},{7,0},{8,9},{9,10},{10,1... | collective-permute-start | bytes 786440 | tf_op jit(solution)/shard_map/ppermute | solution.py:18
  78.4 10.0 %collective-permute-start.14 = (bf16[128,1024]{1,0:T(8,128)(2,1)S(1)}, bf16[128,1024]{1,0:T(8,128)(2,1)S(1)}, u32[]{:S(2)}, u32[]{:S(2)}) collective-permute-start(bf16[128,1024]{1,0:T(8,128)(2,1)S(1)} %get-tuple-element.16), channel_id=1, source_target_pairs={{0,8},{8,16},{16,24},{24,32},{32,40},{40,48},{48,56},{56,64},{64,7... | collective-permute-start | bytes 786440 | tf_op jit(solution)/shard_map/ppermute | solution.py:18
  81.2 13.2 %collective-permute-start.2 = (bf16[1168,128]{1,0:T(8,128)(2,1)S(1)}, bf16[1168,128]{1,0:T(8,128)(2,1)S(1)}, u32[]{:S(2)}, u32[]{:S(2)}) collective-permute-start(bf16[1168,128]{1,0:T(8,128)(2,1)S(1)} %collective-permute-done.1.refs_2_), channel_id=1, source_target_pairs={{0,1},{1,2},{2,3},{3,4},{4,5},{5,6},{6,7},{7,0},{8,9},{9,10},{10,1... | collective-permute-start | bytes 897032 | tf_op jit(solution)/shard_map/ppermute | solution.py:18
  83.1 13.3 %collective-permute-start.5 = (bf16[1168,128]{1,0:T(8,128)(2,1)S(1)}, bf16[1168,128]{1,0:T(8,128)(2,1)S(1)}, u32[]{:S(2)}, u32[]{:S(2)}) collective-permute-start(bf16[1168,128]{1,0:T(8,128)(2,1)S(1)} %collective-permute-done.4.refs_5_), channel_id=1, source_target_pairs={{0,7},{1,0},{2,1},{3,2},{4,3},{5,4},{6,5},{7,6},{8,15},{9,8},{10,9... | collective-permute-start | bytes 897032 | tf_op jit(solution)/shard_map/ppermute | solution.py:18
  89.7 13.6 %collective-permute-start.18 = (bf16[128,1024]{1,0:T(8,128)(2,1)S(1)}, bf16[128,1024]{1,0:T(8,128)(2,1)S(1)}, u32[]{:S(2)}, u32[]{:S(2)}) collective-permute-start(bf16[128,1024]{1,0:T(8,128)(2,1)S(1)} %get-tuple-element.20), channel_id=1, source_target_pairs={{0,8},{8,16},{16,24},{24,32},{32,40},{40,48},{48,56},{56,64},{64,7... | collective-permute-start | bytes 786440 | tf_op jit(solution)/shard_map/ppermute | solution.py:18
  94.4 8.9 %collective-permute-start.17 = (bf16[592,128]{1,0:T(8,128)(2,1)S(1)}, bf16[592,128]{1,0:T(8,128)(2,1)S(1)}, u32[]{:S(2)}, u32[]{:S(2)}) collective-permute-start(bf16[592,128]{1,0:T(8,128)(2,1)S(1)} %shard_map.66), channel_id=1, source_target_pairs={{0,1},{1,2},{2,3},{3,4},{4,5},{5,6},{6,7},{7,0},{8,9},{9,10},{10,1... | collective-permute-start | bytes 454664 | tf_op jit(solution)/shard_map/ppermute | solution.py:18
  96.4 10.9 %collective-permute-start.6 = (bf16[576,128]{1,0:T(8,128)(2,1)S(1)}, bf16[576,128]{1,0:T(8,128)(2,1)S(1)}, u32[]{:S(2)}, u32[]{:S(2)}) collective-permute-start(bf16[576,128]{1,0:T(8,128)(2,1)S(1)} %shard_map.59), channel_id=1, source_target_pairs={{0,7},{1,0},{2,1},{3,2},{4,3},{5,4},{6,5},{7,6},{8,15},{9,8},{10,9... | collective-permute-start | bytes 442376 | tf_op jit(solution)/shard_map/ppermute | solution.py:18
  104.9 10.0 %collective-permute-start.20 = (bf16[144,1024]{1,0:T(8,128)(2,1)S(1)}, bf16[144,1024]{1,0:T(8,128)(2,1)S(1)}, u32[]{:S(2)}, u32[]{:S(2)}) collective-permute-start(bf16[144,1024]{1,0:T(8,128)(2,1)S(1)} %get-tuple-element.23.refs_2_.refs_16_), channel_id=1, source_target_pairs={{0,504},{8,0},{16,8},{24,16},{32,24},{40,32},{48,40},{56,48},{64,5... | collective-permute-start | bytes 884744 | tf_op jit(solution)/shard_map/ppermute | solution.py:18
  111.6 10.4 %collective-permute-start.19 = (bf16[272,1024]{1,0:T(8,128)(2,1)S(1)}, bf16[272,1024]{1,0:T(8,128)(2,1)S(1)}, u32[]{:S(2)}, u32[]{:S(2)}) collective-permute-start(bf16[272,1024]{1,0:T(8,128)(2,1)S(1)} %get-tuple-element.24), channel_id=1, source_target_pairs={{0,504},{8,0},{16,8},{24,16},{32,24},{40,32},{48,40},{56,48},{64,5... | collective-permute-start | bytes 1671176 | tf_op jit(solution)/shard_map/ppermute | solution.py:18
  114.9 7.0 %copy-start.3 = (bf16[2,128,1024]{2,1,0:T(8,128)(2,1)S(1)}, bf16[2,128,1024]{2,1,0:T(8,128)(2,1)}, u32[]{:S(2)}) copy-start(bf16[2,128,1024]{2,1,0:T(8,128)(2,1)} %refs_6_.1) | copy-start | bytes 1572868
  116.5 17.6 %collective-permute-start.21 = (bf16[144,1024]{1,0:T(8,128)(2,1)S(1)}, bf16[144,1024]{1,0:T(8,128)(2,1)S(1)}, u32[]{:S(2)}, u32[]{:S(2)}) collective-permute-start(bf16[144,1024]{1,0:T(8,128)(2,1)S(1)} %shard_map.70.refs_5_), channel_id=1, source_target_pairs={{0,504},{8,0},{16,8},{24,16},{32,24},{40,32},{48,40},{56,48},{64,5... | collective-permute-start | bytes 884744 | tf_op jit(solution)/shard_map/ppermute | solution.py:18
  118.4 15.6 %collective-permute-start.22 = (bf16[128,1024]{1,0:T(8,128)(2,1)S(1)}, bf16[128,1024]{1,0:T(8,128)(2,1)S(1)}, u32[]{:S(2)}, u32[]{:S(2)}) collective-permute-start(bf16[128,1024]{1,0:T(8,128)(2,1)S(1)} %shard_map.68.refs_17_), channel_id=1, source_target_pairs={{0,496},{8,504},{16,0},{24,8},{32,16},{40,24},{48,32},{56,40},{64,... | collective-permute-start | bytes 786440 | tf_op jit(solution)/shard_map/ppermute | solution.py:18
  122.0 12.1 %copy-start.5 = (bf16[2,128]{1,0:T(2,128)(2,1)S(1)}, bf16[2,128]{1,0:T(2,128)(2,1)}, u32[]{:S(2)}) copy-start(bf16[2,128]{1,0:T(2,128)(2,1)} %refs_7_.1) | copy-start | bytes 1540
where the time goes:
time: 137 us; the launch traced here: 136 us
  starting transfers between devices  80.1 us (58%)
  waiting for transfers between devices  38.5 us (28%)
  Pallas kernels  13.3 us (10%)
  local copies, waits for them, and re-layouts  2.74 us (2%)
    ppermute x23, starting transfers between devices, hop(): lax.ppermute(block, axis, [(i, (i + distance) % size) for i in range(size)])  80.1 us
    ppermute x23, waiting for transfers between devices, hop(): lax.ppermute(block, axis, [(i, (i + distance) % size) for i in range(size)])  38.5 us
    pallas_call x15, Pallas kernels, call(): pl.pallas_call(run, in_specs=[VMEM] * count + [HBM] * len(after), out_spe...  13.3 us
    unnamed x12, local copies, waits for them, and re-layouts  2.74 us
  transfers between devices with their start and end apart: 23, of which 7 were waited for; matrix products, arithmetic and copies ran while one was open for 0% of the time, Pallas kernels for 9%

commit v1 on v0

v1 whole, which is shorter than its diff:
```python
import jax
import jax.numpy as jnp
from jax import lax
from jax.experimental import pallas as pl
from jax.experimental.pallas import tpu as pltpu
from jax.sharding import PartitionSpec as P


BF16, F32 = jnp.bfloat16, jnp.float32
HBM = pl.BlockSpec(memory_space=pl.ANY)
VMEM = pl.BlockSpec(memory_space=pltpu.VMEM)
GRANT = 12 * 2**20
TAIL = 16


def hop(block, axis, distance):
    size = lax.axis_size(axis)
    return lax.ppermute(block, axis, [(i, (i + distance) % size) for i in range(size)])


def nn(a, b):
    return lax.dot_general(a, b, (((1,), (0,)), ((), ())), preferred_element_type=F32)


def nt(a, b):
    return lax.dot_general(a, b, (((1,), (1,)), ((), ())), preferred_element_type=F32)


def kept(shape, kind):
    return pltpu.VMEM(shape, kind)


def near(array):
    return pltpu.with_memory_space_constraint(array, pltpu.VMEM)


def apart(array):
    return pltpu.with_memory_space_constraint(array, pltpu.HBM)


def call(body, ins, outs, flops, after=(), wide=(), scratch=()):
    count = len(ins) + len(wide)

    def run(*refs):
        body(*refs[:count], *refs[count + len(after) :])

    return pl.pallas_call(
        run,
        in_specs=[HBM] * len(wide) + [VMEM] * len(ins) + [HBM] * len(after),
        out_specs=tuple(VMEM for _ in outs),
        out_shape=tuple(outs),
        scratch_shapes=scratch,
        cost_estimate=pl.CostEstimate(flops=flops, bytes_accessed=2**20, transcendentals=0),
        compiler_params=pltpu.CompilerParams(vmem_limit_bytes=GRANT),
    )(*[apart(array) for array in wide], *[near(array) for array in ins], *after)


def part(array, picked, shape):
    def copy(ref, out):
        out[...] = ref[picked]

    return call(copy, [array], [kept(shape, BF16)], 1000)[0]


def slot(offset, count):
    return lax.rem(lax.axis_index("row") + (offset + count), count)


def unpack(pieces, whole, count):
    size = whole.shape[0] // count
    half = count // 2
    whole[...] = jnp.zeros(whole.shape, BF16)
    for offset, (ref, base) in pieces:
        s = slot(offset, count)
        row = pl.multiple_of(s * size, size)
        for k in range(half):
            column = pl.multiple_of(lax.rem(s + k, count) * size, size)
            whole[pl.ds(row, size), pl.ds(column, size)] = ref[base + k * size : base + (k + 1) * size, :]
        a = lax.rem(s, half)
        row = pl.multiple_of(a * size + lax.div(s, half) * (size // 2), size // 2)
        column = pl.multiple_of((a + half) * size, size)
        start = base + half * size
        whole[pl.ds(row, size // 2), pl.ds(column, size)] = ref[start : start + size // 2, :]


def by_symmetric(a, whole):
    return nn(a, whole) + nt(a, whole)


def two_rows(row):
    high = row.astype(BF16).astype(F32)
    index = lax.broadcasted_iota(jnp.int32, (TAIL, row.shape[1]), 0)
    return jnp.where(index == 0, high, jnp.where(index == 1, row - high, 0.0)).astype(BF16)


def one_row(tile):
    return tile[0:1].astype(F32) + tile[1:2].astype(F32)


def on_device(trans, offset, spread):
    count = lax.axis_size("row")
    _, rows, size = trans.shape
    half = count // 2
    packed = half * rows + rows // 2
    product = 2 * rows * size * size
    panel = kept((rows, size), BF16)
    wide = kept((rows, size), F32)
    pair = kept((2 * rows, size), BF16)
    whole = kept((size, size), BF16)
    short = kept((rows + TAIL, size), BF16)
    long = kept((2 * rows + TAIL, size), BF16)
    line = kept((8, rows), F32)

    def gather(block, parts):
        fore, back = [block], [block]
        for _ in range(half - 1):
            fore.append(hop(fore[-1], "row", 1))
            back.append(hop(back[-1], "row", -1))
        halves = parts[0](fore[-1]), parts[1](back[-1])
        even = hop(halves[0], "row", 1)
        odd = hop(halves[1], "row", -1)
        arrays = [block] + fore[1:] + back[1:]
        offsets = [0] + [-k for k in range(1, half)] + list(range(1, half))
        return arrays, offsets, even, odd

    e_all = lax.all_gather(trans, "row", axis=1, tiled=True)
    b1_in = hop(part(trans, 1, (rows, size)), "tm", 1)

    def pack(l_ref, g_ref, out):
        z = lax.axis_index("row")
        for b in range(2):
            base = b * (packed + TAIL)
            for k in range(half):
                c = lax.rem(z + k, count)
                tile = l_ref[b, :, pl.ds(pl.multiple_of(c * rows, rows), rows)]
                out[base + k * rows : base + (k + 1) * rows, :] = tile * jnp.asarray(0.5, BF16) if k == 0 else tile
            c = lax.rem(z + half, count)
            tile = l_ref[b, :, pl.ds(pl.multiple_of(c * rows, rows), rows)].astype(F32)
            lower = tile.T[rows // 2 :]
            out[base + half * rows : base + packed, :] = jnp.where(z < half, tile[: rows // 2], lower).astype(BF16)
        g = g_ref[...].astype(F32)
        index = lax.broadcasted_iota(jnp.int32, (TAIL, rows), 0)
        tile = jnp.where(index == 0, g[0:1], jnp.where(index == 1, g[1:2], 0.0))
        out[packed : packed + TAIL, :] = tile.astype(BF16)

    (sent,) = call(pack, [spread, offset], [kept((2 * packed + TAIL, rows), BF16)], 1000)
    l_arrays, offsets, l_even_last, l_odd_last = gather(
        sent,
        (
            lambda x: part(x, slice(0, packed + TAIL), (packed + TAIL, rows)),
            lambda x: part(x, slice(packed + TAIL, 2 * packed + TAIL), (packed, rows)),
        ),
    )
    n = len(l_arrays)

    def opened(*refs):
        even_last, odd_last, b1_ref, own = refs[n : n + 4]
        close_ref, head_ref, line_ref, l_ev, l_od, g_ref = refs[n + 4 :]
        unpack([(way, (ref, 0)) for way, ref in zip(offsets, refs)] + [(half, (even_last, 0))], l_ev, count)
        unpack([(way, (ref, packed + TAIL)) for way, ref in zip(offsets, refs)] + [(half, (odd_last, 0))], l_od, count)
        for way, ref in list(zip(offsets, refs)) + [(half, even_last)]:
            column = pl.multiple_of(slot(way, count) * rows, rows)
            g_ref[:, pl.ds(column, rows)] = ref[packed : packed + TAIL, :]
        g = g_ref[...]
        close_ref[...] = by_symmetric(b1_ref[...], l_ev[...])
        head_ref[...] = by_symmetric(own[0], l_od[...])
        index = lax.broadcasted_iota(jnp.int32, (8, rows), 0)
        line_ref[...] = jnp.where(index == 0, nt(g, b1_ref[...])[0:1], nt(g, own[0])[1:2])

    close, head, line1, l_even, l_odd, g_all = call(
        opened,
        l_arrays + [l_even_last, l_odd_last, b1_in, trans],
        [wide, wide, line, whole, whole, kept((TAIL, size), BF16)],
        4 * product,
    )

    def first(all_ref, own, out, odd, sem):
        copy = pltpu.make_async_copy(all_ref.at[1], odd, sem)
        copy.start()
        copy.wait()
        out[...] = nn(own[0], odd[...]).astype(BF16)

    x1, e_odd = call(
        first, [trans], [panel, whole], product, after=(g_all,), wide=(e_all,), scratch=(pltpu.SemaphoreType.DMA,)
    )
    x1_in = hop(x1, "tm", 1)

    def evens(all_ref, even, sem):
        copy = pltpu.make_async_copy(all_ref.at[0], even, sem)
        copy.start()
        copy.wait()

    (e_even,) = call(evens, [], [whole], 1000, after=(x1,), wide=(e_all,), scratch=(pltpu.SemaphoreType.DMA,))

    def second(x1_ref, b1_ref, even, odd, x3_ref, b3_ref, x2_ref):
        past = lax.axis_index("tm") < 1
        one = jnp.concatenate([x1_ref[...], b1_ref[...]], axis=0)
        two = nn(one, even[...]).astype(BF16)
        three = nn(two, odd[...])
        three = jnp.where(past, one.astype(F32), three).astype(BF16)
        x3_ref[...] = three[:rows]
        b3_ref[...] = three[rows:]
        x2_ref[...] = two

    x3, b3, x2 = call(second, [x1_in, b1_in, e_even, e_odd], [panel, panel, pair], 4 * product)
    b3_in = hop(b3, "tm", 1)

    def third(x1_ref, x2_ref, x3_ref, line_ref, even, l_ev, l_od, g_ref, m_ref, far_ref, row_ref):
        past = lax.axis_index("tm") < 1
        two = x2_ref[...]
        far = by_symmetric(two, l_od[...])
        w = by_symmetric(x1_ref[...], l_ev[...]) + nt(far[:rows].astype(BF16), even[...])
        far_ref[...] = far[rows:]
        row = nt(g_ref[...], two)[1:2]
        row_ref[...] = jnp.broadcast_to(line_ref[0:1] + row[:, rows:], row_ref.shape)
        row = nt(g_ref[...], x1_ref[...])[0:1] + row[:, :rows]
        m_ref[:rows, :] = jnp.where(past, 0.0, w).astype(BF16)
        m_ref[rows : 2 * rows, :] = x3_ref[...]
        m_ref[2 * rows :, :] = jnp.zeros((TAIL, size), BF16)
        m_ref[2 * rows :, :rows] = two_rows(jnp.where(past, 0.0, row))

    w, far, line2 = call(
        third, [x1_in, x2, x3, line1, e_even, l_even, l_odd, g_all], [long, wide, line], 7 * product
    )
    w_in = hop(w, "tm", -1)

    def fourth(b3_ref, l_ev, g_ref, m_ref):
        past = lax.axis_index("tm") < 2
        own = b3_ref[...]
        m_ref[:rows, :] = jnp.where(past, 0.0, by_symmetric(own, l_ev[...])).astype(BF16)
        m_ref[rows:, :] = jnp.zeros((TAIL, size), BF16)
        m_ref[rows:, :rows] = two_rows(jnp.where(past, 0.0, nt(g_ref[...], own)[0:1]))

    (v,) = call(fourth, [b3_in, l_even, g_all], [short], 2 * product, after=(w,))
    v_in = hop(v, "tm", -1)

    def fifth(b3_ref, even, b4_ref):
        own = b3_ref[...]
        past = lax.axis_index("tm") < 2
        b4_ref[...] = jnp.where(past, own.astype(F32), nn(own, even[...])).astype(BF16)

    (b4,) = call(fifth, [b3_in, e_even], [panel], product, after=(v,))
    b4_in = hop(b4, "tm", -2)

    def seventh(w_ref, head_ref, even, odd, l_own, out):
        inner = head_ref[...] + nt(w_ref[:rows, :], odd[...])
        out[...] = (nt(inner.astype(BF16), even[...]) + l_own[0].astype(F32)).astype(BF16)

    (l_first,) = call(seventh, [w_in, head, e_even, e_odd, spread], [panel], 2 * product, after=(b4,))

    def sixth(v_ref, close_ref, far_ref, line_ref, even, odd, m_ref):
        past = lax.axis_index("tm") < 1
        behind = far_ref[...] + nt(v_ref[:rows, :], odd[...])
        u = close_ref[...] + nt(behind.astype(BF16), even[...])
        row = line_ref[0:1] + one_row(v_ref[rows:, :rows])
        m_ref[:rows, :] = jnp.where(past, 0.0, u).astype(BF16)
        m_ref[rows:, :] = jnp.zeros((TAIL, size), BF16)
        m_ref[rows:, :rows] = two_rows(jnp.where(past, 0.0, row))

    (u,) = call(sixth, [v_in, close, far, line2, e_even, e_odd], [short], 2 * product, after=(l_first,))
    u_in = hop(u, "tm", -1)

    def eighth(w_ref, u_ref, b4_ref, line_ref, odd, l_ref, l_own, g_own, e_out, g_out, l_out):
        l_out[1] = (nt(u_ref[:rows, :], odd[...]) + l_own[1].astype(F32)).astype(BF16)
        l_out[0] = l_ref[...]
        e_out[0] = w_ref[rows : 2 * rows, :]
        e_out[1] = b4_ref[...]
        g = g_own[...].astype(F32)
        g_out[0:1, :] = (g[0:1] + line_ref[1:2] + one_row(w_ref[2 * rows :, :rows])).astype(BF16)
        g_out[1:2, :] = (g[1:2] + one_row(u_ref[rows:, :rows])).astype(BF16)

    return call(
        eighth,
        [w_in, u_in, b4_in, line1, e_odd, l_first, spread, offset],
        [jax.ShapeDtypeStruct(x.shape, BF16) for x in (trans, offset, spread)],
        product,
    )


def solution(mesh):
    placed = (P("tm", "row", None), P("tm", "row"), P("tm", "row", None))
    return jax.shard_map(on_device, mesh=mesh, in_specs=placed, out_specs=placed, check_vma=False)
```

time: 137 us -> 155 us (1.13)
  the two profiles are of different devices: /device:TPU:56 before, /device:TPU:62 now
where the time goes in v1:
time: 155 us; the launch traced here: 154 us
  waiting for transfers between devices  65.1 us (42%)
  starting transfers between devices  51.9 us (33%)
  Pallas kernels  17.5 us (11%)
  between operations  14.3 us (9%)
  local copies, waits for them, and re-layouts  5.24 us (3%)
    ppermute x15, waiting for transfers between devices, hop(): lax.ppermute(block, axis, [(i, (i + distance) % size) for i in range(size)])  59.6 us
    ppermute x15, starting transfers between devices, hop(): lax.ppermute(block, axis, [(i, (i + distance) % size) for i in range(size)])  51.8 us
    pallas_call x14, Pallas kernels, call(): pl.pallas_call(run, in_specs=[HBM] * len(wide) + [VMEM] * len(ins) + [HBM...  17.5 us
    unnamed x20, local copies, waits for them, and re-layouts  5.24 us
    all_gather x1, waiting for transfers between devices, on_device(): e_all = lax.all_gather(trans, 'row', axis=1, tiled=True)  4.82 us
  transfers between devices with their start and end apart: 16, of which 10 were waited for; matrix products, arithmetic and copies ran while one was open for 0% of the time, Pallas kernels for 5%

profile of v1, /device:TPU:62, one launch (start us, length us, event | category | flops | bytes accessed | tf_op | source)
XLA Modules:
  0.0 154.0 jit_solution(3491242076362739367)
XLA Ops:
  7.2 0.0 copy-start.3
  7.2 0.0 all-gather.2.cloned.1.call-start
  7.2 0.7 all-gather.2.cloned.1.call-update
  7.9 0.0 copy-start
  7.9 1.0 copy-done
  9.0 0.7 copy-done.8
  9.6 0.2 shard_map.58.refs_0_
  9.8 4.3 %collective-permute-start = (bf16[1168,128]{1,0:T(8,128)(2,1)S(1)}, bf16[1168,128]{1,0:T(8,128)(2,1)S(1)}, u32[]{:S(2)}, u32[]{:S(2)}) collective-permute-start(bf16[1168,128]{1,0:T(8,128)(2,1)S(1)} %shard_map.58.refs_0_), channel_id=1, source_target_pairs={{0,1},{1,2},{2,3},{3,4},{4,5},{5,6},{6,7},{7,0},{8,9},{9,10},{10,1... | collective-permute-start | bytes 897032 | tf_op jit(solution)/shard_map/ppermute | solution.py:18
  14.1 8.6 %collective-permute-start.3 = (bf16[1168,128]{1,0:T(8,128)(2,1)S(1)}, bf16[1168,128]{1,0:T(8,128)(2,1)S(1)}, u32[]{:S(2)}, u32[]{:S(2)}) collective-permute-start(bf16[1168,128]{1,0:T(8,128)(2,1)S(1)} %shard_map.58.refs_0_), channel_id=1, source_target_pairs={{0,7},{1,0},{2,1},{3,2},{4,3},{5,4},{6,5},{7,6},{8,15},{9,8},{10,9... | collective-permute-start | bytes 897032 | tf_op jit(solution)/shard_map/ppermute | solution.py:18
  22.7 5.2 %collective-permute-done.refs_1_ = bf16[1168,128]{1,0:T(8,128)(2,1)S(1)} collective-permute-done((bf16[1168,128]{1,0:T(8,128)(2,1)S(1)}, bf16[1168,128]{1,0:T(8,128)(2,1)S(1)}, u32[]{:S(2)}, u32[]{:S(2)}) %collective-permute-start) | collective-permute-done | bytes 299040 | tf_op jit(solution)/shard_map/ppermute | solution.py:18
  27.8 1.9 %collective-permute-start.1 = (bf16[1168,128]{1,0:T(8,128)(2,1)S(1)}, bf16[1168,128]{1,0:T(8,128)(2,1)S(1)}, u32[]{:S(2)}, u32[]{:S(2)}) collective-permute-start(bf16[1168,128]{1,0:T(8,128)(2,1)S(1)} %collective-permute-done.refs_1_), channel_id=1, source_target_pairs={{0,1},{1,2},{2,3},{3,4},{4,5},{5,6},{6,7},{7,0},{8,9},{9,10},{10,1... | collective-permute-start | bytes 897032 | tf_op jit(solution)/shard_map/ppermute | solution.py:18
  29.7 1.3 collective-permute-done.3.refs_4_
  31.0 5.6 %collective-permute-start.4 = (bf16[1168,128]{1,0:T(8,128)(2,1)S(1)}, bf16[1168,128]{1,0:T(8,128)(2,1)S(1)}, u32[]{:S(2)}, u32[]{:S(2)}) collective-permute-start(bf16[1168,128]{1,0:T(8,128)(2,1)S(1)} %collective-permute-done.3.refs_4_), channel_id=1, source_target_pairs={{0,7},{1,0},{2,1},{3,2},{4,3},{5,4},{6,5},{7,6},{8,15},{9,8},{10,9... | collective-permute-start | bytes 897032 | tf_op jit(solution)/shard_map/ppermute | solution.py:18
  36.6 10.1 %collective-permute-done.1.refs_2_ = bf16[1168,128]{1,0:T(8,128)(2,1)S(1)} collective-permute-done((bf16[1168,128]{1,0:T(8,128)(2,1)S(1)}, bf16[1168,128]{1,0:T(8,128)(2,1)S(1)}, u32[]{:S(2)}, u32[]{:S(2)}) %collective-permute-start.1) | collective-permute-done | bytes 299040 | tf_op jit(solution)/shard_map/ppermute | solution.py:18
  46.7 1.9 %collective-permute-start.2 = (bf16[1168,128]{1,0:T(8,128)(2,1)S(1)}, bf16[1168,128]{1,0:T(8,128)(2,1)S(1)}, u32[]{:S(2)}, u32[]{:S(2)}) collective-permute-start(bf16[1168,128]{1,0:T(8,128)(2,1)S(1)} %collective-permute-done.1.refs_2_), channel_id=1, source_target_pairs={{0,1},{1,2},{2,3},{3,4},{4,5},{5,6},{6,7},{7,0},{8,9},{9,10},{10,1... | collective-permute-start | bytes 897032 | tf_op jit(solution)/shard_map/ppermute | solution.py:18
  48.6 5.1 %collective-permute-start.5 = (bf16[1168,128]{1,0:T(8,128)(2,1)S(1)}, bf16[1168,128]{1,0:T(8,128)(2,1)S(1)}, u32[]{:S(2)}, u32[]{:S(2)}) collective-permute-start(bf16[1168,128]{1,0:T(8,128)(2,1)S(1)} %collective-permute-done.4.refs_5_), channel_id=1, source_target_pairs={{0,7},{1,0},{2,1},{3,2},{4,3},{5,4},{6,5},{7,6},{8,15},{9,8},{10,9... | collective-permute-start | bytes 897032 | tf_op jit(solution)/shard_map/ppermute | solution.py:18
  53.7 0.0 copy-start.2
  53.8 1.0 copy-done.2
  54.8 1.9 %collective-permute-start.8 = (bf16[128,1024]{1,0:T(8,128)(2,1)S(1)}, bf16[128,1024]{1,0:T(8,128)(2,1)S(1)}, u32[]{:S(2)}, u32[]{:S(2)}) collective-permute-start(bf16[128,1024]{1,0:T(8,128)(2,1)S(1)} %shard_map.61), channel_id=1, source_target_pairs={{0,8},{8,16},{16,24},{24,32},{32,40},{40,48},{48,56},{56,64},{64,7... | collective-permute-start | bytes 786440 | tf_op jit(solution)/shard_map/ppermute | solution.py:18
  56.7 8.6 %collective-permute-done.2.refs_0_.refs_3_ = bf16[1168,128]{1,0:T(8,128)(2,1)S(1)} collective-permute-done((bf16[1168,128]{1,0:T(8,128)(2,1)S(1)}, bf16[1168,128]{1,0:T(8,128)(2,1)S(1)}, u32[]{:S(2)}, u32[]{:S(2)}) %collective-permute-start.2) | collective-permute-done | bytes 299040 | tf_op jit(solution)/shard_map/ppermute | solution.py:18
  65.4 1.9 %collective-permute-start.6 = (bf16[592,128]{1,0:T(8,128)(2,1)S(1)}, bf16[592,128]{1,0:T(8,128)(2,1)S(1)}, u32[]{:S(2)}, u32[]{:S(2)}) collective-permute-start(bf16[592,128]{1,0:T(8,128)(2,1)S(1)} %shard_map.59), channel_id=1, source_target_pairs={{0,1},{1,2},{2,3},{3,4},{4,5},{5,6},{6,7},{7,0},{8,9},{9,10},{10,1... | collective-permute-start | bytes 454664 | tf_op jit(solution)/shard_map/ppermute | solution.py:18
  67.3 5.1 %collective-permute-start.7 = (bf16[576,128]{1,0:T(8,128)(2,1)S(1)}, bf16[576,128]{1,0:T(8,128)(2,1)S(1)}, u32[]{:S(2)}, u32[]{:S(2)}) collective-permute-start(bf16[576,128]{1,0:T(8,128)(2,1)S(1)} %shard_map.60), channel_id=1, source_target_pairs={{0,7},{1,0},{2,1},{3,2},{4,3},{5,4},{6,5},{7,6},{8,15},{9,8},{10,9... | collective-permute-start | bytes 442376 | tf_op jit(solution)/shard_map/ppermute | solution.py:18
  72.5 5.8 %collective-permute-done.7.refs_8_ = bf16[576,128]{1,0:T(8,128)(2,1)S(1)} collective-permute-done((bf16[576,128]{1,0:T(8,128)(2,1)S(1)}, bf16[576,128]{1,0:T(8,128)(2,1)S(1)}, u32[]{:S(2)}, u32[]{:S(2)}) %collective-permute-start.7) | collective-permute-done | bytes 147488 | tf_op jit(solution)/shard_map/ppermute | solution.py:18
  78.3 3.0 %shard_map.62 = (f32[128,1024]{1,0:T(8,128)S(1)}, f32[128,1024]{1,0:T(8,128)S(1)}, f32[8,128]{1,0:T(8,128)S(1)}, bf16[1024,1024]{1,0:T(8,128)(2,1)S(1)}, bf16[10...) custom-call(bf16[1168,128]{1,0:T(8,128)(2,1)S(1)} %shard_map.58.refs_0_, ...), custom_call_target="tpu_custom_call" | custom-call | flops 1073741824 | bytes 1048576 | tf_op jit(solution)/shard_map/pallas_call | solution.py:47
  81.3 1.4 copy-done.4
  82.7 0.8 copy-done.6
  83.5 4.8 %all-gather.2.cloned.1.call-done.refs_0_ = bf16[2,1024,1024]{2,1,0:T(8,128)(2,1)} async-done(((bf16[2,128,1024]{2,1,0:T(8,128)(2,1)}), bf16[2,1024,1024]{2,1,0:T(8,128)(2,1)}) %all-gather.2.cloned.1.call-update) | async-done | bytes 4194320 | tf_op jit(solution)/shard_map/all_gather | solution.py:126
  88.3 2.1 %shard_map.63 = (bf16[128,1024]{1,0:T(8,128)(2,1)S(1)}, bf16[1024,1024]{1,0:T(8,128)(2,1)S(1)}) custom-call(bf16[2,1024,1024]{2,1,0:T(8,128)(2,1)} %all-gather.2.cloned.1.call-done.refs_0_, bf16[2,128,1024]{2,1,0:T(8,128)(2,1)S(1)} %copy-done.3, bf16[16,1024]{1,0:T(8,128)(2,1)S(1)} %get-tuple-element.17.refs_2_.refs_7_), custom_call_target="tpu_custom_call" | custom-call | flops 268435456 | bytes 1048576 | tf_op jit(solution)/shard_map/pallas_call | solution.py:47
  90.4 1.9 %collective-permute-start.9 = (bf16[128,1024]{1,0:T(8,128)(2,1)S(1)}, bf16[128,1024]{1,0:T(8,128)(2,1)S(1)}, u32[]{:S(2)}, u32[]{:S(2)}) collective-permute-start(bf16[128,1024]{1,0:T(8,128)(2,1)S(1)} %get-tuple-element.18.refs_1_), channel_id=1, source_target_pairs={{0,8},{8,16},{16,24},{24,32},{32,40},{40,48},{48,56},{56,64},{64,7... | collective-permute-start | bytes 786440 | tf_op jit(solution)/shard_map/ppermute | solution.py:18
  92.3 1.6 %shard_map.64.refs_2_.refs_4_.refs_1_ = bf16[1024,1024]{1,0:T(8,128)(2,1)S(1)} custom-call(bf16[2,1024,1024]{2,1,0:T(8,128)(2,1)} %all-gather.2.cloned.1.call-done.refs_0_, bf16[128,1024]{1,0:T(8,128)(2,1)S(1)} %get-tuple-element.18.refs_1_), custom_call_target="tpu_custom_call" | custom-call | flops 1000 | bytes 1048576 | tf_op jit(solution)/shard_map/pallas_call | solution.py:47
  93.9 4.2 %collective-permute-done.9.refs_0_ = bf16[128,1024]{1,0:T(8,128)(2,1)S(1)} collective-permute-done((bf16[128,1024]{1,0:T(8,128)(2,1)S(1)}, bf16[128,1024]{1,0:T(8,128)(2,1)S(1)}, u32[]{:S(2)}, u32[]{:S(2)}) %collective-permute-start.9) | collective-permute-done | bytes 262176 | tf_op jit(solution)/shard_map/ppermute | solution.py:18
  98.1 1.3 shard_map.65
  99.3 0.3 copy-done.5
  99.7 3.0 %shard_map.66 = (bf16[272,1024]{1,0:T(8,128)(2,1)S(1)}, f32[128,1024]{1,0:T(8,128)S(1)}, f32[8,128]{1,0:T(8,128)S(1)}) custom-call(bf16[128,1024]{1,0:T(8,128)(2,1)S(1)} %collective-permute-done.9.refs_0_, bf16[256,1024]{1,0:T(8,128)(2,1)S(1)} %get-tuple-element.20.refs_1_, bf16[128,1024]{1,0:T(8,128)(2,1)S(1)} %get-tuple-element.21.refs_2_, ...), custom_call_target="tpu_custom_call" | custom-call | flops 1879048192 | bytes 1048576 | tf_op jit(solution)/shard_map/pallas_call | solution.py:47
  102.7 1.9 %collective-permute-start.10 = (bf16[272,1024]{1,0:T(8,128)(2,1)S(1)}, bf16[272,1024]{1,0:T(8,128)(2,1)S(1)}, u32[]{:S(2)}, u32[]{:S(2)}) collective-permute-start(bf16[272,1024]{1,0:T(8,128)(2,1)S(1)} %get-tuple-element.25.refs_3_), channel_id=1, source_target_pairs={{0,504},{8,0},{16,8},{24,16},{32,24},{40,32},{48,40},{56,48},{64,5... | collective-permute-start | bytes 1671176 | tf_op jit(solution)/shard_map/ppermute | solution.py:18
  104.6 2.4 %collective-permute-start.11 = (bf16[128,1024]{1,0:T(8,128)(2,1)S(1)}, bf16[128,1024]{1,0:T(8,128)(2,1)S(1)}, u32[]{:S(2)}, u32[]{:S(2)}) collective-permute-start(bf16[128,1024]{1,0:T(8,128)(2,1)S(1)} %get-tuple-element.26), channel_id=1, source_target_pairs={{0,8},{8,16},{16,24},{24,32},{32,40},{40,48},{48,56},{56,64},{64,7... | collective-permute-start | bytes 786440 | tf_op jit(solution)/shard_map/ppermute | solution.py:18
  107.0 5.3 %collective-permute-done.11.refs_0_ = bf16[128,1024]{1,0:T(8,128)(2,1)S(1)} collective-permute-done((bf16[128,1024]{1,0:T(8,128)(2,1)S(1)}, bf16[128,1024]{1,0:T(8,128)(2,1)S(1)}, u32[]{:S(2)}, u32[]{:S(2)}) %collective-permute-start.11) | collective-permute-done | bytes 262176 | tf_op jit(solution)/shard_map/ppermute | solution.py:18
  112.3 1.1 shard_map.67.refs_2_
  113.5 2.1 %collective-permute-start.12 = (bf16[144,1024]{1,0:T(8,128)(2,1)S(1)}, bf16[144,1024]{1,0:T(8,128)(2,1)S(1)}, u32[]{:S(2)}, u32[]{:S(2)}) collective-permute-start(bf16[144,1024]{1,0:T(8,128)(2,1)S(1)} %shard_map.67.refs_2_), channel_id=1, source_target_pairs={{0,504},{8,0},{16,8},{24,16},{32,24},{40,32},{48,40},{56,48},{64,5... | collective-permute-start | bytes 884744 | tf_op jit(solution)/shard_map/ppermute | solution.py:18
  115.5 0.5 shard_map.68.refs_5_
  116.0 0.0 copy-start.7
  116.0 1.5 shard_map.69.refs_6_.refs_5_
  117.5 2.2 %collective-permute-done.12.refs_0_ = bf16[144,1024]{1,0:T(8,128)(2,1)S(1)} collective-permute-done((bf16[144,1024]{1,0:T(8,128)(2,1)S(1)}, bf16[144,1024]{1,0:T(8,128)(2,1)S(1)}, u32[]{:S(2)}, u32[]{:S(2)}) %collective-permute-start.12) | collective-permute-done | bytes 294944 | tf_op jit(solution)/shard_map/ppermute | solution.py:18
  119.7 1.5 shard_map.70
  121.2 3.8 %collective-permute-start.13 = (bf16[144,1024]{1,0:T(8,128)(2,1)S(1)}, bf16[144,1024]{1,0:T(8,128)(2,1)S(1)}, u32[]{:S(2)}, u32[]{:S(2)}) collective-permute-start(bf16[144,1024]{1,0:T(8,128)(2,1)S(1)} %shard_map.70), channel_id=1, source_target_pairs={{0,504},{8,0},{16,8},{24,16},{32,24},{40,32},{48,40},{56,48},{64,5... | collective-permute-start | bytes 884744 | tf_op jit(solution)/shard_map/ppermute | solution.py:18
  125.1 3.3 %collective-permute-start.14 = (bf16[128,1024]{1,0:T(8,128)(2,1)S(1)}, bf16[128,1024]{1,0:T(8,128)(2,1)S(1)}, u32[]{:S(2)}, u32[]{:S(2)}) collective-permute-start(bf16[128,1024]{1,0:T(8,128)(2,1)S(1)} %shard_map.68.refs_5_), channel_id=1, source_target_pairs={{0,496},{8,504},{16,0},{24,8},{32,16},{40,24},{48,32},{56,40},{64,... | collective-permute-start | bytes 786440 | tf_op jit(solution)/shard_map/ppermute | solution.py:18
  128.4 17.0 %collective-permute-done.14.refs_2_ = bf16[128,1024]{1,0:T(8,128)(2,1)S(1)} collective-permute-done((bf16[128,1024]{1,0:T(8,128)(2,1)S(1)}, bf16[128,1024]{1,0:T(8,128)(2,1)S(1)}, u32[]{:S(2)}, u32[]{:S(2)}) %collective-permute-start.14) | collective-permute-done | bytes 262176 | tf_op jit(solution)/shard_map/ppermute | solution.py:18
  145.5 1.7 %shard_map.71 = (bf16[2,128,1024]{2,1,0:T(8,128)(2,1)}, bf16[2,128]{1,0:T(2,128)(2,1)}, bf16[2,128,1024]{2,1,0:T(8,128)(2,1)}) custom-call(bf16[272,1024]{1,0:T(8,128)(2,1)S(1)} %collective-permute-done.10.refs_0_, bf16[144,1024]{1,0:T(8,128)(2,1)S(1)} %collective-permute-done.13.refs_1_, bf16[128,1024]{1,0:T(8,128)(2,1)S(1)} %collective-permute-done.14.refs_2_, ...), custom_call_target="tpu_custom_call" | custom-call | flops 268435456 | bytes 1048576 | tf_op jit(solution)/shard_map/pallas_call | solution.py:47
  (19 shorter events, 0.1 us)
Async XLA Ops:
  7.2 71.1 %copy-start.3 = (bf16[2,128,1024]{2,1,0:T(8,128)(2,1)S(1)}, bf16[2,128,1024]{2,1,0:T(8,128)(2,1)}, u32[]{:S(2)}) copy-start(bf16[2,128,1024]{2,1,0:T(8,128)(2,1)} %refs_1_.3) | copy-start | bytes 1572868
  7.2 81.1 %all-gather.2.cloned.1.call-start = ((), (), s32[]{:S(2)}) async-start(), calls=%async_computation | async-start | bytes 4718592 | tf_op jit(solution)/shard_map/all_gather | solution.py:126
  7.9 1.0 copy-start
  9.0 0.7 copy-start.8
  9.8 18.0 %collective-permute-start = (bf16[1168,128]{1,0:T(8,128)(2,1)S(1)}, bf16[1168,128]{1,0:T(8,128)(2,1)S(1)}, u32[]{:S(2)}, u32[]{:S(2)}) collective-permute-start(bf16[1168,128]{1,0:T(8,128)(2,1)S(1)} %shard_map.58.refs_0_), channel_id=1, source_target_pairs={{0,1},{1,2},{2,3},{3,4},{4,5},{5,6},{6,7},{7,0},{8,9},{9,10},{10,1... | collective-permute-start | bytes 897032 | tf_op jit(solution)/shard_map/ppermute | solution.py:18
  14.1 17.0 %collective-permute-start.3 = (bf16[1168,128]{1,0:T(8,128)(2,1)S(1)}, bf16[1168,128]{1,0:T(8,128)(2,1)S(1)}, u32[]{:S(2)}, u32[]{:S(2)}) collective-permute-start(bf16[1168,128]{1,0:T(8,128)(2,1)S(1)} %shard_map.58.refs_0_), channel_id=1, source_target_pairs={{0,7},{1,0},{2,1},{3,2},{4,3},{5,4},{6,5},{7,6},{8,15},{9,8},{10,9... | collective-permute-start | bytes 897032 | tf_op jit(solution)/shard_map/ppermute | solution.py:18
  27.8 18.9 %collective-permute-start.1 = (bf16[1168,128]{1,0:T(8,128)(2,1)S(1)}, bf16[1168,128]{1,0:T(8,128)(2,1)S(1)}, u32[]{:S(2)}, u32[]{:S(2)}) collective-permute-start(bf16[1168,128]{1,0:T(8,128)(2,1)S(1)} %collective-permute-done.refs_1_), channel_id=1, source_target_pairs={{0,1},{1,2},{2,3},{3,4},{4,5},{5,6},{6,7},{7,0},{8,9},{9,10},{10,1... | collective-permute-start | bytes 897032 | tf_op jit(solution)/shard_map/ppermute | solution.py:18
  31.0 17.6 %collective-permute-start.4 = (bf16[1168,128]{1,0:T(8,128)(2,1)S(1)}, bf16[1168,128]{1,0:T(8,128)(2,1)S(1)}, u32[]{:S(2)}, u32[]{:S(2)}) collective-permute-start(bf16[1168,128]{1,0:T(8,128)(2,1)S(1)} %collective-permute-done.3.refs_4_), channel_id=1, source_target_pairs={{0,7},{1,0},{2,1},{3,2},{4,3},{5,4},{6,5},{7,6},{8,15},{9,8},{10,9... | collective-permute-start | bytes 897032 | tf_op jit(solution)/shard_map/ppermute | solution.py:18
  46.7 18.7 %collective-permute-start.2 = (bf16[1168,128]{1,0:T(8,128)(2,1)S(1)}, bf16[1168,128]{1,0:T(8,128)(2,1)S(1)}, u32[]{:S(2)}, u32[]{:S(2)}) collective-permute-start(bf16[1168,128]{1,0:T(8,128)(2,1)S(1)} %collective-permute-done.1.refs_2_), channel_id=1, source_target_pairs={{0,1},{1,2},{2,3},{3,4},{4,5},{5,6},{6,7},{7,0},{8,9},{9,10},{10,1... | collective-permute-start | bytes 897032 | tf_op jit(solution)/shard_map/ppermute | solution.py:18
  48.6 18.7 %collective-permute-start.5 = (bf16[1168,128]{1,0:T(8,128)(2,1)S(1)}, bf16[1168,128]{1,0:T(8,128)(2,1)S(1)}, u32[]{:S(2)}, u32[]{:S(2)}) collective-permute-start(bf16[1168,128]{1,0:T(8,128)(2,1)S(1)} %collective-permute-done.4.refs_5_), channel_id=1, source_target_pairs={{0,7},{1,0},{2,1},{3,2},{4,3},{5,4},{6,5},{7,6},{8,15},{9,8},{10,9... | collective-permute-start | bytes 897032 | tf_op jit(solution)/shard_map/ppermute | solution.py:18
  53.7 1.0 copy-start.2
  54.8 17.6 %collective-permute-start.8 = (bf16[128,1024]{1,0:T(8,128)(2,1)S(1)}, bf16[128,1024]{1,0:T(8,128)(2,1)S(1)}, u32[]{:S(2)}, u32[]{:S(2)}) collective-permute-start(bf16[128,1024]{1,0:T(8,128)(2,1)S(1)} %shard_map.61), channel_id=1, source_target_pairs={{0,8},{8,16},{16,24},{24,32},{32,40},{40,48},{48,56},{56,64},{64,7... | collective-permute-start | bytes 786440 | tf_op jit(solution)/shard_map/ppermute | solution.py:18
  65.4 13.0 %collective-permute-start.6 = (bf16[592,128]{1,0:T(8,128)(2,1)S(1)}, bf16[592,128]{1,0:T(8,128)(2,1)S(1)}, u32[]{:S(2)}, u32[]{:S(2)}) collective-permute-start(bf16[592,128]{1,0:T(8,128)(2,1)S(1)} %shard_map.59), channel_id=1, source_target_pairs={{0,1},{1,2},{2,3},{3,4},{4,5},{5,6},{6,7},{7,0},{8,9},{9,10},{10,1... | collective-permute-start | bytes 454664 | tf_op jit(solution)/shard_map/ppermute | solution.py:18
  67.3 11.0 %collective-permute-start.7 = (bf16[576,128]{1,0:T(8,128)(2,1)S(1)}, bf16[576,128]{1,0:T(8,128)(2,1)S(1)}, u32[]{:S(2)}, u32[]{:S(2)}) collective-permute-start(bf16[576,128]{1,0:T(8,128)(2,1)S(1)} %shard_map.60), channel_id=1, source_target_pairs={{0,7},{1,0},{2,1},{3,2},{4,3},{5,4},{6,5},{7,6},{8,15},{9,8},{10,9... | collective-permute-start | bytes 442376 | tf_op jit(solution)/shard_map/ppermute | solution.py:18
  81.3 1.4 copy-start.4
  82.7 0.8 copy-start.6
  90.4 7.7 %collective-permute-start.9 = (bf16[128,1024]{1,0:T(8,128)(2,1)S(1)}, bf16[128,1024]{1,0:T(8,128)(2,1)S(1)}, u32[]{:S(2)}, u32[]{:S(2)}) collective-permute-start(bf16[128,1024]{1,0:T(8,128)(2,1)S(1)} %get-tuple-element.18.refs_1_), channel_id=1, source_target_pairs={{0,8},{8,16},{16,24},{24,32},{32,40},{40,48},{48,56},{56,64},{64,7... | collective-permute-start | bytes 786440 | tf_op jit(solution)/shard_map/ppermute | solution.py:18
  98.1 1.6 %copy-start.5 = (bf16[1024,1024]{1,0:T(8,128)(2,1)S(1)}, bf16[1024,1024]{1,0:T(8,128)(2,1)}, u32[]{:S(2)}) copy-start(bf16[1024,1024]{1,0:T(8,128)(2,1)} %copy-done.4) | copy-start | bytes 6291460
  102.7 13.3 %collective-permute-start.10 = (bf16[272,1024]{1,0:T(8,128)(2,1)S(1)}, bf16[272,1024]{1,0:T(8,128)(2,1)S(1)}, u32[]{:S(2)}, u32[]{:S(2)}) collective-permute-start(bf16[272,1024]{1,0:T(8,128)(2,1)S(1)} %get-tuple-element.25.refs_3_), channel_id=1, source_target_pairs={{0,504},{8,0},{16,8},{24,16},{32,24},{40,32},{48,40},{56,48},{64,5... | collective-permute-start | bytes 1671176 | tf_op jit(solution)/shard_map/ppermute | solution.py:18
  104.6 7.7 %collective-permute-start.11 = (bf16[128,1024]{1,0:T(8,128)(2,1)S(1)}, bf16[128,1024]{1,0:T(8,128)(2,1)S(1)}, u32[]{:S(2)}, u32[]{:S(2)}) collective-permute-start(bf16[128,1024]{1,0:T(8,128)(2,1)S(1)} %get-tuple-element.26), channel_id=1, source_target_pairs={{0,8},{8,16},{16,24},{24,32},{32,40},{40,48},{48,56},{56,64},{64,7... | collective-permute-start | bytes 786440 | tf_op jit(solution)/shard_map/ppermute | solution.py:18
  113.4 2.5 %copy-start.1 = (bf16[2,128,1024]{2,1,0:T(8,128)(2,1)S(1)}, bf16[2,128,1024]{2,1,0:T(8,128)(2,1)}, u32[]{:S(2)}) copy-start(bf16[2,128,1024]{2,1,0:T(8,128)(2,1)} %refs_6_.1) | copy-start | bytes 1572868
  113.5 6.3 %collective-permute-start.12 = (bf16[144,1024]{1,0:T(8,128)(2,1)S(1)}, bf16[144,1024]{1,0:T(8,128)(2,1)S(1)}, u32[]{:S(2)}, u32[]{:S(2)}) collective-permute-start(bf16[144,1024]{1,0:T(8,128)(2,1)S(1)} %shard_map.67.refs_2_), channel_id=1, source_target_pairs={{0,504},{8,0},{16,8},{24,16},{32,24},{40,32},{48,40},{56,48},{64,5... | collective-permute-start | bytes 884744 | tf_op jit(solution)/shard_map/ppermute | solution.py:18
  116.0 3.7 %copy-start.7 = (f32[128,1024]{1,0:T(8,128)S(1)}, f32[128,1024]{1,0:T(8,128)}, u32[]{:S(2)}) copy-start(f32[128,1024]{1,0:T(8,128)} %copy-done.6) | copy-start | bytes 1572868
  119.7 25.7 %copy-start.9 = (bf16[2,128]{1,0:T(2,128)(2,1)S(1)}, bf16[2,128]{1,0:T(2,128)(2,1)}, u32[]{:S(2)}) copy-start(bf16[2,128]{1,0:T(2,128)(2,1)} %refs_7_.1) | copy-start | bytes 1540
  121.2 24.2 %collective-permute-start.13 = (bf16[144,1024]{1,0:T(8,128)(2,1)S(1)}, bf16[144,1024]{1,0:T(8,128)(2,1)S(1)}, u32[]{:S(2)}, u32[]{:S(2)}) collective-permute-start(bf16[144,1024]{1,0:T(8,128)(2,1)S(1)} %shard_map.70), channel_id=1, source_target_pairs={{0,504},{8,0},{16,8},{24,16},{32,24},{40,32},{48,40},{56,48},{64,5... | collective-permute-start | bytes 884744 | tf_op jit(solution)/shard_map/ppermute | solution.py:18
  125.1 20.4 %collective-permute-start.14 = (bf16[128,1024]{1,0:T(8,128)(2,1)S(1)}, bf16[128,1024]{1,0:T(8,128)(2,1)S(1)}, u32[]{:S(2)}, u32[]{:S(2)}) collective-permute-start(bf16[128,1024]{1,0:T(8,128)(2,1)S(1)} %shard_map.68.refs_5_), channel_id=1, source_target_pairs={{0,496},{8,504},{16,0},{24,8},{32,16},{40,24},{48,32},{56,40},{64,... | collective-permute-start | bytes 786440 | tf_op jit(solution)/shard_map/ppermute | solution.py:18
Sparse Core Ops, SparseCore 0:
  10.1 78.1 all-gather.1

commit v2 on v1

--- a/solution.py
+++ b/solution.py
@@ -34,36 +34,38 @@
     return pltpu.with_memory_space_constraint(array, pltpu.VMEM)
 
 
-def apart(array):
-    return pltpu.with_memory_space_constraint(array, pltpu.HBM)
-
-
-def call(body, ins, outs, flops, after=(), wide=(), scratch=()):
-    count = len(ins) + len(wide)
+def call(body, ins, outs, flops, after=()):
+    count = len(ins)
 
     def run(*refs):
         body(*refs[:count], *refs[count + len(after) :])
 
     return pl.pallas_call(
         run,
-        in_specs=[HBM] * len(wide) + [VMEM] * len(ins) + [HBM] * len(after),
+        in_specs=[VMEM] * count + [HBM] * len(after),
         out_specs=tuple(VMEM for _ in outs),
         out_shape=tuple(outs),
-        scratch_shapes=scratch,
         cost_estimate=pl.CostEstimate(flops=flops, bytes_accessed=2**20, transcendentals=0),
         compiler_params=pltpu.CompilerParams(vmem_limit_bytes=GRANT),
-    )(*[apart(array) for array in wide], *[near(array) for array in ins], *after)
-
-
-def part(array, picked, shape):
+    )(*[near(array) for array in ins], *after)
+
+
+def part(array, picked, shape, after=()):
     def copy(ref, out):
         out[...] = ref[picked]
 
-    return call(copy, [array], [kept(shape, BF16)], 1000)[0]
+    return call(copy, [array], [kept(shape, BF16)], 1000, after)[0]
 
 
 def slot(offset, count):
     return lax.rem(lax.axis_index("row") + (offset + count), count)
+
+
+def join(pieces, whole, count):
+    rows = whole.shape[0] // count
+    for offset, panel in pieces:
+        start = pl.multiple_of(slot(offset, count) * rows, rows)
+        whole[pl.ds(start, rows), :] = panel
 
 
 def unpack(pieces, whole, count):
@@ -121,9 +123,11 @@
         odd = hop(halves[1], "row", -1)
         arrays = [block] + fore[1:] + back[1:]
         offsets = [0] + [-k for k in range(1, half)] + list(range(1, half))
-        return arrays, offsets, even, odd
-
-    e_all = lax.all_gather(trans, "row", axis=1, tiled=True)
+        return arrays, offsets, even, odd, halves
+
+    e_arrays, offsets, e_even_last, e_odd_last, e_halves = gather(
+        trans, (lambda x: part(x, 0, (rows, size)), lambda x: part(x, 1, (rows, size)))
+    )
     b1_in = hop(part(trans, 1, (rows, size)), "tm", 1)
 
     def pack(l_ref, g_ref, out):
@@ -144,14 +148,28 @@
         out[packed : packed + TAIL, :] = tile.astype(BF16)
 
     (sent,) = call(pack, [spread, offset], [kept((2 * packed + TAIL, rows), BF16)], 1000)
-    l_arrays, offsets, l_even_last, l_odd_last = gather(
+    l_arrays, _, l_even_last, l_odd_last, _ = gather(
         sent,
         (
-            lambda x: part(x, slice(0, packed + TAIL), (packed + TAIL, rows)),
-            lambda x: part(x, slice(packed + TAIL, 2 * packed + TAIL), (packed, rows)),
+            lambda x: part(x, slice(0, packed + TAIL), (packed + TAIL, rows), e_halves),
+            lambda x: part(x, slice(packed + TAIL, 2 * packed + TAIL), (packed, rows), e_halves),
         ),
     )
     n = len(l_arrays)
+
+    def first(*refs):
+        last, out, joined = refs[n], refs[n + 1], refs[n + 2]
+        join([(way, ref[1]) for way, ref in zip(offsets, refs)] + [(half, last[...])], joined, count)
+        out[...] = nn(refs[0][0], joined[...]).astype(BF16)
+
+    x1, e_odd = call(first, e_arrays + [e_odd_last], [panel, whole], product)
+    x1_in = hop(x1, "tm", 1)
+
+    def evens(*refs):
+        last, joined = refs[n], refs[n + 1]
+        join([(way, ref[0]) for way, ref in zip(offsets, refs)] + [(half, last[...])], joined, count)
+
+    (e_even,) = call(evens, e_arrays + [e_even_last], [whole], 1000, after=(x1,))
 
     def opened(*refs):
         even_last, odd_last, b1_ref, own = refs[n : n + 4]
@@ -172,25 +190,8 @@
         l_arrays + [l_even_last, l_odd_last, b1_in, trans],
         [wide, wide, line, whole, whole, kept((TAIL, size), BF16)],
         4 * product,
-    )
-
-    def first(all_ref, own, out, odd, sem):
-        copy = pltpu.make_async_copy(all_ref.at[1], odd, sem)
-        copy.start()
-        copy.wait()
-        out[...] = nn(own[0], odd[...]).astype(BF16)
-
-    x1, e_odd = call(
-        first, [trans], [panel, whole], product, after=(g_all,), wide=(e_all,), scratch=(pltpu.SemaphoreType.DMA,)
-    )
-    x1_in = hop(x1, "tm", 1)
-
-    def evens(all_ref, even, sem):
-        copy = pltpu.make_async_copy(all_ref.at[0], even, sem)
-        copy.start()
-        copy.wait()
-
-    (e_even,) = call(evens, [], [whole], 1000, after=(x1,), wide=(e_all,), scratch=(pltpu.SemaphoreType.DMA,))
+        after=(e_even,),
+    )
 
     def second(x1_ref, b1_ref, even, odd, x3_ref, b3_ref, x2_ref):
         past = lax.axis_index("tm") < 1
@@ -202,7 +203,7 @@
         b3_ref[...] = three[rows:]
         x2_ref[...] = two
 
-    x3, b3, x2 = call(second, [x1_in, b1_in, e_even, e_odd], [panel, panel, pair], 4 * product)
+    x3, b3, x2 = call(second, [x1_in, b1_in, e_even, e_odd], [panel, panel, pair], 4 * product, after=(g_all,))
     b3_in = hop(b3, "tm", 1)
 
     def third(x1_ref, x2_ref, x3_ref, line_ref, even, l_ev, l_od, g_ref, m_ref, far_ref, row_ref):
@@ -242,12 +243,6 @@
     (b4,) = call(fifth, [b3_in, e_even], [panel], product, after=(v,))
     b4_in = hop(b4, "tm", -2)
 
-    def seventh(w_ref, head_ref, even, odd, l_own, out):
-        inner = head_ref[...] + nt(w_ref[:rows, :], odd[...])
-        out[...] = (nt(inner.astype(BF16), even[...]) + l_own[0].astype(F32)).astype(BF16)
-
-    (l_first,) = call(seventh, [w_in, head, e_even, e_odd, spread], [panel], 2 * product, after=(b4,))
-
     def sixth(v_ref, close_ref, far_ref, line_ref, even, odd, m_ref):
         past = lax.axis_index("tm") < 1
         behind = far_ref[...] + nt(v_ref[:rows, :], odd[...])
@@ -257,8 +252,14 @@
         m_ref[rows:, :] = jnp.zeros((TAIL, size), BF16)
         m_ref[rows:, :rows] = two_rows(jnp.where(past, 0.0, row))
 
-    (u,) = call(sixth, [v_in, close, far, line2, e_even, e_odd], [short], 2 * product, after=(l_first,))
+    (u,) = call(sixth, [v_in, close, far, line2, e_even, e_odd], [short], 2 * product, after=(b4,))
     u_in = hop(u, "tm", -1)
+
+    def seventh(w_ref, head_ref, even, odd, l_own, out):
+        inner = head_ref[...] + nt(w_ref[:rows, :], odd[...])
+        out[...] = (nt(inner.astype(BF16), even[...]) + l_own[0].astype(F32)).astype(BF16)
+
+    (l_first,) = call(seventh, [w_in, head, e_even, e_odd, spread], [panel], 2 * product, after=(u,))
 
     def eighth(w_ref, u_ref, b4_ref, line_ref, odd, l_ref, l_own, g_own, e_out, g_out, l_out):
         l_out[1] = (nt(u_ref[:rows, :], odd[...]) + l_own[1].astype(F32)).astype(BF16)

time: 155 us -> 141 us (0.910)
  starting transfers between devices: 51.9 us -> 81.4 us
  waiting for transfers between devices: 65.1 us -> 41.8 us
  between operations: 14.3 us -> 1.06 us
  local copies, waits for them, and re-layouts: 5.24 us -> 1.71 us
  Pallas kernels: 17.5 us -> 14.7 us
    ppermute x15 -> x23, starting transfers between devices: 51.8 us -> 81.4 us  [hop(): lax.ppermute(block, axis, [(i, (i + distance) % size) for i in range(size)])]
    ppermute x15 -> x23, waiting for transfers between devices: 59.6 us -> 41.8 us  [hop(): lax.ppermute(block, axis, [(i, (i + distance) % size) for i in range(size)])]
    all_gather x1 -> x0, waiting for transfers between devices: 4.82 us -> none  [on_device(): e_all = lax.all_gather(trans, 'row', axis=1, tiled=True)]
    unnamed x20 -> x10, local copies, waits for them, and re-layouts: 5.24 us -> 1.71 us
    pallas_call x14 -> x16, Pallas kernels: 17.5 us -> 14.7 us  [call(): pl.pallas_call(run, in_specs=[VMEM] * count + [HBM] * len(after), out_spe...]
  transfers between devices with their start and end apart: 16 -> 23, of which waited for: 10 -> 8; matrix products, arithmetic and copies ran while one was open for 0% -> 0% of each run, Pallas kernels for 5% -> 7%
where the time goes in v2:
time: 141 us
  starting transfers between devices  81.4 us (58%)
  waiting for transfers between devices  41.8 us (30%)
  Pallas kernels  14.7 us (10%)
  local copies, waits for them, and re-layouts  1.71 us (1%)
    ppermute x23, starting transfers between devices, hop(): lax.ppermute(block, axis, [(i, (i + distance) % size) for i in range(size)])  81.4 us
    ppermute x23, waiting for transfers between devices, hop(): lax.ppermute(block, axis, [(i, (i + distance) % size) for i in range(size)])  41.8 us
    pallas_call x16, Pallas kernels, call(): pl.pallas_call(run, in_specs=[VMEM] * count + [HBM] * len(after), out_spe...  14.7 us
  transfers between devices with their start and end apart: 23, of which 8 were waited for; matrix products, arithmetic and copies ran while one was open for 0% of the time, Pallas kernels for 7%

profile of v2, /device:TPU:62, one launch (start us, length us, event | category | flops | bytes accessed | tf_op | source)
XLA Modules:
  0.0 140.7 jit_solution(16903441500363486412)
XLA Ops:
  0.6 11.1 %collective-permute-start.3 = (bf16[2,128,1024]{2,1,0:T(8,128)(2,1)}, bf16[2,128,1024]{2,1,0:T(8,128)(2,1)S(1)}, u32[]{:S(2)}, u32[]{:S(2)}) collective-permute-start(bf16[2,128,1024]{2,1,0:T(8,128)(2,1)} %refs_10_.1), channel_id=1, source_target_pairs={{0,7},{1,0},{2,1},{3,2},{4,3},{5,4},{6,5},{7,6},{8,15},{9,8},{10,9... | collective-permute-start | bytes 1572872 | tf_op jit(solution)/shard_map/ppermute | solution.py:18
  11.7 1.9 %collective-permute-start = (bf16[2,128,1024]{2,1,0:T(8,128)(2,1)}, bf16[2,128,1024]{2,1,0:T(8,128)(2,1)S(1)}, u32[]{:S(2)}, u32[]{:S(2)}) collective-permute-start(bf16[2,128,1024]{2,1,0:T(8,128)(2,1)} %refs_10_.1), channel_id=1, source_target_pairs={{0,1},{1,2},{2,3},{3,4},{4,5},{5,6},{6,7},{7,0},{8,9},{9,10},{10,1... | collective-permute-start | bytes 1572872 | tf_op jit(solution)/shard_map/ppermute | solution.py:18
  13.7 9.5 %collective-permute-done.3.refs_4_ = bf16[2,128,1024]{2,1,0:T(8,128)(2,1)S(1)} collective-permute-done((bf16[2,128,1024]{2,1,0:T(8,128)(2,1)}, bf16[2,128,1024]{2,1,0:T(8,128)(2,1)S(1)}, u32[]{:S(2)}, u32[]{:S(2)}) %collective-permute-start.3) | collective-permute-done | bytes 524320 | tf_op jit(solution)/shard_map/ppermute | solution.py:18
  23.2 5.5 %collective-permute-start.4 = (bf16[2,128,1024]{2,1,0:T(8,128)(2,1)S(1)}, bf16[2,128,1024]{2,1,0:T(8,128)(2,1)S(1)}, u32[]{:S(2)}, u32[]{:S(2)}) collective-permute-start(bf16[2,128,1024]{2,1,0:T(8,128)(2,1)S(1)} %collective-permute-done.3.refs_4_), channel_id=1, source_target_pairs={{0,7},{1,0},{2,1},{3,2},{4,3},{5,4},{6,5},{7,6},{8,15},{9,8},{10,9... | collective-permute-start | bytes 1572872 | tf_op jit(solution)/shard_map/ppermute | solution.py:18
  28.7 0.0 collective-permute-done.refs_1_
  28.7 1.9 %collective-permute-start.1 = (bf16[2,128,1024]{2,1,0:T(8,128)(2,1)S(1)}, bf16[2,128,1024]{2,1,0:T(8,128)(2,1)S(1)}, u32[]{:S(2)}, u32[]{:S(2)}) collective-permute-start(bf16[2,128,1024]{2,1,0:T(8,128)(2,1)S(1)} %collective-permute-done.refs_1_), channel_id=1, source_target_pairs={{0,1},{1,2},{2,3},{3,4},{4,5},{5,6},{6,7},{7,0},{8,9},{9,10},{10,1... | collective-permute-start | bytes 1572872 | tf_op jit(solution)/shard_map/ppermute | solution.py:18
  30.6 0.0 copy-start.1
  30.6 1.0 copy-done.1
  31.7 0.7 copy-done.3
  32.3 0.2 shard_map.63.refs_0_
  32.5 1.9 %collective-permute-start.10 = (bf16[1168,128]{1,0:T(8,128)(2,1)S(1)}, bf16[1168,128]{1,0:T(8,128)(2,1)S(1)}, u32[]{:S(2)}, u32[]{:S(2)}) collective-permute-start(bf16[1168,128]{1,0:T(8,128)(2,1)S(1)} %shard_map.63.refs_0_), channel_id=1, source_target_pairs={{0,1},{1,2},{2,3},{3,4},{4,5},{5,6},{6,7},{7,0},{8,9},{9,10},{10,1... | collective-permute-start | bytes 897032 | tf_op jit(solution)/shard_map/ppermute | solution.py:18
  34.4 5.1 %collective-permute-start.13 = (bf16[1168,128]{1,0:T(8,128)(2,1)S(1)}, bf16[1168,128]{1,0:T(8,128)(2,1)S(1)}, u32[]{:S(2)}, u32[]{:S(2)}) collective-permute-start(bf16[1168,128]{1,0:T(8,128)(2,1)S(1)} %shard_map.63.refs_0_), channel_id=1, source_target_pairs={{0,7},{1,0},{2,1},{3,2},{4,3},{5,4},{6,5},{7,6},{8,15},{9,8},{10,9... | collective-permute-start | bytes 897032 | tf_op jit(solution)/shard_map/ppermute | solution.py:18
  39.6 0.3 collective-permute-done.4.refs_5_
  39.9 5.6 %collective-permute-start.5 = (bf16[2,128,1024]{2,1,0:T(8,128)(2,1)S(1)}, bf16[2,128,1024]{2,1,0:T(8,128)(2,1)S(1)}, u32[]{:S(2)}, u32[]{:S(2)}) collective-permute-start(bf16[2,128,1024]{2,1,0:T(8,128)(2,1)S(1)} %collective-permute-done.4.refs_5_), channel_id=1, source_target_pairs={{0,7},{1,0},{2,1},{3,2},{4,3},{5,4},{6,5},{7,6},{8,15},{9,8},{10,9... | collective-permute-start | bytes 1572872 | tf_op jit(solution)/shard_map/ppermute | solution.py:18
  45.5 1.1 collective-permute-done.1.refs_2_
  46.6 1.9 %collective-permute-start.2 = (bf16[2,128,1024]{2,1,0:T(8,128)(2,1)S(1)}, bf16[2,128,1024]{2,1,0:T(8,128)(2,1)S(1)}, u32[]{:S(2)}, u32[]{:S(2)}) collective-permute-start(bf16[2,128,1024]{2,1,0:T(8,128)(2,1)S(1)} %collective-permute-done.1.refs_2_), channel_id=1, source_target_pairs={{0,1},{1,2},{2,3},{3,4},{4,5},{5,6},{6,7},{7,0},{8,9},{9,10},{10,1... | collective-permute-start | bytes 1572872 | tf_op jit(solution)/shard_map/ppermute | solution.py:18
  48.5 4.5 %collective-permute-done.10.refs_1_ = bf16[1168,128]{1,0:T(8,128)(2,1)S(1)} collective-permute-done((bf16[1168,128]{1,0:T(8,128)(2,1)S(1)}, bf16[1168,128]{1,0:T(8,128)(2,1)S(1)}, u32[]{:S(2)}, u32[]{:S(2)}) %collective-permute-start.10) | collective-permute-done | bytes 299040 | tf_op jit(solution)/shard_map/ppermute | solution.py:18
  53.0 1.9 %collective-permute-start.11 = (bf16[1168,128]{1,0:T(8,128)(2,1)S(1)}, bf16[1168,128]{1,0:T(8,128)(2,1)S(1)}, u32[]{:S(2)}, u32[]{:S(2)}) collective-permute-start(bf16[1168,128]{1,0:T(8,128)(2,1)S(1)} %collective-permute-done.10.refs_1_), channel_id=1, source_target_pairs={{0,1},{1,2},{2,3},{3,4},{4,5},{5,6},{6,7},{7,0},{8,9},{9,10},{10,1... | collective-permute-start | bytes 897032 | tf_op jit(solution)/shard_map/ppermute | solution.py:18
  54.9 5.1 %collective-permute-start.14 = (bf16[1168,128]{1,0:T(8,128)(2,1)S(1)}, bf16[1168,128]{1,0:T(8,128)(2,1)S(1)}, u32[]{:S(2)}, u32[]{:S(2)}) collective-permute-start(bf16[1168,128]{1,0:T(8,128)(2,1)S(1)} %collective-permute-done.13.refs_4_), channel_id=1, source_target_pairs={{0,7},{1,0},{2,1},{3,2},{4,3},{5,4},{6,5},{7,6},{8,15},{9,8},{10,9... | collective-permute-start | bytes 897032 | tf_op jit(solution)/shard_map/ppermute | solution.py:18
  60.1 8.3 %collective-permute-done.11.refs_2_ = bf16[1168,128]{1,0:T(8,128)(2,1)S(1)} collective-permute-done((bf16[1168,128]{1,0:T(8,128)(2,1)S(1)}, bf16[1168,128]{1,0:T(8,128)(2,1)S(1)}, u32[]{:S(2)}, u32[]{:S(2)}) %collective-permute-start.11) | collective-permute-done | bytes 299040 | tf_op jit(solution)/shard_map/ppermute | solution.py:18
  68.4 1.9 %collective-permute-start.12 = (bf16[1168,128]{1,0:T(8,128)(2,1)S(1)}, bf16[1168,128]{1,0:T(8,128)(2,1)S(1)}, u32[]{:S(2)}, u32[]{:S(2)}) collective-permute-start(bf16[1168,128]{1,0:T(8,128)(2,1)S(1)} %collective-permute-done.11.refs_2_), channel_id=1, source_target_pairs={{0,1},{1,2},{2,3},{3,4},{4,5},{5,6},{6,7},{7,0},{8,9},{9,10},{10,1... | collective-permute-start | bytes 897032 | tf_op jit(solution)/shard_map/ppermute | solution.py:18
  70.3 5.1 %collective-permute-start.6 = (bf16[128,1024]{1,0:T(8,128)(2,1)S(1)}, bf16[128,1024]{1,0:T(8,128)(2,1)S(1)}, u32[]{:S(2)}, u32[]{:S(2)}) collective-permute-start(bf16[128,1024]{1,0:T(8,128)(2,1)S(1)} %shard_map.58.refs_2_), channel_id=1, source_target_pairs={{0,7},{1,0},{2,1},{3,2},{4,3},{5,4},{6,5},{7,6},{8,15},{9,8},{10,9... | collective-permute-start | bytes 786440 | tf_op jit(solution)/shard_map/ppermute | solution.py:18
  75.5 1.9 %collective-permute-start.15 = (bf16[1168,128]{1,0:T(8,128)(2,1)S(1)}, bf16[1168,128]{1,0:T(8,128)(2,1)S(1)}, u32[]{:S(2)}, u32[]{:S(2)}) collective-permute-start(bf16[1168,128]{1,0:T(8,128)(2,1)S(1)} %collective-permute-done.14.refs_5_), channel_id=1, source_target_pairs={{0,7},{1,0},{2,1},{3,2},{4,3},{5,4},{6,5},{7,6},{8,15},{9,8},{10,9... | collective-permute-start | bytes 897032 | tf_op jit(solution)/shard_map/ppermute | solution.py:18
  77.5 3.9 %collective-permute-start.9 = (bf16[128,1024]{1,0:T(8,128)(2,1)S(1)}, bf16[128,1024]{1,0:T(8,128)(2,1)S(1)}, u32[]{:S(2)}, u32[]{:S(2)}) collective-permute-start(bf16[128,1024]{1,0:T(8,128)(2,1)S(1)} %shard_map.61.refs_1_), channel_id=1, source_target_pairs={{0,1},{1,2},{2,3},{3,4},{4,5},{5,6},{6,7},{7,0},{8,9},{9,10},{10,1... | collective-permute-start | bytes 786440 | tf_op jit(solution)/shard_map/ppermute | solution.py:18
  81.4 1.9 %collective-permute-start.8 = (bf16[128,1024]{1,0:T(8,128)(2,1)S(1)}, bf16[128,1024]{1,0:T(8,128)(2,1)S(1)}, u32[]{:S(2)}, u32[]{:S(2)}) collective-permute-start(bf16[128,1024]{1,0:T(8,128)(2,1)S(1)} %shard_map.60), channel_id=1, source_target_pairs={{0,8},{8,16},{16,24},{24,32},{32,40},{40,48},{48,56},{56,64},{64,7... | collective-permute-start | bytes 786440 | tf_op jit(solution)/shard_map/ppermute | solution.py:18
  83.4 0.6 shard_map.59
  84.0 1.9 %collective-permute-start.7 = (bf16[128,1024]{1,0:T(8,128)(2,1)S(1)}, bf16[128,1024]{1,0:T(8,128)(2,1)S(1)}, u32[]{:S(2)}, u32[]{:S(2)}) collective-permute-start(bf16[128,1024]{1,0:T(8,128)(2,1)S(1)} %get-tuple-element.17.refs_8_), channel_id=1, source_target_pairs={{0,8},{8,16},{16,24},{24,32},{32,40},{40,48},{48,56},{56,64},{64,7... | collective-permute-start | bytes 786440 | tf_op jit(solution)/shard_map/ppermute | solution.py:18
  85.9 1.9 %collective-permute-start.16 = (bf16[592,128]{1,0:T(8,128)(2,1)S(1)}, bf16[592,128]{1,0:T(8,128)(2,1)S(1)}, u32[]{:S(2)}, u32[]{:S(2)}) collective-permute-start(bf16[592,128]{1,0:T(8,128)(2,1)S(1)} %shard_map.64), channel_id=1, source_target_pairs={{0,1},{1,2},{2,3},{3,4},{4,5},{5,6},{6,7},{7,0},{8,9},{9,10},{10,1... | collective-permute-start | bytes 454664 | tf_op jit(solution)/shard_map/ppermute | solution.py:18
  87.9 5.1 %collective-permute-start.17 = (bf16[576,128]{1,0:T(8,128)(2,1)S(1)}, bf16[576,128]{1,0:T(8,128)(2,1)S(1)}, u32[]{:S(2)}, u32[]{:S(2)}) collective-permute-start(bf16[576,128]{1,0:T(8,128)(2,1)S(1)} %shard_map.65), channel_id=1, source_target_pairs={{0,7},{1,0},{2,1},{3,2},{4,3},{5,4},{6,5},{7,6},{8,15},{9,8},{10,9... | collective-permute-start | bytes 442376 | tf_op jit(solution)/shard_map/ppermute | solution.py:18
  93.1 0.2 shard_map.62.refs_11_.refs_2_.refs_4_.refs_1_
  93.2 2.6 %collective-permute-done.17.refs_8_ = bf16[576,128]{1,0:T(8,128)(2,1)S(1)} collective-permute-done((bf16[576,128]{1,0:T(8,128)(2,1)S(1)}, bf16[576,128]{1,0:T(8,128)(2,1)S(1)}, u32[]{:S(2)}, u32[]{:S(2)}) %collective-permute-start.17) | collective-permute-done | bytes 147488 | tf_op jit(solution)/shard_map/ppermute | solution.py:18
  95.8 3.0 %shard_map.66 = (f32[128,1024]{1,0:T(8,128)S(1)}, f32[128,1024]{1,0:T(8,128)S(1)}, f32[8,128]{1,0:T(8,128)S(1)}, bf16[1024,1024]{1,0:T(8,128)(2,1)S(1)}, bf16[10...) custom-call(bf16[1168,128]{1,0:T(8,128)(2,1)S(1)} %shard_map.63.refs_0_, ...), custom_call_target="tpu_custom_call" | custom-call | flops 1073741824 | bytes 1048576 | tf_op jit(solution)/shard_map/pallas_call | solution.py:43
  98.8 1.3 shard_map.67
  100.1 1.9 %collective-permute-start.19 = (bf16[128,1024]{1,0:T(8,128)(2,1)S(1)}, bf16[128,1024]{1,0:T(8,128)(2,1)S(1)}, u32[]{:S(2)}, u32[]{:S(2)}) collective-permute-start(bf16[128,1024]{1,0:T(8,128)(2,1)S(1)} %get-tuple-element.26), channel_id=1, source_target_pairs={{0,8},{8,16},{16,24},{24,32},{32,40},{40,48},{48,56},{56,64},{64,7... | collective-permute-start | bytes 786440 | tf_op jit(solution)/shard_map/ppermute | solution.py:18
  102.0 3.0 %shard_map.68 = (bf16[272,1024]{1,0:T(8,128)(2,1)S(1)}, f32[128,1024]{1,0:T(8,128)S(1)}, f32[8,128]{1,0:T(8,128)S(1)}) custom-call(bf16[128,1024]{1,0:T(8,128)(2,1)S(1)} %collective-permute-done.7.refs_0_, bf16[256,1024]{1,0:T(8,128)(2,1)S(1)} %get-tuple-element.20.refs_1_, bf16[128,1024]{1,0:T(8,128)(2,1)S(1)} %get-tuple-element.21.refs_2_, ...), custom_call_target="tpu_custom_call" | custom-call | flops 1879048192 | bytes 1048576 | tf_op jit(solution)/shard_map/pallas_call | solution.py:43
  105.1 2.7 %collective-permute-done.19.refs_0_ = bf16[128,1024]{1,0:T(8,128)(2,1)S(1)} collective-permute-done((bf16[128,1024]{1,0:T(8,128)(2,1)S(1)}, bf16[128,1024]{1,0:T(8,128)(2,1)S(1)}, u32[]{:S(2)}, u32[]{:S(2)}) %collective-permute-start.19) | collective-permute-done | bytes 262176 | tf_op jit(solution)/shard_map/ppermute | solution.py:18
  107.8 1.1 shard_map.69.refs_2_
  109.0 1.9 %collective-permute-start.20 = (bf16[144,1024]{1,0:T(8,128)(2,1)S(1)}, bf16[144,1024]{1,0:T(8,128)(2,1)S(1)}, u32[]{:S(2)}, u32[]{:S(2)}) collective-permute-start(bf16[144,1024]{1,0:T(8,128)(2,1)S(1)} %shard_map.69.refs_2_), channel_id=1, source_target_pairs={{0,504},{8,0},{16,8},{24,16},{32,24},{40,32},{48,40},{56,48},{64,5... | collective-permute-start | bytes 884744 | tf_op jit(solution)/shard_map/ppermute | solution.py:18
  110.9 4.4 %collective-permute-start.18 = (bf16[272,1024]{1,0:T(8,128)(2,1)S(1)}, bf16[272,1024]{1,0:T(8,128)(2,1)S(1)}, u32[]{:S(2)}, u32[]{:S(2)}) collective-permute-start(bf16[272,1024]{1,0:T(8,128)(2,1)S(1)} %get-tuple-element.25.refs_3_), channel_id=1, source_target_pairs={{0,504},{8,0},{16,8},{24,16},{32,24},{40,32},{48,40},{56,48},{64,5... | collective-permute-start | bytes 1671176 | tf_op jit(solution)/shard_map/ppermute | solution.py:18
  115.3 0.5 shard_map.70.refs_6_
  115.7 0.0 copy-start.2
  115.7 1.5 %shard_map.71.refs_5_ = bf16[144,1024]{1,0:T(8,128)(2,1)S(1)} custom-call(bf16[144,1024]{1,0:T(8,128)(2,1)S(1)} %collective-permute-done.20.refs_0_, f32[128,1024]{1,0:T(8,128)S(1)} %get-tuple-element.27.refs_1_, f32[128,1024]{1,0:T(8,128)S(1)} %get-tuple-element.28.refs_2_, f32[8,128]{1,0:T(8,128)S(1)} %get-tuple-element.29.refs_3_, ...), custom_call_target="tpu_custom_call" | custom-call | flops 536870912 | bytes 1048576 | tf_op jit(solution)/shard_map/pallas_call | solution.py:43
  117.3 3.2 %collective-permute-start.21 = (bf16[144,1024]{1,0:T(8,128)(2,1)S(1)}, bf16[144,1024]{1,0:T(8,128)(2,1)S(1)}, u32[]{:S(2)}, u32[]{:S(2)}) collective-permute-start(bf16[144,1024]{1,0:T(8,128)(2,1)S(1)} %shard_map.71.refs_5_), channel_id=1, source_target_pairs={{0,504},{8,0},{16,8},{24,16},{32,24},{40,32},{48,40},{56,48},{64,5... | collective-permute-start | bytes 884744 | tf_op jit(solution)/shard_map/ppermute | solution.py:18
  120.4 4.3 %collective-permute-start.22 = (bf16[128,1024]{1,0:T(8,128)(2,1)S(1)}, bf16[128,1024]{1,0:T(8,128)(2,1)S(1)}, u32[]{:S(2)}, u32[]{:S(2)}) collective-permute-start(bf16[128,1024]{1,0:T(8,128)(2,1)S(1)} %shard_map.70.refs_6_), channel_id=1, source_target_pairs={{0,496},{8,504},{16,0},{24,8},{32,16},{40,24},{48,32},{56,40},{64,... | collective-permute-start | bytes 786440 | tf_op jit(solution)/shard_map/ppermute | solution.py:18
  124.7 0.0 copy-start.4
  124.7 1.5 %shard_map.72.refs_5_ = bf16[128,1024]{1,0:T(8,128)(2,1)S(1)} custom-call(bf16[272,1024]{1,0:T(8,128)(2,1)S(1)} %collective-permute-done.18.refs_0_, f32[128,1024]{1,0:T(8,128)S(1)} %get-tuple-element.30.refs_1_, bf16[1024,1024]{1,0:T(8,128)(2,1)S(1)} %shard_map.62.refs_11_.refs_2_.refs_4_.refs_1_, ...), custom_call_target="tpu_custom_call" | custom-call | flops 536870912 | bytes 1048576 | tf_op jit(solution)/shard_map/pallas_call | solution.py:43
  126.2 12.7 %collective-permute-done.22.refs_2_ = bf16[128,1024]{1,0:T(8,128)(2,1)S(1)} collective-permute-done((bf16[128,1024]{1,0:T(8,128)(2,1)S(1)}, bf16[128,1024]{1,0:T(8,128)(2,1)S(1)}, u32[]{:S(2)}, u32[]{:S(2)}) %collective-permute-start.22) | collective-permute-done | bytes 262176 | tf_op jit(solution)/shard_map/ppermute | solution.py:18
  138.9 1.7 %shard_map.73 = (bf16[2,128,1024]{2,1,0:T(8,128)(2,1)}, bf16[2,128]{1,0:T(2,128)(2,1)}, bf16[2,128,1024]{2,1,0:T(8,128)(2,1)}) custom-call(bf16[272,1024]{1,0:T(8,128)(2,1)S(1)} %collective-permute-done.18.refs_0_, bf16[144,1024]{1,0:T(8,128)(2,1)S(1)} %collective-permute-done.21.refs_1_, bf16[128,1024]{1,0:T(8,128)(2,1)S(1)} %collective-permute-done.22.refs_2_, ...), custom_call_target="tpu_custom_call" | custom-call | flops 268435456 | bytes 1048576 | tf_op jit(solution)/shard_map/pallas_call | solution.py:43
  (24 shorter events, 0.1 us)
Async XLA Ops:
  0.6 80.8 %copy-start = (bf16[2,128,1024]{2,1,0:T(8,128)(2,1)S(1)}, bf16[2,128,1024]{2,1,0:T(8,128)(2,1)}, u32[]{:S(2)}) copy-start(bf16[2,128,1024]{2,1,0:T(8,128)(2,1)} %refs_10_.1) | copy-start | bytes 1572868
  0.6 22.6 %collective-permute-start.3 = (bf16[2,128,1024]{2,1,0:T(8,128)(2,1)}, bf16[2,128,1024]{2,1,0:T(8,128)(2,1)S(1)}, u32[]{:S(2)}, u32[]{:S(2)}) collective-permute-start(bf16[2,128,1024]{2,1,0:T(8,128)(2,1)} %refs_10_.1), channel_id=1, source_target_pairs={{0,7},{1,0},{2,1},{3,2},{4,3},{5,4},{6,5},{7,6},{8,15},{9,8},{10,9... | collective-permute-start | bytes 1572872 | tf_op jit(solution)/shard_map/ppermute | solution.py:18
  11.7 17.0 %collective-permute-start = (bf16[2,128,1024]{2,1,0:T(8,128)(2,1)}, bf16[2,128,1024]{2,1,0:T(8,128)(2,1)S(1)}, u32[]{:S(2)}, u32[]{:S(2)}) collective-permute-start(bf16[2,128,1024]{2,1,0:T(8,128)(2,1)} %refs_10_.1), channel_id=1, source_target_pairs={{0,1},{1,2},{2,3},{3,4},{4,5},{5,6},{6,7},{7,0},{8,9},{9,10},{10,1... | collective-permute-start | bytes 1572872 | tf_op jit(solution)/shard_map/ppermute | solution.py:18
  23.2 16.7 %collective-permute-start.4 = (bf16[2,128,1024]{2,1,0:T(8,128)(2,1)S(1)}, bf16[2,128,1024]{2,1,0:T(8,128)(2,1)S(1)}, u32[]{:S(2)}, u32[]{:S(2)}) collective-permute-start(bf16[2,128,1024]{2,1,0:T(8,128)(2,1)S(1)} %collective-permute-done.3.refs_4_), channel_id=1, source_target_pairs={{0,7},{1,0},{2,1},{3,2},{4,3},{5,4},{6,5},{7,6},{8,15},{9,8},{10,9... | collective-permute-start | bytes 1572872 | tf_op jit(solution)/shard_map/ppermute | solution.py:18
  28.7 17.9 %collective-permute-start.1 = (bf16[2,128,1024]{2,1,0:T(8,128)(2,1)S(1)}, bf16[2,128,1024]{2,1,0:T(8,128)(2,1)S(1)}, u32[]{:S(2)}, u32[]{:S(2)}) collective-permute-start(bf16[2,128,1024]{2,1,0:T(8,128)(2,1)S(1)} %collective-permute-done.refs_1_), channel_id=1, source_target_pairs={{0,1},{1,2},{2,3},{3,4},{4,5},{5,6},{6,7},{7,0},{8,9},{9,10},{10,1... | collective-permute-start | bytes 1572872 | tf_op jit(solution)/shard_map/ppermute | solution.py:18
  30.6 1.0 copy-start.1
  31.7 0.7 copy-start.3
  32.5 20.5 %collective-permute-start.10 = (bf16[1168,128]{1,0:T(8,128)(2,1)S(1)}, bf16[1168,128]{1,0:T(8,128)(2,1)S(1)}, u32[]{:S(2)}, u32[]{:S(2)}) collective-permute-start(bf16[1168,128]{1,0:T(8,128)(2,1)S(1)} %shard_map.63.refs_0_), channel_id=1, source_target_pairs={{0,1},{1,2},{2,3},{3,4},{4,5},{5,6},{6,7},{7,0},{8,9},{9,10},{10,1... | collective-permute-start | bytes 897032 | tf_op jit(solution)/shard_map/ppermute | solution.py:18
  34.4 20.5 %collective-permute-start.13 = (bf16[1168,128]{1,0:T(8,128)(2,1)S(1)}, bf16[1168,128]{1,0:T(8,128)(2,1)S(1)}, u32[]{:S(2)}, u32[]{:S(2)}) collective-permute-start(bf16[1168,128]{1,0:T(8,128)(2,1)S(1)} %shard_map.63.refs_0_), channel_id=1, source_target_pairs={{0,7},{1,0},{2,1},{3,2},{4,3},{5,4},{6,5},{7,6},{8,15},{9,8},{10,9... | collective-permute-start | bytes 897032 | tf_op jit(solution)/shard_map/ppermute | solution.py:18
  39.9 30.4 %collective-permute-start.5 = (bf16[2,128,1024]{2,1,0:T(8,128)(2,1)S(1)}, bf16[2,128,1024]{2,1,0:T(8,128)(2,1)S(1)}, u32[]{:S(2)}, u32[]{:S(2)}) collective-permute-start(bf16[2,128,1024]{2,1,0:T(8,128)(2,1)S(1)} %collective-permute-done.4.refs_5_), channel_id=1, source_target_pairs={{0,7},{1,0},{2,1},{3,2},{4,3},{5,4},{6,5},{7,6},{8,15},{9,8},{10,9... | collective-permute-start | bytes 1572872 | tf_op jit(solution)/shard_map/ppermute | solution.py:18
  46.6 30.8 %collective-permute-start.2 = (bf16[2,128,1024]{2,1,0:T(8,128)(2,1)S(1)}, bf16[2,128,1024]{2,1,0:T(8,128)(2,1)S(1)}, u32[]{:S(2)}, u32[]{:S(2)}) collective-permute-start(bf16[2,128,1024]{2,1,0:T(8,128)(2,1)S(1)} %collective-permute-done.1.refs_2_), channel_id=1, source_target_pairs={{0,1},{1,2},{2,3},{3,4},{4,5},{5,6},{6,7},{7,0},{8,9},{9,10},{10,1... | collective-permute-start | bytes 1572872 | tf_op jit(solution)/shard_map/ppermute | solution.py:18
  53.0 15.4 %collective-permute-start.11 = (bf16[1168,128]{1,0:T(8,128)(2,1)S(1)}, bf16[1168,128]{1,0:T(8,128)(2,1)S(1)}, u32[]{:S(2)}, u32[]{:S(2)}) collective-permute-start(bf16[1168,128]{1,0:T(8,128)(2,1)S(1)} %collective-permute-done.10.refs_1_), channel_id=1, source_target_pairs={{0,1},{1,2},{2,3},{3,4},{4,5},{5,6},{6,7},{7,0},{8,9},{9,10},{10,1... | collective-permute-start | bytes 897032 | tf_op jit(solution)/shard_map/ppermute | solution.py:18
  54.9 20.5 %collective-permute-start.14 = (bf16[1168,128]{1,0:T(8,128)(2,1)S(1)}, bf16[1168,128]{1,0:T(8,128)(2,1)S(1)}, u32[]{:S(2)}, u32[]{:S(2)}) collective-permute-start(bf16[1168,128]{1,0:T(8,128)(2,1)S(1)} %collective-permute-done.13.refs_4_), channel_id=1, source_target_pairs={{0,7},{1,0},{2,1},{3,2},{4,3},{5,4},{6,5},{7,6},{8,15},{9,8},{10,9... | collective-permute-start | bytes 897032 | tf_op jit(solution)/shard_map/ppermute | solution.py:18
  68.4 17.5 %collective-permute-start.12 = (bf16[1168,128]{1,0:T(8,128)(2,1)S(1)}, bf16[1168,128]{1,0:T(8,128)(2,1)S(1)}, u32[]{:S(2)}, u32[]{:S(2)}) collective-permute-start(bf16[1168,128]{1,0:T(8,128)(2,1)S(1)} %collective-permute-done.11.refs_2_), channel_id=1, source_target_pairs={{0,1},{1,2},{2,3},{3,4},{4,5},{5,6},{6,7},{7,0},{8,9},{9,10},{10,1... | collective-permute-start | bytes 897032 | tf_op jit(solution)/shard_map/ppermute | solution.py:18
  70.3 13.0 %collective-permute-start.6 = (bf16[128,1024]{1,0:T(8,128)(2,1)S(1)}, bf16[128,1024]{1,0:T(8,128)(2,1)S(1)}, u32[]{:S(2)}, u32[]{:S(2)}) collective-permute-start(bf16[128,1024]{1,0:T(8,128)(2,1)S(1)} %shard_map.58.refs_2_), channel_id=1, source_target_pairs={{0,7},{1,0},{2,1},{3,2},{4,3},{5,4},{6,5},{7,6},{8,15},{9,8},{10,9... | collective-permute-start | bytes 786440 | tf_op jit(solution)/shard_map/ppermute | solution.py:18
  75.5 12.4 %collective-permute-start.15 = (bf16[1168,128]{1,0:T(8,128)(2,1)S(1)}, bf16[1168,128]{1,0:T(8,128)(2,1)S(1)}, u32[]{:S(2)}, u32[]{:S(2)}) collective-permute-start(bf16[1168,128]{1,0:T(8,128)(2,1)S(1)} %collective-permute-done.14.refs_5_), channel_id=1, source_target_pairs={{0,7},{1,0},{2,1},{3,2},{4,3},{5,4},{6,5},{7,6},{8,15},{9,8},{10,9... | collective-permute-start | bytes 897032 | tf_op jit(solution)/shard_map/ppermute | solution.py:18
  77.5 15.6 %collective-permute-start.9 = (bf16[128,1024]{1,0:T(8,128)(2,1)S(1)}, bf16[128,1024]{1,0:T(8,128)(2,1)S(1)}, u32[]{:S(2)}, u32[]{:S(2)}) collective-permute-start(bf16[128,1024]{1,0:T(8,128)(2,1)S(1)} %shard_map.61.refs_1_), channel_id=1, source_target_pairs={{0,1},{1,2},{2,3},{3,4},{4,5},{5,6},{6,7},{7,0},{8,9},{9,10},{10,1... | collective-permute-start | bytes 786440 | tf_op jit(solution)/shard_map/ppermute | solution.py:18
  81.4 11.8 %collective-permute-start.8 = (bf16[128,1024]{1,0:T(8,128)(2,1)S(1)}, bf16[128,1024]{1,0:T(8,128)(2,1)S(1)}, u32[]{:S(2)}, u32[]{:S(2)}) collective-permute-start(bf16[128,1024]{1,0:T(8,128)(2,1)S(1)} %shard_map.60), channel_id=1, source_target_pairs={{0,8},{8,16},{16,24},{24,32},{32,40},{40,48},{48,56},{56,64},{64,7... | collective-permute-start | bytes 786440 | tf_op jit(solution)/shard_map/ppermute | solution.py:18
  84.0 14.8 %collective-permute-start.7 = (bf16[128,1024]{1,0:T(8,128)(2,1)S(1)}, bf16[128,1024]{1,0:T(8,128)(2,1)S(1)}, u32[]{:S(2)}, u32[]{:S(2)}) collective-permute-start(bf16[128,1024]{1,0:T(8,128)(2,1)S(1)} %get-tuple-element.17.refs_8_), channel_id=1, source_target_pairs={{0,8},{8,16},{16,24},{24,32},{32,40},{40,48},{48,56},{56,64},{64,7... | collective-permute-start | bytes 786440 | tf_op jit(solution)/shard_map/ppermute | solution.py:18
  85.9 9.9 %collective-permute-start.16 = (bf16[592,128]{1,0:T(8,128)(2,1)S(1)}, bf16[592,128]{1,0:T(8,128)(2,1)S(1)}, u32[]{:S(2)}, u32[]{:S(2)}) collective-permute-start(bf16[592,128]{1,0:T(8,128)(2,1)S(1)} %shard_map.64), channel_id=1, source_target_pairs={{0,1},{1,2},{2,3},{3,4},{4,5},{5,6},{6,7},{7,0},{8,9},{9,10},{10,1... | collective-permute-start | bytes 454664 | tf_op jit(solution)/shard_map/ppermute | solution.py:18
  87.9 7.9 %collective-permute-start.17 = (bf16[576,128]{1,0:T(8,128)(2,1)S(1)}, bf16[576,128]{1,0:T(8,128)(2,1)S(1)}, u32[]{:S(2)}, u32[]{:S(2)}) collective-permute-start(bf16[576,128]{1,0:T(8,128)(2,1)S(1)} %shard_map.65), channel_id=1, source_target_pairs={{0,7},{1,0},{2,1},{3,2},{4,3},{5,4},{6,5},{7,6},{8,15},{9,8},{10,9... | collective-permute-start | bytes 442376 | tf_op jit(solution)/shard_map/ppermute | solution.py:18
  100.1 7.7 %collective-permute-start.19 = (bf16[128,1024]{1,0:T(8,128)(2,1)S(1)}, bf16[128,1024]{1,0:T(8,128)(2,1)S(1)}, u32[]{:S(2)}, u32[]{:S(2)}) collective-permute-start(bf16[128,1024]{1,0:T(8,128)(2,1)S(1)} %get-tuple-element.26), channel_id=1, source_target_pairs={{0,8},{8,16},{16,24},{24,32},{32,40},{40,48},{48,56},{56,64},{64,7... | collective-permute-start | bytes 786440 | tf_op jit(solution)/shard_map/ppermute | solution.py:18
  109.0 6.8 %collective-permute-start.20 = (bf16[144,1024]{1,0:T(8,128)(2,1)S(1)}, bf16[144,1024]{1,0:T(8,128)(2,1)S(1)}, u32[]{:S(2)}, u32[]{:S(2)}) collective-permute-start(bf16[144,1024]{1,0:T(8,128)(2,1)S(1)} %shard_map.69.refs_2_), channel_id=1, source_target_pairs={{0,504},{8,0},{16,8},{24,16},{32,24},{40,32},{48,40},{56,48},{64,5... | collective-permute-start | bytes 884744 | tf_op jit(solution)/shard_map/ppermute | solution.py:18
  110.9 13.8 %collective-permute-start.18 = (bf16[272,1024]{1,0:T(8,128)(2,1)S(1)}, bf16[272,1024]{1,0:T(8,128)(2,1)S(1)}, u32[]{:S(2)}, u32[]{:S(2)}) collective-permute-start(bf16[272,1024]{1,0:T(8,128)(2,1)S(1)} %get-tuple-element.25.refs_3_), channel_id=1, source_target_pairs={{0,504},{8,0},{16,8},{24,16},{32,24},{40,32},{48,40},{56,48},{64,5... | collective-permute-start | bytes 1671176 | tf_op jit(solution)/shard_map/ppermute | solution.py:18
  115.7 9.0 %copy-start.2 = (bf16[2,128,1024]{2,1,0:T(8,128)(2,1)S(1)}, bf16[2,128,1024]{2,1,0:T(8,128)(2,1)}, u32[]{:S(2)}) copy-start(bf16[2,128,1024]{2,1,0:T(8,128)(2,1)} %refs_6_.1) | copy-start | bytes 1572868
  117.3 21.7 %collective-permute-start.21 = (bf16[144,1024]{1,0:T(8,128)(2,1)S(1)}, bf16[144,1024]{1,0:T(8,128)(2,1)S(1)}, u32[]{:S(2)}, u32[]{:S(2)}) collective-permute-start(bf16[144,1024]{1,0:T(8,128)(2,1)S(1)} %shard_map.71.refs_5_), channel_id=1, source_target_pairs={{0,504},{8,0},{16,8},{24,16},{32,24},{40,32},{48,40},{56,48},{64,5... | collective-permute-start | bytes 884744 | tf_op jit(solution)/shard_map/ppermute | solution.py:18
  120.4 18.5 %collective-permute-start.22 = (bf16[128,1024]{1,0:T(8,128)(2,1)S(1)}, bf16[128,1024]{1,0:T(8,128)(2,1)S(1)}, u32[]{:S(2)}, u32[]{:S(2)}) collective-permute-start(bf16[128,1024]{1,0:T(8,128)(2,1)S(1)} %shard_map.70.refs_6_), channel_id=1, source_target_pairs={{0,496},{8,504},{16,0},{24,8},{32,16},{40,24},{48,32},{56,40},{64,... | collective-permute-start | bytes 786440 | tf_op jit(solution)/shard_map/ppermute | solution.py:18
  124.7 14.2 %copy-start.4 = (bf16[2,128]{1,0:T(2,128)(2,1)S(1)}, bf16[2,128]{1,0:T(2,128)(2,1)}, u32[]{:S(2)}) copy-start(bf16[2,128]{1,0:T(2,128)(2,1)} %refs_7_.1) | copy-start | bytes 1540

commit v3 on v2

--- a/solution.py
+++ b/solution.py
@@ -158,22 +158,25 @@
     n = len(l_arrays)
 
     def first(*refs):
-        last, out, joined = refs[n], refs[n + 1], refs[n + 2]
-        join([(way, ref[1]) for way, ref in zip(offsets, refs)] + [(half, last[...])], joined, count)
-        out[...] = nn(refs[0][0], joined[...]).astype(BF16)
-
-    x1, e_odd = call(first, e_arrays + [e_odd_last], [panel, whole], product)
-    x1_in = hop(x1, "tm", 1)
-
-    def evens(*refs):
-        last, joined = refs[n], refs[n + 1]
-        join([(way, ref[0]) for way, ref in zip(offsets, refs)] + [(half, last[...])], joined, count)
-
-    (e_even,) = call(evens, e_arrays + [e_even_last], [whole], 1000, after=(x1,))
+        even_last, odd_last, b1_ref, out, b2_ref, even, odd = refs[n:]
+        past = lax.axis_index("tm") < 1
+        join([(way, ref[0]) for way, ref in zip(offsets, refs)] + [(half, even_last[...])], even, count)
+        b1 = b1_ref[...]
+        b2 = nn(b1, even[...]).astype(BF16)
+        b2_ref[...] = b2
+        join([(way, ref[1]) for way, ref in zip(offsets, refs)] + [(half, odd_last[...])], odd, count)
+        both = nn(jnp.concatenate([refs[0][0], b2], axis=0), odd[...])
+        out[:rows, :] = both[:rows].astype(BF16)
+        out[rows:, :] = jnp.where(past, b1.astype(F32), both[rows:]).astype(BF16)
+
+    m, b2, e_even, e_odd = call(
+        first, e_arrays + [e_even_last, e_odd_last, b1_in], [pair, panel, whole, whole], 3 * product
+    )
+    m_in = hop(m, "tm", 1)
 
     def opened(*refs):
-        even_last, odd_last, b1_ref, own = refs[n : n + 4]
-        close_ref, head_ref, line_ref, l_ev, l_od, g_ref = refs[n + 4 :]
+        even_last, odd_last, b1_ref, b2_ref, own = refs[n : n + 5]
+        close_ref, far_ref, head_ref, line_ref, l_ev, l_od, g_ref = refs[n + 5 :]
         unpack([(way, (ref, 0)) for way, ref in zip(offsets, refs)] + [(half, (even_last, 0))], l_ev, count)
         unpack([(way, (ref, packed + TAIL)) for way, ref in zip(offsets, refs)] + [(half, (odd_last, 0))], l_od, count)
         for way, ref in list(zip(offsets, refs)) + [(half, even_last)]:
@@ -181,66 +184,53 @@
             g_ref[:, pl.ds(column, rows)] = ref[packed : packed + TAIL, :]
         g = g_ref[...]
         close_ref[...] = by_symmetric(b1_ref[...], l_ev[...])
-        head_ref[...] = by_symmetric(own[0], l_od[...])
+        far = by_symmetric(jnp.concatenate([own[0], b2_ref[...]], axis=0), l_od[...])
+        head_ref[...] = far[:rows]
+        far_ref[...] = far[rows:]
         index = lax.broadcasted_iota(jnp.int32, (8, rows), 0)
-        line_ref[...] = jnp.where(index == 0, nt(g, b1_ref[...])[0:1], nt(g, own[0])[1:2])
-
-    close, head, line1, l_even, l_odd, g_all = call(
+        row = nt(g, b1_ref[...])[0:1] + nt(g, b2_ref[...])[1:2]
+        line_ref[...] = jnp.where(index == 0, row, nt(g, own[0])[1:2])
+
+    close, far, head, line_, l_even, l_odd, g_all = call(
         opened,
-        l_arrays + [l_even_last, l_odd_last, b1_in, trans],
-        [wide, wide, line, whole, whole, kept((TAIL, size), BF16)],
-        4 * product,
-        after=(e_even,),
-    )
-
-    def second(x1_ref, b1_ref, even, odd, x3_ref, b3_ref, x2_ref):
+        l_arrays + [l_even_last, l_odd_last, b1_in, b2, trans],
+        [wide, wide, wide, line, whole, whole, kept((TAIL, size), BF16)],
+        6 * product,
+        after=(m,),
+    )
+
+    def fourth(m_ref, l_ev, g_ref, out):
+        past = lax.axis_index("tm") < 2
+        own = m_ref[rows:, :]
+        out[:rows, :] = jnp.where(past, 0.0, by_symmetric(own, l_ev[...])).astype(BF16)
+        out[rows:, :] = jnp.zeros((TAIL, size), BF16)
+        out[rows:, :rows] = two_rows(jnp.where(past, 0.0, nt(g_ref[...], own)[0:1]))
+
+    (v,) = call(fourth, [m_in, l_even, g_all], [short], 2 * product)
+    v_in = hop(v, "tm", -1)
+
+    def third(m_ref, even, odd, l_ev, l_od, g_ref, out):
         past = lax.axis_index("tm") < 1
-        one = jnp.concatenate([x1_ref[...], b1_ref[...]], axis=0)
+        one = m_ref[:rows, :]
         two = nn(one, even[...]).astype(BF16)
-        three = nn(two, odd[...])
-        three = jnp.where(past, one.astype(F32), three).astype(BF16)
-        x3_ref[...] = three[:rows]
-        b3_ref[...] = three[rows:]
-        x2_ref[...] = two
-
-    x3, b3, x2 = call(second, [x1_in, b1_in, e_even, e_odd], [panel, panel, pair], 4 * product, after=(g_all,))
-    b3_in = hop(b3, "tm", 1)
-
-    def third(x1_ref, x2_ref, x3_ref, line_ref, even, l_ev, l_od, g_ref, m_ref, far_ref, row_ref):
-        past = lax.axis_index("tm") < 1
-        two = x2_ref[...]
+        three = jnp.where(past, one.astype(F32), nn(two, odd[...]))
         far = by_symmetric(two, l_od[...])
-        w = by_symmetric(x1_ref[...], l_ev[...]) + nt(far[:rows].astype(BF16), even[...])
-        far_ref[...] = far[rows:]
-        row = nt(g_ref[...], two)[1:2]
-        row_ref[...] = jnp.broadcast_to(line_ref[0:1] + row[:, rows:], row_ref.shape)
-        row = nt(g_ref[...], x1_ref[...])[0:1] + row[:, :rows]
-        m_ref[:rows, :] = jnp.where(past, 0.0, w).astype(BF16)
-        m_ref[rows : 2 * rows, :] = x3_ref[...]
-        m_ref[2 * rows :, :] = jnp.zeros((TAIL, size), BF16)
-        m_ref[2 * rows :, :rows] = two_rows(jnp.where(past, 0.0, row))
-
-    w, far, line2 = call(
-        third, [x1_in, x2, x3, line1, e_even, l_even, l_odd, g_all], [long, wide, line], 7 * product
-    )
+        w = by_symmetric(one, l_ev[...]) + nt(far.astype(BF16), even[...])
+        row = nt(g_ref[...], one)[0:1] + nt(g_ref[...], two)[1:2]
+        out[:rows, :] = jnp.where(past, 0.0, w).astype(BF16)
+        out[rows : 2 * rows, :] = three.astype(BF16)
+        out[2 * rows :, :] = jnp.zeros((TAIL, size), BF16)
+        out[2 * rows :, :rows] = two_rows(jnp.where(past, 0.0, row))
+
+    (w,) = call(third, [m_in, e_even, e_odd, l_even, l_odd, g_all], [long], 7 * product, after=(v,))
     w_in = hop(w, "tm", -1)
 
-    def fourth(b3_ref, l_ev, g_ref, m_ref):
-        past = lax.axis_index("tm") < 2
-        own = b3_ref[...]
-        m_ref[:rows, :] = jnp.where(past, 0.0, by_symmetric(own, l_ev[...])).astype(BF16)
-        m_ref[rows:, :] = jnp.zeros((TAIL, size), BF16)
-        m_ref[rows:, :rows] = two_rows(jnp.where(past, 0.0, nt(g_ref[...], own)[0:1]))
-
-    (v,) = call(fourth, [b3_in, l_even, g_all], [short], 2 * product, after=(w,))
-    v_in = hop(v, "tm", -1)
-
-    def fifth(b3_ref, even, b4_ref):
-        own = b3_ref[...]
+    def fifth(m_ref, even, b4_ref):
+        own = m_ref[rows:, :]
         past = lax.axis_index("tm") < 2
         b4_ref[...] = jnp.where(past, own.astype(F32), nn(own, even[...])).astype(BF16)
 
-    (b4,) = call(fifth, [b3_in, e_even], [panel], product, after=(v,))
+    (b4,) = call(fifth, [m_in, e_even], [panel], product, after=(w,))
     b4_in = hop(b4, "tm", -2)
 
     def sixth(v_ref, close_ref, far_ref, line_ref, even, odd, m_ref):
@@ -252,7 +242,7 @@
         m_ref[rows:, :] = jnp.zeros((TAIL, size), BF16)
         m_ref[rows:, :rows] = two_rows(jnp.where(past, 0.0, row))
 
-    (u,) = call(sixth, [v_in, close, far, line2, e_even, e_odd], [short], 2 * product, after=(b4,))
+    (u,) = call(sixth, [v_in, close, far, line_, e_even, e_odd], [short], 2 * product, after=(b4,))
     u_in = hop(u, "tm", -1)
 
     def seventh(w_ref, head_ref, even, odd, l_own, out):
@@ -272,7 +262,7 @@
 
     return call(
         eighth,
-        [w_in, u_in, b4_in, line1, e_odd, l_first, spread, offset],
+        [w_in, u_in, b4_in, line_, e_odd, l_first, spread, offset],
         [jax.ShapeDtypeStruct(x.shape, BF16) for x in (trans, offset, spread)],
         product,
     )

time: 141 us -> 136 us (0.965)
  the two profiles are of different devices: /device:TPU:62 before, /device:TPU:30 now
where the time goes in v3:
time: 136 us; the launch traced here: 135 us
  starting transfers between devices  76.4 us (56%)
  waiting for transfers between devices  40.5 us (30%)
  Pallas kernels  14.6 us (11%)
  local copies, waits for them, and re-layouts  2.74 us (2%)
    ppermute x22, starting transfers between devices, hop(): lax.ppermute(block, axis, [(i, (i + distance) % size) for i in range(size)])  76.4 us
    ppermute x22, waiting for transfers between devices, hop(): lax.ppermute(block, axis, [(i, (i + distance) % size) for i in range(size)])  40.5 us
    pallas_call x14, Pallas kernels, call(): pl.pallas_call(run, in_specs=[VMEM] * count + [HBM] * len(after), out_spe...  14.6 us
    unnamed x12, local copies, waits for them, and re-layouts  2.74 us
  transfers between devices with their start and end apart: 22, of which 6 were waited for; matrix products, arithmetic and copies ran while one was open for 0% of the time, Pallas kernels for 9%

profile of v3, /device:TPU:30, one launch (start us, length us, event | category | flops | bytes accessed | tf_op | source)
XLA Modules:
  0.0 135.2 jit_solution(15843146255844851027)
XLA Ops:
  0.6 4.3 %collective-permute-start = (bf16[2,128,1024]{2,1,0:T(8,128)(2,1)}, bf16[2,128,1024]{2,1,0:T(8,128)(2,1)S(1)}, u32[]{:S(2)}, u32[]{:S(2)}) collective-permute-start(bf16[2,128,1024]{2,1,0:T(8,128)(2,1)} %refs_11_.1), channel_id=1, source_target_pairs={{0,1},{1,2},{2,3},{3,4},{4,5},{5,6},{6,7},{7,0},{8,9},{9,10},{10,1... | collective-permute-start | bytes 1572872 | tf_op jit(solution)/shard_map/ppermute | solution.py:18
  4.9 8.6 %collective-permute-start.3 = (bf16[2,128,1024]{2,1,0:T(8,128)(2,1)}, bf16[2,128,1024]{2,1,0:T(8,128)(2,1)S(1)}, u32[]{:S(2)}, u32[]{:S(2)}) collective-permute-start(bf16[2,128,1024]{2,1,0:T(8,128)(2,1)} %refs_11_.1), channel_id=1, source_target_pairs={{0,7},{1,0},{2,1},{3,2},{4,3},{5,4},{6,5},{7,6},{8,15},{9,8},{10,9... | collective-permute-start | bytes 1572872 | tf_op jit(solution)/shard_map/ppermute | solution.py:18
  13.5 10.2 %collective-permute-done.refs_1_ = bf16[2,128,1024]{2,1,0:T(8,128)(2,1)S(1)} collective-permute-done((bf16[2,128,1024]{2,1,0:T(8,128)(2,1)}, bf16[2,128,1024]{2,1,0:T(8,128)(2,1)S(1)}, u32[]{:S(2)}, u32[]{:S(2)}) %collective-permute-start) | collective-permute-done | bytes 524320 | tf_op jit(solution)/shard_map/ppermute | solution.py:18
  23.7 1.9 %collective-permute-start.1 = (bf16[2,128,1024]{2,1,0:T(8,128)(2,1)S(1)}, bf16[2,128,1024]{2,1,0:T(8,128)(2,1)S(1)}, u32[]{:S(2)}, u32[]{:S(2)}) collective-permute-start(bf16[2,128,1024]{2,1,0:T(8,128)(2,1)S(1)} %collective-permute-done.refs_1_), channel_id=1, source_target_pairs={{0,1},{1,2},{2,3},{3,4},{4,5},{5,6},{6,7},{7,0},{8,9},{9,10},{10,1... | collective-permute-start | bytes 1572872 | tf_op jit(solution)/shard_map/ppermute | solution.py:18
  25.6 0.0 collective-permute-done.3.refs_4_
  25.6 5.1 %collective-permute-start.4 = (bf16[2,128,1024]{2,1,0:T(8,128)(2,1)S(1)}, bf16[2,128,1024]{2,1,0:T(8,128)(2,1)S(1)}, u32[]{:S(2)}, u32[]{:S(2)}) collective-permute-start(bf16[2,128,1024]{2,1,0:T(8,128)(2,1)S(1)} %collective-permute-done.3.refs_4_), channel_id=1, source_target_pairs={{0,7},{1,0},{2,1},{3,2},{4,3},{5,4},{6,5},{7,6},{8,15},{9,8},{10,9... | collective-permute-start | bytes 1572872 | tf_op jit(solution)/shard_map/ppermute | solution.py:18
  30.8 9.1 %collective-permute-done.1.refs_2_ = bf16[2,128,1024]{2,1,0:T(8,128)(2,1)S(1)} collective-permute-done((bf16[2,128,1024]{2,1,0:T(8,128)(2,1)S(1)}, bf16[2,128,1024]{2,1,0:T(8,128)(2,1)S(1)}, u32[]{:S(2)}, u32[]{:S(2)}) %collective-permute-start.1) | collective-permute-done | bytes 524320 | tf_op jit(solution)/shard_map/ppermute | solution.py:18
  39.9 1.9 %collective-permute-start.2 = (bf16[2,128,1024]{2,1,0:T(8,128)(2,1)S(1)}, bf16[2,128,1024]{2,1,0:T(8,128)(2,1)S(1)}, u32[]{:S(2)}, u32[]{:S(2)}) collective-permute-start(bf16[2,128,1024]{2,1,0:T(8,128)(2,1)S(1)} %collective-permute-done.1.refs_2_), channel_id=1, source_target_pairs={{0,1},{1,2},{2,3},{3,4},{4,5},{5,6},{6,7},{7,0},{8,9},{9,10},{10,1... | collective-permute-start | bytes 1572872 | tf_op jit(solution)/shard_map/ppermute | solution.py:18
  41.8 0.0 collective-permute-done.4.refs_5_
  41.8 5.1 %collective-permute-start.5 = (bf16[2,128,1024]{2,1,0:T(8,128)(2,1)S(1)}, bf16[2,128,1024]{2,1,0:T(8,128)(2,1)S(1)}, u32[]{:S(2)}, u32[]{:S(2)}) collective-permute-start(bf16[2,128,1024]{2,1,0:T(8,128)(2,1)S(1)} %collective-permute-done.4.refs_5_), channel_id=1, source_target_pairs={{0,7},{1,0},{2,1},{3,2},{4,3},{5,4},{6,5},{7,6},{8,15},{9,8},{10,9... | collective-permute-start | bytes 1572872 | tf_op jit(solution)/shard_map/ppermute | solution.py:18
  47.0 0.0 copy-start
  47.0 1.0 copy-done
  48.0 0.7 copy-done.4
  48.7 0.2 shard_map.62.refs_0_
  48.8 1.9 %collective-permute-start.10 = (bf16[1168,128]{1,0:T(8,128)(2,1)S(1)}, bf16[1168,128]{1,0:T(8,128)(2,1)S(1)}, u32[]{:S(2)}, u32[]{:S(2)}) collective-permute-start(bf16[1168,128]{1,0:T(8,128)(2,1)S(1)} %shard_map.62.refs_0_), channel_id=1, source_target_pairs={{0,1},{1,2},{2,3},{3,4},{4,5},{5,6},{6,7},{7,0},{8,9},{9,10},{10,1... | collective-permute-start | bytes 897032 | tf_op jit(solution)/shard_map/ppermute | solution.py:18
  50.8 5.1 %collective-permute-start.13 = (bf16[1168,128]{1,0:T(8,128)(2,1)S(1)}, bf16[1168,128]{1,0:T(8,128)(2,1)S(1)}, u32[]{:S(2)}, u32[]{:S(2)}) collective-permute-start(bf16[1168,128]{1,0:T(8,128)(2,1)S(1)} %shard_map.62.refs_0_), channel_id=1, source_target_pairs={{0,7},{1,0},{2,1},{3,2},{4,3},{5,4},{6,5},{7,6},{8,15},{9,8},{10,9... | collective-permute-start | bytes 897032 | tf_op jit(solution)/shard_map/ppermute | solution.py:18
  55.9 5.7 %collective-permute-done.10.refs_1_ = bf16[1168,128]{1,0:T(8,128)(2,1)S(1)} collective-permute-done((bf16[1168,128]{1,0:T(8,128)(2,1)S(1)}, bf16[1168,128]{1,0:T(8,128)(2,1)S(1)}, u32[]{:S(2)}, u32[]{:S(2)}) %collective-permute-start.10) | collective-permute-done | bytes 299040 | tf_op jit(solution)/shard_map/ppermute | solution.py:18
  61.6 1.9 %collective-permute-start.11 = (bf16[1168,128]{1,0:T(8,128)(2,1)S(1)}, bf16[1168,128]{1,0:T(8,128)(2,1)S(1)}, u32[]{:S(2)}, u32[]{:S(2)}) collective-permute-start(bf16[1168,128]{1,0:T(8,128)(2,1)S(1)} %collective-permute-done.10.refs_1_), channel_id=1, source_target_pairs={{0,1},{1,2},{2,3},{3,4},{4,5},{5,6},{6,7},{7,0},{8,9},{9,10},{10,1... | collective-permute-start | bytes 897032 | tf_op jit(solution)/shard_map/ppermute | solution.py:18
  63.5 0.0 collective-permute-done.13.refs_4_
  63.5 5.1 %collective-permute-start.14 = (bf16[1168,128]{1,0:T(8,128)(2,1)S(1)}, bf16[1168,128]{1,0:T(8,128)(2,1)S(1)}, u32[]{:S(2)}, u32[]{:S(2)}) collective-permute-start(bf16[1168,128]{1,0:T(8,128)(2,1)S(1)} %collective-permute-done.13.refs_4_), channel_id=1, source_target_pairs={{0,7},{1,0},{2,1},{3,2},{4,3},{5,4},{6,5},{7,6},{8,15},{9,8},{10,9... | collective-permute-start | bytes 897032 | tf_op jit(solution)/shard_map/ppermute | solution.py:18
  68.7 0.0 copy-start.2
  68.7 1.0 copy-done.2
  69.8 1.9 %collective-permute-start.8 = (bf16[128,1024]{1,0:T(8,128)(2,1)S(1)}, bf16[128,1024]{1,0:T(8,128)(2,1)S(1)}, u32[]{:S(2)}, u32[]{:S(2)}) collective-permute-start(bf16[128,1024]{1,0:T(8,128)(2,1)S(1)} %shard_map.60), channel_id=1, source_target_pairs={{0,8},{8,16},{16,24},{24,32},{32,40},{40,48},{48,56},{56,64},{64,7... | collective-permute-start | bytes 786440 | tf_op jit(solution)/shard_map/ppermute | solution.py:18
  71.7 1.9 %collective-permute-start.6 = (bf16[128,1024]{1,0:T(8,128)(2,1)S(1)}, bf16[128,1024]{1,0:T(8,128)(2,1)S(1)}, u32[]{:S(2)}, u32[]{:S(2)}) collective-permute-start(bf16[128,1024]{1,0:T(8,128)(2,1)S(1)} %shard_map.58.refs_1_), channel_id=1, source_target_pairs={{0,1},{1,2},{2,3},{3,4},{4,5},{5,6},{6,7},{7,0},{8,9},{9,10},{10,1... | collective-permute-start | bytes 786440 | tf_op jit(solution)/shard_map/ppermute | solution.py:18
  73.6 0.0 collective-permute-done.5.refs_0_.refs_6_
  73.7 5.1 %collective-permute-start.7 = (bf16[128,1024]{1,0:T(8,128)(2,1)S(1)}, bf16[128,1024]{1,0:T(8,128)(2,1)S(1)}, u32[]{:S(2)}, u32[]{:S(2)}) collective-permute-start(bf16[128,1024]{1,0:T(8,128)(2,1)S(1)} %shard_map.59.refs_2_), channel_id=1, source_target_pairs={{0,7},{1,0},{2,1},{3,2},{4,3},{5,4},{6,5},{7,6},{8,15},{9,8},{10,9... | collective-permute-start | bytes 786440 | tf_op jit(solution)/shard_map/ppermute | solution.py:18
  78.8 1.9 %collective-permute-start.12 = (bf16[1168,128]{1,0:T(8,128)(2,1)S(1)}, bf16[1168,128]{1,0:T(8,128)(2,1)S(1)}, u32[]{:S(2)}, u32[]{:S(2)}) collective-permute-start(bf16[1168,128]{1,0:T(8,128)(2,1)S(1)} %collective-permute-done.11.refs_2_), channel_id=1, source_target_pairs={{0,1},{1,2},{2,3},{3,4},{4,5},{5,6},{6,7},{7,0},{8,9},{9,10},{10,1... | collective-permute-start | bytes 897032 | tf_op jit(solution)/shard_map/ppermute | solution.py:18
  80.8 0.0 collective-permute-done.14.refs_5_
  80.8 5.1 %collective-permute-start.15 = (bf16[1168,128]{1,0:T(8,128)(2,1)S(1)}, bf16[1168,128]{1,0:T(8,128)(2,1)S(1)}, u32[]{:S(2)}, u32[]{:S(2)}) collective-permute-start(bf16[1168,128]{1,0:T(8,128)(2,1)S(1)} %collective-permute-done.14.refs_5_), channel_id=1, source_target_pairs={{0,7},{1,0},{2,1},{3,2},{4,3},{5,4},{6,5},{7,6},{8,15},{9,8},{10,9... | collective-permute-start | bytes 897032 | tf_op jit(solution)/shard_map/ppermute | solution.py:18
  86.0 1.3 shard_map.61
  87.3 3.7 %collective-permute-start.9 = (bf16[256,1024]{1,0:T(8,128)(2,1)S(1)}, bf16[256,1024]{1,0:T(8,128)(2,1)S(1)}, u32[]{:S(2)}, u32[]{:S(2)}) collective-permute-start(bf16[256,1024]{1,0:T(8,128)(2,1)S(1)} %get-tuple-element.14.refs_12_), channel_id=1, source_target_pairs={{0,8},{8,16},{16,24},{24,32},{32,40},{40,48},{48,56},{56,64},{64,7... | collective-permute-start | bytes 1572872 | tf_op jit(solution)/shard_map/ppermute | solution.py:18
  91.0 1.9 %collective-permute-start.16 = (bf16[592,128]{1,0:T(8,128)(2,1)S(1)}, bf16[592,128]{1,0:T(8,128)(2,1)S(1)}, u32[]{:S(2)}, u32[]{:S(2)}) collective-permute-start(bf16[592,128]{1,0:T(8,128)(2,1)S(1)} %shard_map.63), channel_id=1, source_target_pairs={{0,1},{1,2},{2,3},{3,4},{4,5},{5,6},{6,7},{7,0},{8,9},{9,10},{10,1... | collective-permute-start | bytes 454664 | tf_op jit(solution)/shard_map/ppermute | solution.py:18
  92.9 5.1 %collective-permute-start.17 = (bf16[576,128]{1,0:T(8,128)(2,1)S(1)}, bf16[576,128]{1,0:T(8,128)(2,1)S(1)}, u32[]{:S(2)}, u32[]{:S(2)}) collective-permute-start(bf16[576,128]{1,0:T(8,128)(2,1)S(1)} %shard_map.64), channel_id=1, source_target_pairs={{0,7},{1,0},{2,1},{3,2},{4,3},{5,4},{6,5},{7,6},{8,15},{9,8},{10,9... | collective-permute-start | bytes 442376 | tf_op jit(solution)/shard_map/ppermute | solution.py:18
  98.1 4.1 %collective-permute-done.17.refs_8_ = bf16[576,128]{1,0:T(8,128)(2,1)S(1)} collective-permute-done((bf16[576,128]{1,0:T(8,128)(2,1)S(1)}, bf16[576,128]{1,0:T(8,128)(2,1)S(1)}, u32[]{:S(2)}, u32[]{:S(2)}) %collective-permute-start.17) | collective-permute-done | bytes 147488 | tf_op jit(solution)/shard_map/ppermute | solution.py:18
  102.2 3.3 %shard_map.65 = (f32[128,1024]{1,0:T(8,128)S(1)}, f32[128,1024]{1,0:T(8,128)S(1)}, f32[128,1024]{1,0:T(8,128)S(1)}, f32[8,128]{1,0:T(8,128)S(1)}, bf16[1024,1024...) custom-call(bf16[1168,128]{1,0:T(8,128)(2,1)S(1)} %shard_map.62.refs_0_, ...), custom_call_target="tpu_custom_call" | custom-call | flops 1610612736 | bytes 1048576 | tf_op jit(solution)/shard_map/pallas_call | solution.py:43
  105.4 1.2 shard_map.66.refs_6_
  106.6 1.9 %collective-permute-start.19 = (bf16[144,1024]{1,0:T(8,128)(2,1)S(1)}, bf16[144,1024]{1,0:T(8,128)(2,1)S(1)}, u32[]{:S(2)}, u32[]{:S(2)}) collective-permute-start(bf16[144,1024]{1,0:T(8,128)(2,1)S(1)} %shard_map.66.refs_6_), channel_id=1, source_target_pairs={{0,504},{8,0},{16,8},{24,16},{32,24},{40,32},{48,40},{56,48},{64,5... | collective-permute-start | bytes 884744 | tf_op jit(solution)/shard_map/ppermute | solution.py:18
  108.5 3.4 %shard_map.67.refs_2_ = bf16[272,1024]{1,0:T(8,128)(2,1)S(1)} custom-call(bf16[256,1024]{1,0:T(8,128)(2,1)S(1)} %collective-permute-done.9.refs_0_, bf16[1024,1024]{1,0:T(8,128)(2,1)S(1)} %get-tuple-element.15.refs_1_.refs_4_.refs_2_, bf16[1024,1024]{1,0:T(8,128)(2,1)S(1)} %get-tuple-element.16.refs_2_.refs_5_.refs_3_.refs_4_, ...), custom_call_target="tpu_custom_call" | custom-call | flops 1879048192 | bytes 1048576 | tf_op jit(solution)/shard_map/pallas_call | solution.py:43
  112.0 2.4 %collective-permute-start.18 = (bf16[272,1024]{1,0:T(8,128)(2,1)S(1)}, bf16[272,1024]{1,0:T(8,128)(2,1)S(1)}, u32[]{:S(2)}, u32[]{:S(2)}) collective-permute-start(bf16[272,1024]{1,0:T(8,128)(2,1)S(1)} %shard_map.67.refs_2_), channel_id=1, source_target_pairs={{0,504},{8,0},{16,8},{24,16},{32,24},{40,32},{48,40},{56,48},{64,5... | collective-permute-start | bytes 1671176 | tf_op jit(solution)/shard_map/ppermute | solution.py:18
  114.4 0.5 shard_map.68.refs_6_
  114.8 0.0 copy-start.1
  114.9 1.5 %shard_map.69.refs_5_ = bf16[144,1024]{1,0:T(8,128)(2,1)S(1)} custom-call(bf16[144,1024]{1,0:T(8,128)(2,1)S(1)} %collective-permute-done.19.refs_0_, f32[128,1024]{1,0:T(8,128)S(1)} %get-tuple-element.21.refs_1_, f32[128,1024]{1,0:T(8,128)S(1)} %get-tuple-element.22.refs_2_, f32[8,128]{1,0:T(8,128)S(1)} %get-tuple-element.23.refs_3_, ...), custom_call_target="tpu_custom_call" | custom-call | flops 536870912 | bytes 1048576 | tf_op jit(solution)/shard_map/pallas_call | solution.py:43
  116.4 1.9 %collective-permute-start.20 = (bf16[144,1024]{1,0:T(8,128)(2,1)S(1)}, bf16[144,1024]{1,0:T(8,128)(2,1)S(1)}, u32[]{:S(2)}, u32[]{:S(2)}) collective-permute-start(bf16[144,1024]{1,0:T(8,128)(2,1)S(1)} %shard_map.69.refs_5_), channel_id=1, source_target_pairs={{0,504},{8,0},{16,8},{24,16},{32,24},{40,32},{48,40},{56,48},{64,5... | collective-permute-start | bytes 884744 | tf_op jit(solution)/shard_map/ppermute | solution.py:18
  118.3 2.4 %collective-permute-start.21 = (bf16[128,1024]{1,0:T(8,128)(2,1)S(1)}, bf16[128,1024]{1,0:T(8,128)(2,1)S(1)}, u32[]{:S(2)}, u32[]{:S(2)}) collective-permute-start(bf16[128,1024]{1,0:T(8,128)(2,1)S(1)} %shard_map.68.refs_6_), channel_id=1, source_target_pairs={{0,496},{8,504},{16,0},{24,8},{32,16},{40,24},{48,32},{56,40},{64,... | collective-permute-start | bytes 786440 | tf_op jit(solution)/shard_map/ppermute | solution.py:18
  120.7 0.7 collective-permute-done.18.refs_0_
  121.4 1.5 %shard_map.70.refs_5_ = bf16[128,1024]{1,0:T(8,128)(2,1)S(1)} custom-call(bf16[272,1024]{1,0:T(8,128)(2,1)S(1)} %collective-permute-done.18.refs_0_, f32[128,1024]{1,0:T(8,128)S(1)} %get-tuple-element.24.refs_1_, bf16[1024,1024]{1,0:T(8,128)(2,1)S(1)} %get-tuple-element.15.refs_1_.refs_4_.refs_2_, ...), custom_call_target="tpu_custom_call" | custom-call | flops 536870912 | bytes 1048576 | tf_op jit(solution)/shard_map/pallas_call | solution.py:43
  122.9 10.6 %collective-permute-done.21.refs_2_ = bf16[128,1024]{1,0:T(8,128)(2,1)S(1)} collective-permute-done((bf16[128,1024]{1,0:T(8,128)(2,1)S(1)}, bf16[128,1024]{1,0:T(8,128)(2,1)S(1)}, u32[]{:S(2)}, u32[]{:S(2)}) %collective-permute-start.21) | collective-permute-done | bytes 262176 | tf_op jit(solution)/shard_map/ppermute | solution.py:18
  133.5 1.7 %shard_map.71 = (bf16[2,128,1024]{2,1,0:T(8,128)(2,1)}, bf16[2,128]{1,0:T(2,128)(2,1)}, bf16[2,128,1024]{2,1,0:T(8,128)(2,1)}) custom-call(bf16[272,1024]{1,0:T(8,128)(2,1)S(1)} %collective-permute-done.18.refs_0_, bf16[144,1024]{1,0:T(8,128)(2,1)S(1)} %collective-permute-done.20.refs_1_, bf16[128,1024]{1,0:T(8,128)(2,1)S(1)} %collective-permute-done.21.refs_2_, ...), custom_call_target="tpu_custom_call" | custom-call | flops 268435456 | bytes 1048576 | tf_op jit(solution)/shard_map/pallas_call | solution.py:43
  (22 shorter events, 0.1 us)
Async XLA Ops:
  0.6 23.1 %collective-permute-start = (bf16[2,128,1024]{2,1,0:T(8,128)(2,1)}, bf16[2,128,1024]{2,1,0:T(8,128)(2,1)S(1)}, u32[]{:S(2)}, u32[]{:S(2)}) collective-permute-start(bf16[2,128,1024]{2,1,0:T(8,128)(2,1)} %refs_11_.1), channel_id=1, source_target_pairs={{0,1},{1,2},{2,3},{3,4},{4,5},{5,6},{6,7},{7,0},{8,9},{9,10},{10,1... | collective-permute-start | bytes 1572872 | tf_op jit(solution)/shard_map/ppermute | solution.py:18
  4.9 20.7 %collective-permute-start.3 = (bf16[2,128,1024]{2,1,0:T(8,128)(2,1)}, bf16[2,128,1024]{2,1,0:T(8,128)(2,1)S(1)}, u32[]{:S(2)}, u32[]{:S(2)}) collective-permute-start(bf16[2,128,1024]{2,1,0:T(8,128)(2,1)} %refs_11_.1), channel_id=1, source_target_pairs={{0,7},{1,0},{2,1},{3,2},{4,3},{5,4},{6,5},{7,6},{8,15},{9,8},{10,9... | collective-permute-start | bytes 1572872 | tf_op jit(solution)/shard_map/ppermute | solution.py:18
  23.7 16.2 %collective-permute-start.1 = (bf16[2,128,1024]{2,1,0:T(8,128)(2,1)S(1)}, bf16[2,128,1024]{2,1,0:T(8,128)(2,1)S(1)}, u32[]{:S(2)}, u32[]{:S(2)}) collective-permute-start(bf16[2,128,1024]{2,1,0:T(8,128)(2,1)S(1)} %collective-permute-done.refs_1_), channel_id=1, source_target_pairs={{0,1},{1,2},{2,3},{3,4},{4,5},{5,6},{6,7},{7,0},{8,9},{9,10},{10,1... | collective-permute-start | bytes 1572872 | tf_op jit(solution)/shard_map/ppermute | solution.py:18
  25.6 16.2 %collective-permute-start.4 = (bf16[2,128,1024]{2,1,0:T(8,128)(2,1)S(1)}, bf16[2,128,1024]{2,1,0:T(8,128)(2,1)S(1)}, u32[]{:S(2)}, u32[]{:S(2)}) collective-permute-start(bf16[2,128,1024]{2,1,0:T(8,128)(2,1)S(1)} %collective-permute-done.3.refs_4_), channel_id=1, source_target_pairs={{0,7},{1,0},{2,1},{3,2},{4,3},{5,4},{6,5},{7,6},{8,15},{9,8},{10,9... | collective-permute-start | bytes 1572872 | tf_op jit(solution)/shard_map/ppermute | solution.py:18
  39.9 31.8 %collective-permute-start.2 = (bf16[2,128,1024]{2,1,0:T(8,128)(2,1)S(1)}, bf16[2,128,1024]{2,1,0:T(8,128)(2,1)S(1)}, u32[]{:S(2)}, u32[]{:S(2)}) collective-permute-start(bf16[2,128,1024]{2,1,0:T(8,128)(2,1)S(1)} %collective-permute-done.1.refs_2_), channel_id=1, source_target_pairs={{0,1},{1,2},{2,3},{3,4},{4,5},{5,6},{6,7},{7,0},{8,9},{9,10},{10,1... | collective-permute-start | bytes 1572872 | tf_op jit(solution)/shard_map/ppermute | solution.py:18
  41.8 31.8 %collective-permute-start.5 = (bf16[2,128,1024]{2,1,0:T(8,128)(2,1)S(1)}, bf16[2,128,1024]{2,1,0:T(8,128)(2,1)S(1)}, u32[]{:S(2)}, u32[]{:S(2)}) collective-permute-start(bf16[2,128,1024]{2,1,0:T(8,128)(2,1)S(1)} %collective-permute-done.4.refs_5_), channel_id=1, source_target_pairs={{0,7},{1,0},{2,1},{3,2},{4,3},{5,4},{6,5},{7,6},{8,15},{9,8},{10,9... | collective-permute-start | bytes 1572872 | tf_op jit(solution)/shard_map/ppermute | solution.py:18
  47.0 1.0 copy-start
  48.0 0.7 copy-start.4
  48.7 37.3 %copy-start.3 = (bf16[2,128,1024]{2,1,0:T(8,128)(2,1)S(1)}, bf16[2,128,1024]{2,1,0:T(8,128)(2,1)}, u32[]{:S(2)}) copy-start(bf16[2,128,1024]{2,1,0:T(8,128)(2,1)} %refs_11_.1) | copy-start | bytes 1572868
  48.8 12.8 %collective-permute-start.10 = (bf16[1168,128]{1,0:T(8,128)(2,1)S(1)}, bf16[1168,128]{1,0:T(8,128)(2,1)S(1)}, u32[]{:S(2)}, u32[]{:S(2)}) collective-permute-start(bf16[1168,128]{1,0:T(8,128)(2,1)S(1)} %shard_map.62.refs_0_), channel_id=1, source_target_pairs={{0,1},{1,2},{2,3},{3,4},{4,5},{5,6},{6,7},{7,0},{8,9},{9,10},{10,1... | collective-permute-start | bytes 897032 | tf_op jit(solution)/shard_map/ppermute | solution.py:18
  50.8 12.8 %collective-permute-start.13 = (bf16[1168,128]{1,0:T(8,128)(2,1)S(1)}, bf16[1168,128]{1,0:T(8,128)(2,1)S(1)}, u32[]{:S(2)}, u32[]{:S(2)}) collective-permute-start(bf16[1168,128]{1,0:T(8,128)(2,1)S(1)} %shard_map.62.refs_0_), channel_id=1, source_target_pairs={{0,7},{1,0},{2,1},{3,2},{4,3},{5,4},{6,5},{7,6},{8,15},{9,8},{10,9... | collective-permute-start | bytes 897032 | tf_op jit(solution)/shard_map/ppermute | solution.py:18
  61.6 17.2 %collective-permute-start.11 = (bf16[1168,128]{1,0:T(8,128)(2,1)S(1)}, bf16[1168,128]{1,0:T(8,128)(2,1)S(1)}, u32[]{:S(2)}, u32[]{:S(2)}) collective-permute-start(bf16[1168,128]{1,0:T(8,128)(2,1)S(1)} %collective-permute-done.10.refs_1_), channel_id=1, source_target_pairs={{0,1},{1,2},{2,3},{3,4},{4,5},{5,6},{6,7},{7,0},{8,9},{9,10},{10,1... | collective-permute-start | bytes 897032 | tf_op jit(solution)/shard_map/ppermute | solution.py:18
  63.5 17.2 %collective-permute-start.14 = (bf16[1168,128]{1,0:T(8,128)(2,1)S(1)}, bf16[1168,128]{1,0:T(8,128)(2,1)S(1)}, u32[]{:S(2)}, u32[]{:S(2)}) collective-permute-start(bf16[1168,128]{1,0:T(8,128)(2,1)S(1)} %collective-permute-done.13.refs_4_), channel_id=1, source_target_pairs={{0,7},{1,0},{2,1},{3,2},{4,3},{5,4},{6,5},{7,6},{8,15},{9,8},{10,9... | collective-permute-start | bytes 897032 | tf_op jit(solution)/shard_map/ppermute | solution.py:18
  68.7 1.0 copy-start.2
  69.8 16.2 %collective-permute-start.8 = (bf16[128,1024]{1,0:T(8,128)(2,1)S(1)}, bf16[128,1024]{1,0:T(8,128)(2,1)S(1)}, u32[]{:S(2)}, u32[]{:S(2)}) collective-permute-start(bf16[128,1024]{1,0:T(8,128)(2,1)S(1)} %shard_map.60), channel_id=1, source_target_pairs={{0,8},{8,16},{16,24},{24,32},{32,40},{40,48},{48,56},{56,64},{64,7... | collective-permute-start | bytes 786440 | tf_op jit(solution)/shard_map/ppermute | solution.py:18
  71.7 14.2 %collective-permute-start.6 = (bf16[128,1024]{1,0:T(8,128)(2,1)S(1)}, bf16[128,1024]{1,0:T(8,128)(2,1)S(1)}, u32[]{:S(2)}, u32[]{:S(2)}) collective-permute-start(bf16[128,1024]{1,0:T(8,128)(2,1)S(1)} %shard_map.58.refs_1_), channel_id=1, source_target_pairs={{0,1},{1,2},{2,3},{3,4},{4,5},{5,6},{6,7},{7,0},{8,9},{9,10},{10,1... | collective-permute-start | bytes 786440 | tf_op jit(solution)/shard_map/ppermute | solution.py:18
  73.7 12.3 %collective-permute-start.7 = (bf16[128,1024]{1,0:T(8,128)(2,1)S(1)}, bf16[128,1024]{1,0:T(8,128)(2,1)S(1)}, u32[]{:S(2)}, u32[]{:S(2)}) collective-permute-start(bf16[128,1024]{1,0:T(8,128)(2,1)S(1)} %shard_map.59.refs_2_), channel_id=1, source_target_pairs={{0,7},{1,0},{2,1},{3,2},{4,3},{5,4},{6,5},{7,6},{8,15},{9,8},{10,9... | collective-permute-start | bytes 786440 | tf_op jit(solution)/shard_map/ppermute | solution.py:18
  78.8 12.1 %collective-permute-start.12 = (bf16[1168,128]{1,0:T(8,128)(2,1)S(1)}, bf16[1168,128]{1,0:T(8,128)(2,1)S(1)}, u32[]{:S(2)}, u32[]{:S(2)}) collective-permute-start(bf16[1168,128]{1,0:T(8,128)(2,1)S(1)} %collective-permute-done.11.refs_2_), channel_id=1, source_target_pairs={{0,1},{1,2},{2,3},{3,4},{4,5},{5,6},{6,7},{7,0},{8,9},{9,10},{10,1... | collective-permute-start | bytes 897032 | tf_op jit(solution)/shard_map/ppermute | solution.py:18
  80.8 12.1 %collective-permute-start.15 = (bf16[1168,128]{1,0:T(8,128)(2,1)S(1)}, bf16[1168,128]{1,0:T(8,128)(2,1)S(1)}, u32[]{:S(2)}, u32[]{:S(2)}) collective-permute-start(bf16[1168,128]{1,0:T(8,128)(2,1)S(1)} %collective-permute-done.14.refs_5_), channel_id=1, source_target_pairs={{0,7},{1,0},{2,1},{3,2},{4,3},{5,4},{6,5},{7,6},{8,15},{9,8},{10,9... | collective-permute-start | bytes 897032 | tf_op jit(solution)/shard_map/ppermute | solution.py:18
  87.3 18.2 %collective-permute-start.9 = (bf16[256,1024]{1,0:T(8,128)(2,1)S(1)}, bf16[256,1024]{1,0:T(8,128)(2,1)S(1)}, u32[]{:S(2)}, u32[]{:S(2)}) collective-permute-start(bf16[256,1024]{1,0:T(8,128)(2,1)S(1)} %get-tuple-element.14.refs_12_), channel_id=1, source_target_pairs={{0,8},{8,16},{16,24},{24,32},{32,40},{40,48},{48,56},{56,64},{64,7... | collective-permute-start | bytes 1572872 | tf_op jit(solution)/shard_map/ppermute | solution.py:18
  91.0 11.2 %collective-permute-start.16 = (bf16[592,128]{1,0:T(8,128)(2,1)S(1)}, bf16[592,128]{1,0:T(8,128)(2,1)S(1)}, u32[]{:S(2)}, u32[]{:S(2)}) collective-permute-start(bf16[592,128]{1,0:T(8,128)(2,1)S(1)} %shard_map.63), channel_id=1, source_target_pairs={{0,1},{1,2},{2,3},{3,4},{4,5},{5,6},{6,7},{7,0},{8,9},{9,10},{10,1... | collective-permute-start | bytes 454664 | tf_op jit(solution)/shard_map/ppermute | solution.py:18
  92.9 9.2 %collective-permute-start.17 = (bf16[576,128]{1,0:T(8,128)(2,1)S(1)}, bf16[576,128]{1,0:T(8,128)(2,1)S(1)}, u32[]{:S(2)}, u32[]{:S(2)}) collective-permute-start(bf16[576,128]{1,0:T(8,128)(2,1)S(1)} %shard_map.64), channel_id=1, source_target_pairs={{0,7},{1,0},{2,1},{3,2},{4,3},{5,4},{6,5},{7,6},{8,15},{9,8},{10,9... | collective-permute-start | bytes 442376 | tf_op jit(solution)/shard_map/ppermute | solution.py:18
  106.6 8.2 %collective-permute-start.19 = (bf16[144,1024]{1,0:T(8,128)(2,1)S(1)}, bf16[144,1024]{1,0:T(8,128)(2,1)S(1)}, u32[]{:S(2)}, u32[]{:S(2)}) collective-permute-start(bf16[144,1024]{1,0:T(8,128)(2,1)S(1)} %shard_map.66.refs_6_), channel_id=1, source_target_pairs={{0,504},{8,0},{16,8},{24,16},{32,24},{40,32},{48,40},{56,48},{64,5... | collective-permute-start | bytes 884744 | tf_op jit(solution)/shard_map/ppermute | solution.py:18
  112.0 9.4 %collective-permute-start.18 = (bf16[272,1024]{1,0:T(8,128)(2,1)S(1)}, bf16[272,1024]{1,0:T(8,128)(2,1)S(1)}, u32[]{:S(2)}, u32[]{:S(2)}) collective-permute-start(bf16[272,1024]{1,0:T(8,128)(2,1)S(1)} %shard_map.67.refs_2_), channel_id=1, source_target_pairs={{0,504},{8,0},{16,8},{24,16},{32,24},{40,32},{48,40},{56,48},{64,5... | collective-permute-start | bytes 1671176 | tf_op jit(solution)/shard_map/ppermute | solution.py:18
  114.8 6.6 %copy-start.1 = (bf16[2,128,1024]{2,1,0:T(8,128)(2,1)S(1)}, bf16[2,128,1024]{2,1,0:T(8,128)(2,1)}, u32[]{:S(2)}) copy-start(bf16[2,128,1024]{2,1,0:T(8,128)(2,1)} %refs_6_.1) | copy-start | bytes 1572868
  116.4 17.1 %collective-permute-start.20 = (bf16[144,1024]{1,0:T(8,128)(2,1)S(1)}, bf16[144,1024]{1,0:T(8,128)(2,1)S(1)}, u32[]{:S(2)}, u32[]{:S(2)}) collective-permute-start(bf16[144,1024]{1,0:T(8,128)(2,1)S(1)} %shard_map.69.refs_5_), channel_id=1, source_target_pairs={{0,504},{8,0},{16,8},{24,16},{32,24},{40,32},{48,40},{56,48},{64,5... | collective-permute-start | bytes 884744 | tf_op jit(solution)/shard_map/ppermute | solution.py:18
  118.3 15.2 %collective-permute-start.21 = (bf16[128,1024]{1,0:T(8,128)(2,1)S(1)}, bf16[128,1024]{1,0:T(8,128)(2,1)S(1)}, u32[]{:S(2)}, u32[]{:S(2)}) collective-permute-start(bf16[128,1024]{1,0:T(8,128)(2,1)S(1)} %shard_map.68.refs_6_), channel_id=1, source_target_pairs={{0,496},{8,504},{16,0},{24,8},{32,16},{40,24},{48,32},{56,40},{64,... | collective-permute-start | bytes 786440 | tf_op jit(solution)/shard_map/ppermute | solution.py:18
  121.4 12.1 %copy-start.5 = (bf16[2,128]{1,0:T(2,128)(2,1)S(1)}, bf16[2,128]{1,0:T(2,128)(2,1)}, u32[]{:S(2)}) copy-start(bf16[2,128]{1,0:T(2,128)(2,1)} %refs_7_.1) | copy-start | bytes 1540

commit v4 on v3

--- a/solution.py
+++ b/solution.py
@@ -175,15 +175,37 @@
     m_in = hop(m, "tm", 1)
 
     def opened(*refs):
-        even_last, odd_last, b1_ref, b2_ref, own = refs[n : n + 5]
-        close_ref, far_ref, head_ref, line_ref, l_ev, l_od, g_ref = refs[n + 5 :]
-        unpack([(way, (ref, 0)) for way, ref in zip(offsets, refs)] + [(half, (even_last, 0))], l_ev, count)
-        unpack([(way, (ref, packed + TAIL)) for way, ref in zip(offsets, refs)] + [(half, (odd_last, 0))], l_od, count)
-        for way, ref in list(zip(offsets, refs)) + [(half, even_last)]:
+        last, b1_ref = refs[n : n + 2]
+        close_ref, l_ev, g_ref = refs[n + 2 :]
+        unpack([(way, (ref, 0)) for way, ref in zip(offsets, refs)] + [(half, (last, 0))], l_ev, count)
+        for way, ref in list(zip(offsets, refs)) + [(half, last)]:
             column = pl.multiple_of(slot(way, count) * rows, rows)
             g_ref[:, pl.ds(column, rows)] = ref[packed : packed + TAIL, :]
+        close_ref[...] = by_symmetric(b1_ref[...], l_ev[...])
+
+    close, l_even, g_all = call(
+        opened,
+        l_arrays + [l_even_last, b1_in],
+        [wide, whole, kept((TAIL, size), BF16)],
+        2 * product,
+        after=(m,),
+    )
+
+    def fourth(m_ref, l_ev, g_ref, out):
+        past = lax.axis_index("tm") < 2
+        own = m_ref[rows:, :]
+        out[:rows, :] = jnp.where(past, 0.0, by_symmetric(own, l_ev[...])).astype(BF16)
+        out[rows:, :] = jnp.zeros((TAIL, size), BF16)
+        out[rows:, :rows] = two_rows(jnp.where(past, 0.0, nt(g_ref[...], own)[0:1]))
+
+    (v,) = call(fourth, [m_in, l_even, g_all], [short], 2 * product)
+    v_in = hop(v, "tm", -1)
+
+    def odds(*refs):
+        last, b1_ref, b2_ref, own, g_ref = refs[n : n + 5]
+        far_ref, head_ref, line_ref, l_od = refs[n + 5 :]
+        unpack([(way, (ref, packed + TAIL)) for way, ref in zip(offsets, refs)] + [(half, (last, 0))], l_od, count)
         g = g_ref[...]
-        close_ref[...] = by_symmetric(b1_ref[...], l_ev[...])
         far = by_symmetric(jnp.concatenate([own[0], b2_ref[...]], axis=0), l_od[...])
         head_ref[...] = far[:rows]
         far_ref[...] = far[rows:]
@@ -191,23 +213,13 @@
         row = nt(g, b1_ref[...])[0:1] + nt(g, b2_ref[...])[1:2]
         line_ref[...] = jnp.where(index == 0, row, nt(g, own[0])[1:2])
 
-    close, far, head, line_, l_even, l_odd, g_all = call(
-        opened,
-        l_arrays + [l_even_last, l_odd_last, b1_in, b2, trans],
-        [wide, wide, wide, line, whole, whole, kept((TAIL, size), BF16)],
-        6 * product,
-        after=(m,),
-    )
-
-    def fourth(m_ref, l_ev, g_ref, out):
-        past = lax.axis_index("tm") < 2
-        own = m_ref[rows:, :]
-        out[:rows, :] = jnp.where(past, 0.0, by_symmetric(own, l_ev[...])).astype(BF16)
-        out[rows:, :] = jnp.zeros((TAIL, size), BF16)
-        out[rows:, :rows] = two_rows(jnp.where(past, 0.0, nt(g_ref[...], own)[0:1]))
-
-    (v,) = call(fourth, [m_in, l_even, g_all], [short], 2 * product)
-    v_in = hop(v, "tm", -1)
+    far, head, line_, l_odd = call(
+        odds,
+        l_arrays + [l_odd_last, b1_in, b2, trans, g_all],
+        [wide, wide, line, whole],
+        4 * product,
+        after=(v,),
+    )
 
     def third(m_ref, even, odd, l_ev, l_od, g_ref, out):
         past = lax.axis_index("tm") < 1
@@ -225,14 +237,6 @@
     (w,) = call(third, [m_in, e_even, e_odd, l_even, l_odd, g_all], [long], 7 * product, after=(v,))
     w_in = hop(w, "tm", -1)
 
-    def fifth(m_ref, even, b4_ref):
-        own = m_ref[rows:, :]
-        past = lax.axis_index("tm") < 2
-        b4_ref[...] = jnp.where(past, own.astype(F32), nn(own, even[...])).astype(BF16)
-
-    (b4,) = call(fifth, [m_in, e_even], [panel], product, after=(w,))
-    b4_in = hop(b4, "tm", -2)
-
     def sixth(v_ref, close_ref, far_ref, line_ref, even, odd, m_ref):
         past = lax.axis_index("tm") < 1
         behind = far_ref[...] + nt(v_ref[:rows, :], odd[...])
@@ -242,14 +246,22 @@
         m_ref[rows:, :] = jnp.zeros((TAIL, size), BF16)
         m_ref[rows:, :rows] = two_rows(jnp.where(past, 0.0, row))
 
-    (u,) = call(sixth, [v_in, close, far, line_, e_even, e_odd], [short], 2 * product, after=(b4,))
+    (u,) = call(sixth, [v_in, close, far, line_, e_even, e_odd], [short], 2 * product, after=(w,))
     u_in = hop(u, "tm", -1)
+
+    def fifth(m_ref, even, b4_ref):
+        own = m_ref[rows:, :]
+        past = lax.axis_index("tm") < 2
+        b4_ref[...] = jnp.where(past, own.astype(F32), nn(own, even[...])).astype(BF16)
+
+    (b4,) = call(fifth, [m_in, e_even], [panel], product, after=(u,))
+    b4_in = hop(b4, "tm", -2)
 
     def seventh(w_ref, head_ref, even, odd, l_own, out):
         inner = head_ref[...] + nt(w_ref[:rows, :], odd[...])
         out[...] = (nt(inner.astype(BF16), even[...]) + l_own[0].astype(F32)).astype(BF16)
 
-    (l_first,) = call(seventh, [w_in, head, e_even, e_odd, spread], [panel], 2 * product, after=(u,))
+    (l_first,) = call(seventh, [w_in, head, e_even, e_odd, spread], [panel], 2 * product, after=(b4,))
 
     def eighth(w_ref, u_ref, b4_ref, line_ref, odd, l_ref, l_own, g_own, e_out, g_out, l_out):
         l_out[1] = (nt(u_ref[:rows, :], odd[...]) + l_own[1].astype(F32)).astype(BF16)

time: 136 us -> 134 us (0.985)
  waiting for transfers between devices: 40.5 us -> 38.9 us
    ppermute x22, waiting for transfers between devices: 40.5 us -> 38.9 us  [hop(): lax.ppermute(block, axis, [(i, (i + distance) % size) for i in range(size)])]
    pallas_call x14 -> x15, Pallas kernels: 14.6 us -> 14.7 us  [call(): pl.pallas_call(run, in_specs=[VMEM] * count + [HBM] * len(after), out_spe...]
  transfers between devices with their start and end apart: 22 -> 22, of which waited for: 6 -> 6; matrix products, arithmetic and copies ran while one was open for 0% -> 0% of each run, Pallas kernels for 9% -> 10%
where the time goes in v4:
time: 134 us; the launch traced here: 133 us
  starting transfers between devices  76 us (57%)
  waiting for transfers between devices  38.9 us (29%)
  Pallas kernels  14.7 us (11%)
  local copies, waits for them, and re-layouts  2.74 us (2%)
    ppermute x22, starting transfers between devices, hop(): lax.ppermute(block, axis, [(i, (i + distance) % size) for i in range(size)])  76 us
    ppermute x22, waiting for transfers between devices, hop(): lax.ppermute(block, axis, [(i, (i + distance) % size) for i in range(size)])  38.9 us
    pallas_call x15, Pallas kernels, call(): pl.pallas_call(run, in_specs=[VMEM] * count + [HBM] * len(after), out_spe...  14.7 us
    unnamed x12, local copies, waits for them, and re-layouts  2.74 us
  transfers between devices with their start and end apart: 22, of which 6 were waited for; matrix products, arithmetic and copies ran while one was open for 0% of the time, Pallas kernels for 10%

profile of v4, /device:TPU:30, one launch (start us, length us, event | category | flops | bytes accessed | tf_op | source)
XLA Modules:
  0.0 133.4 jit_solution(17260259994055250724)
XLA Ops:
  0.6 4.3 %collective-permute-start = (bf16[2,128,1024]{2,1,0:T(8,128)(2,1)}, bf16[2,128,1024]{2,1,0:T(8,128)(2,1)S(1)}, u32[]{:S(2)}, u32[]{:S(2)}) collective-permute-start(bf16[2,128,1024]{2,1,0:T(8,128)(2,1)} %refs_10_.1), channel_id=1, source_target_pairs={{0,1},{1,2},{2,3},{3,4},{4,5},{5,6},{6,7},{7,0},{8,9},{9,10},{10,1... | collective-permute-start | bytes 1572872 | tf_op jit(solution)/shard_map/ppermute | solution.py:18
  4.9 8.6 %collective-permute-start.3 = (bf16[2,128,1024]{2,1,0:T(8,128)(2,1)}, bf16[2,128,1024]{2,1,0:T(8,128)(2,1)S(1)}, u32[]{:S(2)}, u32[]{:S(2)}) collective-permute-start(bf16[2,128,1024]{2,1,0:T(8,128)(2,1)} %refs_10_.1), channel_id=1, source_target_pairs={{0,7},{1,0},{2,1},{3,2},{4,3},{5,4},{6,5},{7,6},{8,15},{9,8},{10,9... | collective-permute-start | bytes 1572872 | tf_op jit(solution)/shard_map/ppermute | solution.py:18
  13.5 10.2 %collective-permute-done.refs_1_ = bf16[2,128,1024]{2,1,0:T(8,128)(2,1)S(1)} collective-permute-done((bf16[2,128,1024]{2,1,0:T(8,128)(2,1)}, bf16[2,128,1024]{2,1,0:T(8,128)(2,1)S(1)}, u32[]{:S(2)}, u32[]{:S(2)}) %collective-permute-start) | collective-permute-done | bytes 524320 | tf_op jit(solution)/shard_map/ppermute | solution.py:18
  23.7 1.9 %collective-permute-start.1 = (bf16[2,128,1024]{2,1,0:T(8,128)(2,1)S(1)}, bf16[2,128,1024]{2,1,0:T(8,128)(2,1)S(1)}, u32[]{:S(2)}, u32[]{:S(2)}) collective-permute-start(bf16[2,128,1024]{2,1,0:T(8,128)(2,1)S(1)} %collective-permute-done.refs_1_), channel_id=1, source_target_pairs={{0,1},{1,2},{2,3},{3,4},{4,5},{5,6},{6,7},{7,0},{8,9},{9,10},{10,1... | collective-permute-start | bytes 1572872 | tf_op jit(solution)/shard_map/ppermute | solution.py:18
  25.6 0.0 collective-permute-done.3.refs_4_
  25.6 5.1 %collective-permute-start.4 = (bf16[2,128,1024]{2,1,0:T(8,128)(2,1)S(1)}, bf16[2,128,1024]{2,1,0:T(8,128)(2,1)S(1)}, u32[]{:S(2)}, u32[]{:S(2)}) collective-permute-start(bf16[2,128,1024]{2,1,0:T(8,128)(2,1)S(1)} %collective-permute-done.3.refs_4_), channel_id=1, source_target_pairs={{0,7},{1,0},{2,1},{3,2},{4,3},{5,4},{6,5},{7,6},{8,15},{9,8},{10,9... | collective-permute-start | bytes 1572872 | tf_op jit(solution)/shard_map/ppermute | solution.py:18
  30.8 9.1 %collective-permute-done.1.refs_2_ = bf16[2,128,1024]{2,1,0:T(8,128)(2,1)S(1)} collective-permute-done((bf16[2,128,1024]{2,1,0:T(8,128)(2,1)S(1)}, bf16[2,128,1024]{2,1,0:T(8,128)(2,1)S(1)}, u32[]{:S(2)}, u32[]{:S(2)}) %collective-permute-start.1) | collective-permute-done | bytes 524320 | tf_op jit(solution)/shard_map/ppermute | solution.py:18
  39.9 1.9 %collective-permute-start.2 = (bf16[2,128,1024]{2,1,0:T(8,128)(2,1)S(1)}, bf16[2,128,1024]{2,1,0:T(8,128)(2,1)S(1)}, u32[]{:S(2)}, u32[]{:S(2)}) collective-permute-start(bf16[2,128,1024]{2,1,0:T(8,128)(2,1)S(1)} %collective-permute-done.1.refs_2_), channel_id=1, source_target_pairs={{0,1},{1,2},{2,3},{3,4},{4,5},{5,6},{6,7},{7,0},{8,9},{9,10},{10,1... | collective-permute-start | bytes 1572872 | tf_op jit(solution)/shard_map/ppermute | solution.py:18
  41.8 0.0 collective-permute-done.4.refs_5_
  41.8 5.1 %collective-permute-start.5 = (bf16[2,128,1024]{2,1,0:T(8,128)(2,1)S(1)}, bf16[2,128,1024]{2,1,0:T(8,128)(2,1)S(1)}, u32[]{:S(2)}, u32[]{:S(2)}) collective-permute-start(bf16[2,128,1024]{2,1,0:T(8,128)(2,1)S(1)} %collective-permute-done.4.refs_5_), channel_id=1, source_target_pairs={{0,7},{1,0},{2,1},{3,2},{4,3},{5,4},{6,5},{7,6},{8,15},{9,8},{10,9... | collective-permute-start | bytes 1572872 | tf_op jit(solution)/shard_map/ppermute | solution.py:18
  47.0 0.0 copy-start
  47.0 1.0 copy-done
  48.0 0.7 copy-done.4
  48.7 0.2 shard_map.62.refs_0_
  48.8 1.9 %collective-permute-start.10 = (bf16[1168,128]{1,0:T(8,128)(2,1)S(1)}, bf16[1168,128]{1,0:T(8,128)(2,1)S(1)}, u32[]{:S(2)}, u32[]{:S(2)}) collective-permute-start(bf16[1168,128]{1,0:T(8,128)(2,1)S(1)} %shard_map.62.refs_0_), channel_id=1, source_target_pairs={{0,1},{1,2},{2,3},{3,4},{4,5},{5,6},{6,7},{7,0},{8,9},{9,10},{10,1... | collective-permute-start | bytes 897032 | tf_op jit(solution)/shard_map/ppermute | solution.py:18
  50.8 5.1 %collective-permute-start.13 = (bf16[1168,128]{1,0:T(8,128)(2,1)S(1)}, bf16[1168,128]{1,0:T(8,128)(2,1)S(1)}, u32[]{:S(2)}, u32[]{:S(2)}) collective-permute-start(bf16[1168,128]{1,0:T(8,128)(2,1)S(1)} %shard_map.62.refs_0_), channel_id=1, source_target_pairs={{0,7},{1,0},{2,1},{3,2},{4,3},{5,4},{6,5},{7,6},{8,15},{9,8},{10,9... | collective-permute-start | bytes 897032 | tf_op jit(solution)/shard_map/ppermute | solution.py:18
  55.9 0.0 copy-start.2
  55.9 1.0 copy-done.2
  57.0 1.9 %collective-permute-start.8 = (bf16[128,1024]{1,0:T(8,128)(2,1)S(1)}, bf16[128,1024]{1,0:T(8,128)(2,1)S(1)}, u32[]{:S(2)}, u32[]{:S(2)}) collective-permute-start(bf16[128,1024]{1,0:T(8,128)(2,1)S(1)} %shard_map.60), channel_id=1, source_target_pairs={{0,8},{8,16},{16,24},{24,32},{32,40},{40,48},{48,56},{56,64},{64,7... | collective-permute-start | bytes 786440 | tf_op jit(solution)/shard_map/ppermute | solution.py:18
  58.9 1.9 %collective-permute-start.6 = (bf16[128,1024]{1,0:T(8,128)(2,1)S(1)}, bf16[128,1024]{1,0:T(8,128)(2,1)S(1)}, u32[]{:S(2)}, u32[]{:S(2)}) collective-permute-start(bf16[128,1024]{1,0:T(8,128)(2,1)S(1)} %shard_map.58.refs_1_), channel_id=1, source_target_pairs={{0,1},{1,2},{2,3},{3,4},{4,5},{5,6},{6,7},{7,0},{8,9},{9,10},{10,1... | collective-permute-start | bytes 786440 | tf_op jit(solution)/shard_map/ppermute | solution.py:18
  60.9 0.0 collective-permute-done.5.refs_0_.refs_6_
  60.9 5.1 %collective-permute-start.7 = (bf16[128,1024]{1,0:T(8,128)(2,1)S(1)}, bf16[128,1024]{1,0:T(8,128)(2,1)S(1)}, u32[]{:S(2)}, u32[]{:S(2)}) collective-permute-start(bf16[128,1024]{1,0:T(8,128)(2,1)S(1)} %shard_map.59.refs_2_), channel_id=1, source_target_pairs={{0,7},{1,0},{2,1},{3,2},{4,3},{5,4},{6,5},{7,6},{8,15},{9,8},{10,9... | collective-permute-start | bytes 786440 | tf_op jit(solution)/shard_map/ppermute | solution.py:18
  66.0 0.0 collective-permute-done.10.refs_1_
  66.0 1.9 %collective-permute-start.11 = (bf16[1168,128]{1,0:T(8,128)(2,1)S(1)}, bf16[1168,128]{1,0:T(8,128)(2,1)S(1)}, u32[]{:S(2)}, u32[]{:S(2)}) collective-permute-start(bf16[1168,128]{1,0:T(8,128)(2,1)S(1)} %collective-permute-done.10.refs_1_), channel_id=1, source_target_pairs={{0,1},{1,2},{2,3},{3,4},{4,5},{5,6},{6,7},{7,0},{8,9},{9,10},{10,1... | collective-permute-start | bytes 897032 | tf_op jit(solution)/shard_map/ppermute | solution.py:18
  68.0 5.1 %collective-permute-start.14 = (bf16[1168,128]{1,0:T(8,128)(2,1)S(1)}, bf16[1168,128]{1,0:T(8,128)(2,1)S(1)}, u32[]{:S(2)}, u32[]{:S(2)}) collective-permute-start(bf16[1168,128]{1,0:T(8,128)(2,1)S(1)} %collective-permute-done.13.refs_4_), channel_id=1, source_target_pairs={{0,7},{1,0},{2,1},{3,2},{4,3},{5,4},{6,5},{7,6},{8,15},{9,8},{10,9... | collective-permute-start | bytes 897032 | tf_op jit(solution)/shard_map/ppermute | solution.py:18
  73.2 1.3 shard_map.61
  74.5 3.7 %collective-permute-start.9 = (bf16[256,1024]{1,0:T(8,128)(2,1)S(1)}, bf16[256,1024]{1,0:T(8,128)(2,1)S(1)}, u32[]{:S(2)}, u32[]{:S(2)}) collective-permute-start(bf16[256,1024]{1,0:T(8,128)(2,1)S(1)} %get-tuple-element.14.refs_9_), channel_id=1, source_target_pairs={{0,8},{8,16},{16,24},{24,32},{32,40},{40,48},{48,56},{56,64},{64,7... | collective-permute-start | bytes 1572872 | tf_op jit(solution)/shard_map/ppermute | solution.py:18
  78.2 1.9 %collective-permute-start.12 = (bf16[1168,128]{1,0:T(8,128)(2,1)S(1)}, bf16[1168,128]{1,0:T(8,128)(2,1)S(1)}, u32[]{:S(2)}, u32[]{:S(2)}) collective-permute-start(bf16[1168,128]{1,0:T(8,128)(2,1)S(1)} %collective-permute-done.11.refs_2_), channel_id=1, source_target_pairs={{0,1},{1,2},{2,3},{3,4},{4,5},{5,6},{6,7},{7,0},{8,9},{9,10},{10,1... | collective-permute-start | bytes 897032 | tf_op jit(solution)/shard_map/ppermute | solution.py:18
  80.1 5.1 %collective-permute-start.15 = (bf16[1168,128]{1,0:T(8,128)(2,1)S(1)}, bf16[1168,128]{1,0:T(8,128)(2,1)S(1)}, u32[]{:S(2)}, u32[]{:S(2)}) collective-permute-start(bf16[1168,128]{1,0:T(8,128)(2,1)S(1)} %collective-permute-done.14.refs_5_), channel_id=1, source_target_pairs={{0,7},{1,0},{2,1},{3,2},{4,3},{5,4},{6,5},{7,6},{8,15},{9,8},{10,9... | collective-permute-start | bytes 897032 | tf_op jit(solution)/shard_map/ppermute | solution.py:18
  85.2 5.8 %collective-permute-done.12.refs_0_.refs_3_ = bf16[1168,128]{1,0:T(8,128)(2,1)S(1)} collective-permute-done((bf16[1168,128]{1,0:T(8,128)(2,1)S(1)}, bf16[1168,128]{1,0:T(8,128)(2,1)S(1)}, u32[]{:S(2)}, u32[]{:S(2)}) %collective-permute-start.12) | collective-permute-done | bytes 299040 | tf_op jit(solution)/shard_map/ppermute | solution.py:18
  91.1 1.9 %collective-permute-start.16 = (bf16[592,128]{1,0:T(8,128)(2,1)S(1)}, bf16[592,128]{1,0:T(8,128)(2,1)S(1)}, u32[]{:S(2)}, u32[]{:S(2)}) collective-permute-start(bf16[592,128]{1,0:T(8,128)(2,1)S(1)} %shard_map.63), channel_id=1, source_target_pairs={{0,1},{1,2},{2,3},{3,4},{4,5},{5,6},{6,7},{7,0},{8,9},{9,10},{10,1... | collective-permute-start | bytes 454664 | tf_op jit(solution)/shard_map/ppermute | solution.py:18
  93.0 5.1 %collective-permute-start.17 = (bf16[576,128]{1,0:T(8,128)(2,1)S(1)}, bf16[576,128]{1,0:T(8,128)(2,1)S(1)}, u32[]{:S(2)}, u32[]{:S(2)}) collective-permute-start(bf16[576,128]{1,0:T(8,128)(2,1)S(1)} %shard_map.65), channel_id=1, source_target_pairs={{0,7},{1,0},{2,1},{3,2},{4,3},{5,4},{6,5},{7,6},{8,15},{9,8},{10,9... | collective-permute-start | bytes 442376 | tf_op jit(solution)/shard_map/ppermute | solution.py:18
  98.2 1.9 %collective-permute-done.16.refs_7_ = bf16[592,128]{1,0:T(8,128)(2,1)S(1)} collective-permute-done((bf16[592,128]{1,0:T(8,128)(2,1)S(1)}, bf16[592,128]{1,0:T(8,128)(2,1)S(1)}, u32[]{:S(2)}, u32[]{:S(2)}) %collective-permute-start.16) | collective-permute-done | bytes 151584 | tf_op jit(solution)/shard_map/ppermute | solution.py:18
  100.2 1.5 %shard_map.64 = (f32[128,1024]{1,0:T(8,128)S(1)}, bf16[1024,1024]{1,0:T(8,128)(2,1)S(1)}, bf16[16,1024]{1,0:T(8,128)(2,1)S(1)}) custom-call(bf16[1168,128]{1,0:T(8,128)(2,1)S(1)} %shard_map.62.refs_0_, bf16[1168,128]{1,0:T(8,128)(2,1)S(1)} %collective-permute-done.10.refs_1_, bf16[1168,128]{1,0:T(8,128)(2,1)S(1)} %collective-permute-done.11.refs_2_, ...), custom_call_target="tpu_custom_call" | custom-call | flops 536870912 | bytes 1048576 | tf_op jit(solution)/shard_map/pallas_call | solution.py:43
  101.7 1.1 shard_map.66.refs_12_.refs_6_
  102.9 1.9 %collective-permute-start.19 = (bf16[144,1024]{1,0:T(8,128)(2,1)S(1)}, bf16[144,1024]{1,0:T(8,128)(2,1)S(1)}, u32[]{:S(2)}, u32[]{:S(2)}) collective-permute-start(bf16[144,1024]{1,0:T(8,128)(2,1)S(1)} %shard_map.66.refs_12_.refs_6_), channel_id=1, source_target_pairs={{0,504},{8,0},{16,8},{24,16},{32,24},{40,32},{48,40},{56,48},{64,5... | collective-permute-start | bytes 884744 | tf_op jit(solution)/shard_map/ppermute | solution.py:18
  104.8 1.9 %shard_map.67 = (f32[128,1024]{1,0:T(8,128)S(1)}, f32[128,1024]{1,0:T(8,128)S(1)}, f32[8,128]{1,0:T(8,128)S(1)}, bf16[1024,1024]{1,0:T(8,128)(2,1)S(1)}) custom-call(bf16[1168,128]{1,0:T(8,128)(2,1)S(1)} %shard_map.62.refs_0_, bf16[1168,128]{1,0:T(8,128)(2,1)S(1)} %collective-permute-done.10.refs_1_, bf16[1168,128]{1,0:T(8,128)(2,1)S(1)} %collective-permute-done.11.refs_2_, ...), custom_call_target="tpu_custom_call" | custom-call | flops 1073741824 | bytes 1048576 | tf_op jit(solution)/shard_map/pallas_call | solution.py:43
  106.7 3.4 %shard_map.68.refs_6_ = bf16[272,1024]{1,0:T(8,128)(2,1)S(1)} custom-call(bf16[256,1024]{1,0:T(8,128)(2,1)S(1)} %collective-permute-done.9.refs_0_, bf16[1024,1024]{1,0:T(8,128)(2,1)S(1)} %get-tuple-element.15.refs_1_.refs_4_.refs_2_, bf16[1024,1024]{1,0:T(8,128)(2,1)S(1)} %get-tuple-element.16.refs_2_.refs_5_.refs_3_.refs_4_, ...), custom_call_target="tpu_custom_call" | custom-call | flops 1879048192 | bytes 1048576 | tf_op jit(solution)/shard_map/pallas_call | solution.py:43
  110.1 1.9 %collective-permute-start.18 = (bf16[272,1024]{1,0:T(8,128)(2,1)S(1)}, bf16[272,1024]{1,0:T(8,128)(2,1)S(1)}, u32[]{:S(2)}, u32[]{:S(2)}) collective-permute-start(bf16[272,1024]{1,0:T(8,128)(2,1)S(1)} %shard_map.68.refs_6_), channel_id=1, source_target_pairs={{0,504},{8,0},{16,8},{24,16},{32,24},{40,32},{48,40},{56,48},{64,5... | collective-permute-start | bytes 1671176 | tf_op jit(solution)/shard_map/ppermute | solution.py:18
  112.1 1.5 %shard_map.69.refs_2_ = bf16[144,1024]{1,0:T(8,128)(2,1)S(1)} custom-call(bf16[144,1024]{1,0:T(8,128)(2,1)S(1)} %collective-permute-done.19.refs_0_, f32[128,1024]{1,0:T(8,128)S(1)} %get-tuple-element.21.refs_1_, f32[128,1024]{1,0:T(8,128)S(1)} %get-tuple-element.22.refs_2_, f32[8,128]{1,0:T(8,128)S(1)} %get-tuple-element.23.refs_3_, ...), custom_call_target="tpu_custom_call" | custom-call | flops 536870912 | bytes 1048576 | tf_op jit(solution)/shard_map/pallas_call | solution.py:43
  113.6 0.0 copy-start.1
  113.6 2.1 %collective-permute-start.20 = (bf16[144,1024]{1,0:T(8,128)(2,1)S(1)}, bf16[144,1024]{1,0:T(8,128)(2,1)S(1)}, u32[]{:S(2)}, u32[]{:S(2)}) collective-permute-start(bf16[144,1024]{1,0:T(8,128)(2,1)S(1)} %shard_map.69.refs_2_), channel_id=1, source_target_pairs={{0,504},{8,0},{16,8},{24,16},{32,24},{40,32},{48,40},{56,48},{64,5... | collective-permute-start | bytes 884744 | tf_op jit(solution)/shard_map/ppermute | solution.py:18
  115.7 0.4 shard_map.70.refs_5_
  116.1 2.2 %collective-permute-start.21 = (bf16[128,1024]{1,0:T(8,128)(2,1)S(1)}, bf16[128,1024]{1,0:T(8,128)(2,1)S(1)}, u32[]{:S(2)}, u32[]{:S(2)}) collective-permute-start(bf16[128,1024]{1,0:T(8,128)(2,1)S(1)} %shard_map.70.refs_5_), channel_id=1, source_target_pairs={{0,496},{8,504},{16,0},{24,8},{32,16},{40,24},{48,32},{56,40},{64,... | collective-permute-start | bytes 786440 | tf_op jit(solution)/shard_map/ppermute | solution.py:18
  118.4 0.9 collective-permute-done.18.refs_0_
  119.2 1.5 %shard_map.71.refs_5_ = bf16[128,1024]{1,0:T(8,128)(2,1)S(1)} custom-call(bf16[272,1024]{1,0:T(8,128)(2,1)S(1)} %collective-permute-done.18.refs_0_, f32[128,1024]{1,0:T(8,128)S(1)} %get-tuple-element.24.refs_1_, bf16[1024,1024]{1,0:T(8,128)(2,1)S(1)} %get-tuple-element.15.refs_1_.refs_4_.refs_2_, ...), custom_call_target="tpu_custom_call" | custom-call | flops 536870912 | bytes 1048576 | tf_op jit(solution)/shard_map/pallas_call | solution.py:43
  120.7 10.9 %collective-permute-done.21.refs_2_ = bf16[128,1024]{1,0:T(8,128)(2,1)S(1)} collective-permute-done((bf16[128,1024]{1,0:T(8,128)(2,1)S(1)}, bf16[128,1024]{1,0:T(8,128)(2,1)S(1)}, u32[]{:S(2)}, u32[]{:S(2)}) %collective-permute-start.21) | collective-permute-done | bytes 262176 | tf_op jit(solution)/shard_map/ppermute | solution.py:18
  131.6 1.7 %shard_map.72 = (bf16[2,128,1024]{2,1,0:T(8,128)(2,1)}, bf16[2,128]{1,0:T(2,128)(2,1)}, bf16[2,128,1024]{2,1,0:T(8,128)(2,1)}) custom-call(bf16[272,1024]{1,0:T(8,128)(2,1)S(1)} %collective-permute-done.18.refs_0_, bf16[144,1024]{1,0:T(8,128)(2,1)S(1)} %collective-permute-done.20.refs_1_, bf16[128,1024]{1,0:T(8,128)(2,1)S(1)} %collective-permute-done.21.refs_2_, ...), custom_call_target="tpu_custom_call" | custom-call | flops 268435456 | bytes 1048576 | tf_op jit(solution)/shard_map/pallas_call | solution.py:43
  (23 shorter events, 0.1 us)
Async XLA Ops:
  0.6 23.1 %collective-permute-start = (bf16[2,128,1024]{2,1,0:T(8,128)(2,1)}, bf16[2,128,1024]{2,1,0:T(8,128)(2,1)S(1)}, u32[]{:S(2)}, u32[]{:S(2)}) collective-permute-start(bf16[2,128,1024]{2,1,0:T(8,128)(2,1)} %refs_10_.1), channel_id=1, source_target_pairs={{0,1},{1,2},{2,3},{3,4},{4,5},{5,6},{6,7},{7,0},{8,9},{9,10},{10,1... | collective-permute-start | bytes 1572872 | tf_op jit(solution)/shard_map/ppermute | solution.py:18
  4.9 20.7 %collective-permute-start.3 = (bf16[2,128,1024]{2,1,0:T(8,128)(2,1)}, bf16[2,128,1024]{2,1,0:T(8,128)(2,1)S(1)}, u32[]{:S(2)}, u32[]{:S(2)}) collective-permute-start(bf16[2,128,1024]{2,1,0:T(8,128)(2,1)} %refs_10_.1), channel_id=1, source_target_pairs={{0,7},{1,0},{2,1},{3,2},{4,3},{5,4},{6,5},{7,6},{8,15},{9,8},{10,9... | collective-permute-start | bytes 1572872 | tf_op jit(solution)/shard_map/ppermute | solution.py:18
  23.7 16.2 %collective-permute-start.1 = (bf16[2,128,1024]{2,1,0:T(8,128)(2,1)S(1)}, bf16[2,128,1024]{2,1,0:T(8,128)(2,1)S(1)}, u32[]{:S(2)}, u32[]{:S(2)}) collective-permute-start(bf16[2,128,1024]{2,1,0:T(8,128)(2,1)S(1)} %collective-permute-done.refs_1_), channel_id=1, source_target_pairs={{0,1},{1,2},{2,3},{3,4},{4,5},{5,6},{6,7},{7,0},{8,9},{9,10},{10,1... | collective-permute-start | bytes 1572872 | tf_op jit(solution)/shard_map/ppermute | solution.py:18
  25.6 16.2 %collective-permute-start.4 = (bf16[2,128,1024]{2,1,0:T(8,128)(2,1)S(1)}, bf16[2,128,1024]{2,1,0:T(8,128)(2,1)S(1)}, u32[]{:S(2)}, u32[]{:S(2)}) collective-permute-start(bf16[2,128,1024]{2,1,0:T(8,128)(2,1)S(1)} %collective-permute-done.3.refs_4_), channel_id=1, source_target_pairs={{0,7},{1,0},{2,1},{3,2},{4,3},{5,4},{6,5},{7,6},{8,15},{9,8},{10,9... | collective-permute-start | bytes 1572872 | tf_op jit(solution)/shard_map/ppermute | solution.py:18
  39.9 19.0 %collective-permute-start.2 = (bf16[2,128,1024]{2,1,0:T(8,128)(2,1)S(1)}, bf16[2,128,1024]{2,1,0:T(8,128)(2,1)S(1)}, u32[]{:S(2)}, u32[]{:S(2)}) collective-permute-start(bf16[2,128,1024]{2,1,0:T(8,128)(2,1)S(1)} %collective-permute-done.1.refs_2_), channel_id=1, source_target_pairs={{0,1},{1,2},{2,3},{3,4},{4,5},{5,6},{6,7},{7,0},{8,9},{9,10},{10,1... | collective-permute-start | bytes 1572872 | tf_op jit(solution)/shard_map/ppermute | solution.py:18
  41.8 19.0 %collective-permute-start.5 = (bf16[2,128,1024]{2,1,0:T(8,128)(2,1)S(1)}, bf16[2,128,1024]{2,1,0:T(8,128)(2,1)S(1)}, u32[]{:S(2)}, u32[]{:S(2)}) collective-permute-start(bf16[2,128,1024]{2,1,0:T(8,128)(2,1)S(1)} %collective-permute-done.4.refs_5_), channel_id=1, source_target_pairs={{0,7},{1,0},{2,1},{3,2},{4,3},{5,4},{6,5},{7,6},{8,15},{9,8},{10,9... | collective-permute-start | bytes 1572872 | tf_op jit(solution)/shard_map/ppermute | solution.py:18
  47.0 1.0 copy-start
  48.0 0.7 copy-start.4
  48.7 24.5 %copy-start.3 = (bf16[2,128,1024]{2,1,0:T(8,128)(2,1)S(1)}, bf16[2,128,1024]{2,1,0:T(8,128)(2,1)}, u32[]{:S(2)}) copy-start(bf16[2,128,1024]{2,1,0:T(8,128)(2,1)} %refs_10_.1) | copy-start | bytes 1572868
  48.8 17.2 %collective-permute-start.10 = (bf16[1168,128]{1,0:T(8,128)(2,1)S(1)}, bf16[1168,128]{1,0:T(8,128)(2,1)S(1)}, u32[]{:S(2)}, u32[]{:S(2)}) collective-permute-start(bf16[1168,128]{1,0:T(8,128)(2,1)S(1)} %shard_map.62.refs_0_), channel_id=1, source_target_pairs={{0,1},{1,2},{2,3},{3,4},{4,5},{5,6},{6,7},{7,0},{8,9},{9,10},{10,1... | collective-permute-start | bytes 897032 | tf_op jit(solution)/shard_map/ppermute | solution.py:18
  50.8 17.2 %collective-permute-start.13 = (bf16[1168,128]{1,0:T(8,128)(2,1)S(1)}, bf16[1168,128]{1,0:T(8,128)(2,1)S(1)}, u32[]{:S(2)}, u32[]{:S(2)}) collective-permute-start(bf16[1168,128]{1,0:T(8,128)(2,1)S(1)} %shard_map.62.refs_0_), channel_id=1, source_target_pairs={{0,7},{1,0},{2,1},{3,2},{4,3},{5,4},{6,5},{7,6},{8,15},{9,8},{10,9... | collective-permute-start | bytes 897032 | tf_op jit(solution)/shard_map/ppermute | solution.py:18
  55.9 1.0 copy-start.2
  57.0 16.2 %collective-permute-start.8 = (bf16[128,1024]{1,0:T(8,128)(2,1)S(1)}, bf16[128,1024]{1,0:T(8,128)(2,1)S(1)}, u32[]{:S(2)}, u32[]{:S(2)}) collective-permute-start(bf16[128,1024]{1,0:T(8,128)(2,1)S(1)} %shard_map.60), channel_id=1, source_target_pairs={{0,8},{8,16},{16,24},{24,32},{32,40},{40,48},{48,56},{56,64},{64,7... | collective-permute-start | bytes 786440 | tf_op jit(solution)/shard_map/ppermute | solution.py:18
  58.9 14.2 %collective-permute-start.6 = (bf16[128,1024]{1,0:T(8,128)(2,1)S(1)}, bf16[128,1024]{1,0:T(8,128)(2,1)S(1)}, u32[]{:S(2)}, u32[]{:S(2)}) collective-permute-start(bf16[128,1024]{1,0:T(8,128)(2,1)S(1)} %shard_map.58.refs_1_), channel_id=1, source_target_pairs={{0,1},{1,2},{2,3},{3,4},{4,5},{5,6},{6,7},{7,0},{8,9},{9,10},{10,1... | collective-permute-start | bytes 786440 | tf_op jit(solution)/shard_map/ppermute | solution.py:18
  60.9 12.3 %collective-permute-start.7 = (bf16[128,1024]{1,0:T(8,128)(2,1)S(1)}, bf16[128,1024]{1,0:T(8,128)(2,1)S(1)}, u32[]{:S(2)}, u32[]{:S(2)}) collective-permute-start(bf16[128,1024]{1,0:T(8,128)(2,1)S(1)} %shard_map.59.refs_2_), channel_id=1, source_target_pairs={{0,7},{1,0},{2,1},{3,2},{4,3},{5,4},{6,5},{7,6},{8,15},{9,8},{10,9... | collective-permute-start | bytes 786440 | tf_op jit(solution)/shard_map/ppermute | solution.py:18
  66.0 12.1 %collective-permute-start.11 = (bf16[1168,128]{1,0:T(8,128)(2,1)S(1)}, bf16[1168,128]{1,0:T(8,128)(2,1)S(1)}, u32[]{:S(2)}, u32[]{:S(2)}) collective-permute-start(bf16[1168,128]{1,0:T(8,128)(2,1)S(1)} %collective-permute-done.10.refs_1_), channel_id=1, source_target_pairs={{0,1},{1,2},{2,3},{3,4},{4,5},{5,6},{6,7},{7,0},{8,9},{9,10},{10,1... | collective-permute-start | bytes 897032 | tf_op jit(solution)/shard_map/ppermute | solution.py:18
  68.0 12.1 %collective-permute-start.14 = (bf16[1168,128]{1,0:T(8,128)(2,1)S(1)}, bf16[1168,128]{1,0:T(8,128)(2,1)S(1)}, u32[]{:S(2)}, u32[]{:S(2)}) collective-permute-start(bf16[1168,128]{1,0:T(8,128)(2,1)S(1)} %collective-permute-done.13.refs_4_), channel_id=1, source_target_pairs={{0,7},{1,0},{2,1},{3,2},{4,3},{5,4},{6,5},{7,6},{8,15},{9,8},{10,9... | collective-permute-start | bytes 897032 | tf_op jit(solution)/shard_map/ppermute | solution.py:18
  74.5 27.2 %collective-permute-start.9 = (bf16[256,1024]{1,0:T(8,128)(2,1)S(1)}, bf16[256,1024]{1,0:T(8,128)(2,1)S(1)}, u32[]{:S(2)}, u32[]{:S(2)}) collective-permute-start(bf16[256,1024]{1,0:T(8,128)(2,1)S(1)} %get-tuple-element.14.refs_9_), channel_id=1, source_target_pairs={{0,8},{8,16},{16,24},{24,32},{32,40},{40,48},{48,56},{56,64},{64,7... | collective-permute-start | bytes 1572872 | tf_op jit(solution)/shard_map/ppermute | solution.py:18
  78.2 12.9 %collective-permute-start.12 = (bf16[1168,128]{1,0:T(8,128)(2,1)S(1)}, bf16[1168,128]{1,0:T(8,128)(2,1)S(1)}, u32[]{:S(2)}, u32[]{:S(2)}) collective-permute-start(bf16[1168,128]{1,0:T(8,128)(2,1)S(1)} %collective-permute-done.11.refs_2_), channel_id=1, source_target_pairs={{0,1},{1,2},{2,3},{3,4},{4,5},{5,6},{6,7},{7,0},{8,9},{9,10},{10,1... | collective-permute-start | bytes 897032 | tf_op jit(solution)/shard_map/ppermute | solution.py:18
  80.1 12.9 %collective-permute-start.15 = (bf16[1168,128]{1,0:T(8,128)(2,1)S(1)}, bf16[1168,128]{1,0:T(8,128)(2,1)S(1)}, u32[]{:S(2)}, u32[]{:S(2)}) collective-permute-start(bf16[1168,128]{1,0:T(8,128)(2,1)S(1)} %collective-permute-done.14.refs_5_), channel_id=1, source_target_pairs={{0,7},{1,0},{2,1},{3,2},{4,3},{5,4},{6,5},{7,6},{8,15},{9,8},{10,9... | collective-permute-start | bytes 897032 | tf_op jit(solution)/shard_map/ppermute | solution.py:18
  91.1 9.1 %collective-permute-start.16 = (bf16[592,128]{1,0:T(8,128)(2,1)S(1)}, bf16[592,128]{1,0:T(8,128)(2,1)S(1)}, u32[]{:S(2)}, u32[]{:S(2)}) collective-permute-start(bf16[592,128]{1,0:T(8,128)(2,1)S(1)} %shard_map.63), channel_id=1, source_target_pairs={{0,1},{1,2},{2,3},{3,4},{4,5},{5,6},{6,7},{7,0},{8,9},{9,10},{10,1... | collective-permute-start | bytes 454664 | tf_op jit(solution)/shard_map/ppermute | solution.py:18
  93.0 11.8 %collective-permute-start.17 = (bf16[576,128]{1,0:T(8,128)(2,1)S(1)}, bf16[576,128]{1,0:T(8,128)(2,1)S(1)}, u32[]{:S(2)}, u32[]{:S(2)}) collective-permute-start(bf16[576,128]{1,0:T(8,128)(2,1)S(1)} %shard_map.65), channel_id=1, source_target_pairs={{0,7},{1,0},{2,1},{3,2},{4,3},{5,4},{6,5},{7,6},{8,15},{9,8},{10,9... | collective-permute-start | bytes 442376 | tf_op jit(solution)/shard_map/ppermute | solution.py:18
  102.9 9.2 %collective-permute-start.19 = (bf16[144,1024]{1,0:T(8,128)(2,1)S(1)}, bf16[144,1024]{1,0:T(8,128)(2,1)S(1)}, u32[]{:S(2)}, u32[]{:S(2)}) collective-permute-start(bf16[144,1024]{1,0:T(8,128)(2,1)S(1)} %shard_map.66.refs_12_.refs_6_), channel_id=1, source_target_pairs={{0,504},{8,0},{16,8},{24,16},{32,24},{40,32},{48,40},{56,48},{64,5... | collective-permute-start | bytes 884744 | tf_op jit(solution)/shard_map/ppermute | solution.py:18
  110.1 9.1 %collective-permute-start.18 = (bf16[272,1024]{1,0:T(8,128)(2,1)S(1)}, bf16[272,1024]{1,0:T(8,128)(2,1)S(1)}, u32[]{:S(2)}, u32[]{:S(2)}) collective-permute-start(bf16[272,1024]{1,0:T(8,128)(2,1)S(1)} %shard_map.68.refs_6_), channel_id=1, source_target_pairs={{0,504},{8,0},{16,8},{24,16},{32,24},{40,32},{48,40},{56,48},{64,5... | collective-permute-start | bytes 1671176 | tf_op jit(solution)/shard_map/ppermute | solution.py:18
  113.6 5.6 %copy-start.1 = (bf16[2,128,1024]{2,1,0:T(8,128)(2,1)S(1)}, bf16[2,128,1024]{2,1,0:T(8,128)(2,1)}, u32[]{:S(2)}) copy-start(bf16[2,128,1024]{2,1,0:T(8,128)(2,1)} %refs_6_.1) | copy-start | bytes 1572868
  113.6 18.0 %collective-permute-start.20 = (bf16[144,1024]{1,0:T(8,128)(2,1)S(1)}, bf16[144,1024]{1,0:T(8,128)(2,1)S(1)}, u32[]{:S(2)}, u32[]{:S(2)}) collective-permute-start(bf16[144,1024]{1,0:T(8,128)(2,1)S(1)} %shard_map.69.refs_2_), channel_id=1, source_target_pairs={{0,504},{8,0},{16,8},{24,16},{32,24},{40,32},{48,40},{56,48},{64,5... | collective-permute-start | bytes 884744 | tf_op jit(solution)/shard_map/ppermute | solution.py:18
  116.1 15.5 %collective-permute-start.21 = (bf16[128,1024]{1,0:T(8,128)(2,1)S(1)}, bf16[128,1024]{1,0:T(8,128)(2,1)S(1)}, u32[]{:S(2)}, u32[]{:S(2)}) collective-permute-start(bf16[128,1024]{1,0:T(8,128)(2,1)S(1)} %shard_map.70.refs_5_), channel_id=1, source_target_pairs={{0,496},{8,504},{16,0},{24,8},{32,16},{40,24},{48,32},{56,40},{64,... | collective-permute-start | bytes 786440 | tf_op jit(solution)/shard_map/ppermute | solution.py:18
  119.2 12.4 %copy-start.5 = (bf16[2,128]{1,0:T(2,128)(2,1)S(1)}, bf16[2,128]{1,0:T(2,128)(2,1)}, u32[]{:S(2)}) copy-start(bf16[2,128]{1,0:T(2,128)(2,1)} %refs_7_.1) | copy-start | bytes 1540

commit v5 on v4

--- a/solution.py
+++ b/solution.py
@@ -191,16 +191,6 @@
         after=(m,),
     )
 
-    def fourth(m_ref, l_ev, g_ref, out):
-        past = lax.axis_index("tm") < 2
-        own = m_ref[rows:, :]
-        out[:rows, :] = jnp.where(past, 0.0, by_symmetric(own, l_ev[...])).astype(BF16)
-        out[rows:, :] = jnp.zeros((TAIL, size), BF16)
-        out[rows:, :rows] = two_rows(jnp.where(past, 0.0, nt(g_ref[...], own)[0:1]))
-
-    (v,) = call(fourth, [m_in, l_even, g_all], [short], 2 * product)
-    v_in = hop(v, "tm", -1)
-
     def odds(*refs):
         last, b1_ref, b2_ref, own, g_ref = refs[n : n + 5]
         far_ref, head_ref, line_ref, l_od = refs[n + 5 :]
@@ -218,8 +208,18 @@
         l_arrays + [l_odd_last, b1_in, b2, trans, g_all],
         [wide, wide, line, whole],
         4 * product,
-        after=(v,),
-    )
+        after=(close,),
+    )
+
+    def fourth(m_ref, l_ev, g_ref, out):
+        past = lax.axis_index("tm") < 2
+        own = m_ref[rows:, :]
+        out[:rows, :] = jnp.where(past, 0.0, by_symmetric(own, l_ev[...])).astype(BF16)
+        out[rows:, :] = jnp.zeros((TAIL, size), BF16)
+        out[rows:, :rows] = two_rows(jnp.where(past, 0.0, nt(g_ref[...], own)[0:1]))
+
+    (v,) = call(fourth, [m_in, l_even, g_all], [short], 2 * product, after=(line_,))
+    v_in = hop(v, "tm", -1)
 
     def third(m_ref, even, odd, l_ev, l_od, g_ref, out):
         past = lax.axis_index("tm") < 1
@@ -237,6 +237,14 @@
     (w,) = call(third, [m_in, e_even, e_odd, l_even, l_odd, g_all], [long], 7 * product, after=(v,))
     w_in = hop(w, "tm", -1)
 
+    def fifth(m_ref, even, b4_ref):
+        own = m_ref[rows:, :]
+        past = lax.axis_index("tm") < 2
+        b4_ref[...] = jnp.where(past, own.astype(F32), nn(own, even[...])).astype(BF16)
+
+    (b4,) = call(fifth, [m_in, e_even], [panel], product, after=(w,))
+    b4_in = hop(b4, "tm", -2)
+
     def sixth(v_ref, close_ref, far_ref, line_ref, even, odd, m_ref):
         past = lax.axis_index("tm") < 1
         behind = far_ref[...] + nt(v_ref[:rows, :], odd[...])
@@ -246,22 +254,14 @@
         m_ref[rows:, :] = jnp.zeros((TAIL, size), BF16)
         m_ref[rows:, :rows] = two_rows(jnp.where(past, 0.0, row))
 
-    (u,) = call(sixth, [v_in, close, far, line_, e_even, e_odd], [short], 2 * product, after=(w,))
+    (u,) = call(sixth, [v_in, close, far, line_, e_even, e_odd], [short], 2 * product, after=(b4,))
     u_in = hop(u, "tm", -1)
-
-    def fifth(m_ref, even, b4_ref):
-        own = m_ref[rows:, :]
-        past = lax.axis_index("tm") < 2
-        b4_ref[...] = jnp.where(past, own.astype(F32), nn(own, even[...])).astype(BF16)
-
-    (b4,) = call(fifth, [m_in, e_even], [panel], product, after=(u,))
-    b4_in = hop(b4, "tm", -2)
 
     def seventh(w_ref, head_ref, even, odd, l_own, out):
         inner = head_ref[...] + nt(w_ref[:rows, :], odd[...])
         out[...] = (nt(inner.astype(BF16), even[...]) + l_own[0].astype(F32)).astype(BF16)
 
-    (l_first,) = call(seventh, [w_in, head, e_even, e_odd, spread], [panel], 2 * product, after=(b4,))
+    (l_first,) = call(seventh, [w_in, head, e_even, e_odd, spread], [panel], 2 * product, after=(u,))
 
     def eighth(w_ref, u_ref, b4_ref, line_ref, odd, l_ref, l_own, g_own, e_out, g_out, l_out):
         l_out[1] = (nt(u_ref[:rows, :], odd[...]) + l_own[1].astype(F32)).astype(BF16)

time: 134 us -> 140 us (1.045)
  the two profiles are of different devices: /device:TPU:30 before, /device:TPU:56 now
where the time goes in v5:
time: 140 us; the launch traced here: 139 us
  starting transfers between devices  76.1 us (54%)
  waiting for transfers between devices  44.7 us (32%)
  Pallas kernels  14.7 us (10%)
  local copies, waits for them, and re-layouts  2.74 us (2%)
    ppermute x22, starting transfers between devices, hop(): lax.ppermute(block, axis, [(i, (i + distance) % size) for i in range(size)])  76.1 us
    ppermute x22, waiting for transfers between devices, hop(): lax.ppermute(block, axis, [(i, (i + distance) % size) for i in range(size)])  44.7 us
    pallas_call x15, Pallas kernels, call(): pl.pallas_call(run, in_specs=[VMEM] * count + [HBM] * len(after), out_spe...  14.7 us
  transfers between devices with their start and end apart: 22, of which 7 were waited for; matrix products, arithmetic and copies ran while one was open for 0% of the time, Pallas kernels for 8%

profile of v5, /device:TPU:56, one launch (start us, length us, event | category | flops | bytes accessed | tf_op | source)
XLA Modules:
  0.0 139.2 jit_solution(6011709585831946414)
XLA Ops:
  0.6 10.9 %collective-permute-start.3 = (bf16[2,128,1024]{2,1,0:T(8,128)(2,1)}, bf16[2,128,1024]{2,1,0:T(8,128)(2,1)S(1)}, u32[]{:S(2)}, u32[]{:S(2)}) collective-permute-start(bf16[2,128,1024]{2,1,0:T(8,128)(2,1)} %refs_10_.1), channel_id=1, source_target_pairs={{0,7},{1,0},{2,1},{3,2},{4,3},{5,4},{6,5},{7,6},{8,15},{9,8},{10,9... | collective-permute-start | bytes 1572872 | tf_op jit(solution)/shard_map/ppermute | solution.py:18
  11.6 1.9 %collective-permute-start = (bf16[2,128,1024]{2,1,0:T(8,128)(2,1)}, bf16[2,128,1024]{2,1,0:T(8,128)(2,1)S(1)}, u32[]{:S(2)}, u32[]{:S(2)}) collective-permute-start(bf16[2,128,1024]{2,1,0:T(8,128)(2,1)} %refs_10_.1), channel_id=1, source_target_pairs={{0,1},{1,2},{2,3},{3,4},{4,5},{5,6},{6,7},{7,0},{8,9},{9,10},{10,1... | collective-permute-start | bytes 1572872 | tf_op jit(solution)/shard_map/ppermute | solution.py:18
  13.5 9.5 %collective-permute-done.3.refs_4_ = bf16[2,128,1024]{2,1,0:T(8,128)(2,1)S(1)} collective-permute-done((bf16[2,128,1024]{2,1,0:T(8,128)(2,1)}, bf16[2,128,1024]{2,1,0:T(8,128)(2,1)S(1)}, u32[]{:S(2)}, u32[]{:S(2)}) %collective-permute-start.3) | collective-permute-done | bytes 524320 | tf_op jit(solution)/shard_map/ppermute | solution.py:18
  23.1 5.5 %collective-permute-start.4 = (bf16[2,128,1024]{2,1,0:T(8,128)(2,1)S(1)}, bf16[2,128,1024]{2,1,0:T(8,128)(2,1)S(1)}, u32[]{:S(2)}, u32[]{:S(2)}) collective-permute-start(bf16[2,128,1024]{2,1,0:T(8,128)(2,1)S(1)} %collective-permute-done.3.refs_4_), channel_id=1, source_target_pairs={{0,7},{1,0},{2,1},{3,2},{4,3},{5,4},{6,5},{7,6},{8,15},{9,8},{10,9... | collective-permute-start | bytes 1572872 | tf_op jit(solution)/shard_map/ppermute | solution.py:18
  28.6 0.0 collective-permute-done.refs_1_
  28.6 1.9 %collective-permute-start.1 = (bf16[2,128,1024]{2,1,0:T(8,128)(2,1)S(1)}, bf16[2,128,1024]{2,1,0:T(8,128)(2,1)S(1)}, u32[]{:S(2)}, u32[]{:S(2)}) collective-permute-start(bf16[2,128,1024]{2,1,0:T(8,128)(2,1)S(1)} %collective-permute-done.refs_1_), channel_id=1, source_target_pairs={{0,1},{1,2},{2,3},{3,4},{4,5},{5,6},{6,7},{7,0},{8,9},{9,10},{10,1... | collective-permute-start | bytes 1572872 | tf_op jit(solution)/shard_map/ppermute | solution.py:18
  30.5 8.4 %collective-permute-done.4.refs_5_ = bf16[2,128,1024]{2,1,0:T(8,128)(2,1)S(1)} collective-permute-done((bf16[2,128,1024]{2,1,0:T(8,128)(2,1)S(1)}, bf16[2,128,1024]{2,1,0:T(8,128)(2,1)S(1)}, u32[]{:S(2)}, u32[]{:S(2)}) %collective-permute-start.4) | collective-permute-done | bytes 524320 | tf_op jit(solution)/shard_map/ppermute | solution.py:18
  38.9 5.6 %collective-permute-start.5 = (bf16[2,128,1024]{2,1,0:T(8,128)(2,1)S(1)}, bf16[2,128,1024]{2,1,0:T(8,128)(2,1)S(1)}, u32[]{:S(2)}, u32[]{:S(2)}) collective-permute-start(bf16[2,128,1024]{2,1,0:T(8,128)(2,1)S(1)} %collective-permute-done.4.refs_5_), channel_id=1, source_target_pairs={{0,7},{1,0},{2,1},{3,2},{4,3},{5,4},{6,5},{7,6},{8,15},{9,8},{10,9... | collective-permute-start | bytes 1572872 | tf_op jit(solution)/shard_map/ppermute | solution.py:18
  44.5 0.0 collective-permute-done.1.refs_2_
  44.5 1.9 %collective-permute-start.2 = (bf16[2,128,1024]{2,1,0:T(8,128)(2,1)S(1)}, bf16[2,128,1024]{2,1,0:T(8,128)(2,1)S(1)}, u32[]{:S(2)}, u32[]{:S(2)}) collective-permute-start(bf16[2,128,1024]{2,1,0:T(8,128)(2,1)S(1)} %collective-permute-done.1.refs_2_), channel_id=1, source_target_pairs={{0,1},{1,2},{2,3},{3,4},{4,5},{5,6},{6,7},{7,0},{8,9},{9,10},{10,1... | collective-permute-start | bytes 1572872 | tf_op jit(solution)/shard_map/ppermute | solution.py:18
  46.4 0.0 copy-start
  46.4 1.0 copy-done
  47.4 0.7 copy-done.4
  48.1 0.2 shard_map.62.refs_0_
  48.3 1.9 %collective-permute-start.10 = (bf16[1168,128]{1,0:T(8,128)(2,1)S(1)}, bf16[1168,128]{1,0:T(8,128)(2,1)S(1)}, u32[]{:S(2)}, u32[]{:S(2)}) collective-permute-start(bf16[1168,128]{1,0:T(8,128)(2,1)S(1)} %shard_map.62.refs_0_), channel_id=1, source_target_pairs={{0,1},{1,2},{2,3},{3,4},{4,5},{5,6},{6,7},{7,0},{8,9},{9,10},{10,1... | collective-permute-start | bytes 897032 | tf_op jit(solution)/shard_map/ppermute | solution.py:18
  50.2 5.1 %collective-permute-start.13 = (bf16[1168,128]{1,0:T(8,128)(2,1)S(1)}, bf16[1168,128]{1,0:T(8,128)(2,1)S(1)}, u32[]{:S(2)}, u32[]{:S(2)}) collective-permute-start(bf16[1168,128]{1,0:T(8,128)(2,1)S(1)} %shard_map.62.refs_0_), channel_id=1, source_target_pairs={{0,7},{1,0},{2,1},{3,2},{4,3},{5,4},{6,5},{7,6},{8,15},{9,8},{10,9... | collective-permute-start | bytes 897032 | tf_op jit(solution)/shard_map/ppermute | solution.py:18
  55.3 10.3 %collective-permute-done.10.refs_1_ = bf16[1168,128]{1,0:T(8,128)(2,1)S(1)} collective-permute-done((bf16[1168,128]{1,0:T(8,128)(2,1)S(1)}, bf16[1168,128]{1,0:T(8,128)(2,1)S(1)}, u32[]{:S(2)}, u32[]{:S(2)}) %collective-permute-start.10) | collective-permute-done | bytes 299040 | tf_op jit(solution)/shard_map/ppermute | solution.py:18
  65.7 1.9 %collective-permute-start.11 = (bf16[1168,128]{1,0:T(8,128)(2,1)S(1)}, bf16[1168,128]{1,0:T(8,128)(2,1)S(1)}, u32[]{:S(2)}, u32[]{:S(2)}) collective-permute-start(bf16[1168,128]{1,0:T(8,128)(2,1)S(1)} %collective-permute-done.10.refs_1_), channel_id=1, source_target_pairs={{0,1},{1,2},{2,3},{3,4},{4,5},{5,6},{6,7},{7,0},{8,9},{9,10},{10,1... | collective-permute-start | bytes 897032 | tf_op jit(solution)/shard_map/ppermute | solution.py:18
  67.6 5.1 %collective-permute-start.14 = (bf16[1168,128]{1,0:T(8,128)(2,1)S(1)}, bf16[1168,128]{1,0:T(8,128)(2,1)S(1)}, u32[]{:S(2)}, u32[]{:S(2)}) collective-permute-start(bf16[1168,128]{1,0:T(8,128)(2,1)S(1)} %collective-permute-done.13.refs_4_), channel_id=1, source_target_pairs={{0,7},{1,0},{2,1},{3,2},{4,3},{5,4},{6,5},{7,6},{8,15},{9,8},{10,9... | collective-permute-start | bytes 897032 | tf_op jit(solution)/shard_map/ppermute | solution.py:18
  72.7 0.0 copy-start.2
  72.7 1.0 copy-done.2
  73.8 1.9 %collective-permute-start.8 = (bf16[128,1024]{1,0:T(8,128)(2,1)S(1)}, bf16[128,1024]{1,0:T(8,128)(2,1)S(1)}, u32[]{:S(2)}, u32[]{:S(2)}) collective-permute-start(bf16[128,1024]{1,0:T(8,128)(2,1)S(1)} %shard_map.60), channel_id=1, source_target_pairs={{0,8},{8,16},{16,24},{24,32},{32,40},{40,48},{48,56},{56,64},{64,7... | collective-permute-start | bytes 786440 | tf_op jit(solution)/shard_map/ppermute | solution.py:18
  75.7 0.0 collective-permute-done.5.refs_0_.refs_6_
  75.8 1.9 %collective-permute-start.7 = (bf16[128,1024]{1,0:T(8,128)(2,1)S(1)}, bf16[128,1024]{1,0:T(8,128)(2,1)S(1)}, u32[]{:S(2)}, u32[]{:S(2)}) collective-permute-start(bf16[128,1024]{1,0:T(8,128)(2,1)S(1)} %shard_map.59.refs_2_), channel_id=1, source_target_pairs={{0,7},{1,0},{2,1},{3,2},{4,3},{5,4},{6,5},{7,6},{8,15},{9,8},{10,9... | collective-permute-start | bytes 786440 | tf_op jit(solution)/shard_map/ppermute | solution.py:18
  77.7 3.9 %collective-permute-start.6 = (bf16[128,1024]{1,0:T(8,128)(2,1)S(1)}, bf16[128,1024]{1,0:T(8,128)(2,1)S(1)}, u32[]{:S(2)}, u32[]{:S(2)}) collective-permute-start(bf16[128,1024]{1,0:T(8,128)(2,1)S(1)} %shard_map.58.refs_1_), channel_id=1, source_target_pairs={{0,1},{1,2},{2,3},{3,4},{4,5},{5,6},{6,7},{7,0},{8,9},{9,10},{10,1... | collective-permute-start | bytes 786440 | tf_op jit(solution)/shard_map/ppermute | solution.py:18
  81.7 1.9 %collective-permute-start.12 = (bf16[1168,128]{1,0:T(8,128)(2,1)S(1)}, bf16[1168,128]{1,0:T(8,128)(2,1)S(1)}, u32[]{:S(2)}, u32[]{:S(2)}) collective-permute-start(bf16[1168,128]{1,0:T(8,128)(2,1)S(1)} %collective-permute-done.11.refs_2_), channel_id=1, source_target_pairs={{0,1},{1,2},{2,3},{3,4},{4,5},{5,6},{6,7},{7,0},{8,9},{9,10},{10,1... | collective-permute-start | bytes 897032 | tf_op jit(solution)/shard_map/ppermute | solution.py:18
  83.6 5.1 %collective-permute-start.15 = (bf16[1168,128]{1,0:T(8,128)(2,1)S(1)}, bf16[1168,128]{1,0:T(8,128)(2,1)S(1)}, u32[]{:S(2)}, u32[]{:S(2)}) collective-permute-start(bf16[1168,128]{1,0:T(8,128)(2,1)S(1)} %collective-permute-done.14.refs_5_), channel_id=1, source_target_pairs={{0,7},{1,0},{2,1},{3,2},{4,3},{5,4},{6,5},{7,6},{8,15},{9,8},{10,9... | collective-permute-start | bytes 897032 | tf_op jit(solution)/shard_map/ppermute | solution.py:18
  88.8 1.2 collective-permute-done.6.refs_7_
  90.0 1.3 shard_map.61
  91.3 1.9 %collective-permute-start.9 = (bf16[256,1024]{1,0:T(8,128)(2,1)S(1)}, bf16[256,1024]{1,0:T(8,128)(2,1)S(1)}, u32[]{:S(2)}, u32[]{:S(2)}) collective-permute-start(bf16[256,1024]{1,0:T(8,128)(2,1)S(1)} %get-tuple-element.14.refs_9_), channel_id=1, source_target_pairs={{0,8},{8,16},{16,24},{24,32},{32,40},{40,48},{48,56},{56,64},{64,7... | collective-permute-start | bytes 1572872 | tf_op jit(solution)/shard_map/ppermute | solution.py:18
  93.2 3.0 %collective-permute-done.12.refs_0_.refs_3_ = bf16[1168,128]{1,0:T(8,128)(2,1)S(1)} collective-permute-done((bf16[1168,128]{1,0:T(8,128)(2,1)S(1)}, bf16[1168,128]{1,0:T(8,128)(2,1)S(1)}, u32[]{:S(2)}, u32[]{:S(2)}) %collective-permute-start.12) | collective-permute-done | bytes 299040 | tf_op jit(solution)/shard_map/ppermute | solution.py:18
  96.3 2.4 %collective-permute-start.16 = (bf16[592,128]{1,0:T(8,128)(2,1)S(1)}, bf16[592,128]{1,0:T(8,128)(2,1)S(1)}, u32[]{:S(2)}, u32[]{:S(2)}) collective-permute-start(bf16[592,128]{1,0:T(8,128)(2,1)S(1)} %shard_map.63), channel_id=1, source_target_pairs={{0,1},{1,2},{2,3},{3,4},{4,5},{5,6},{6,7},{7,0},{8,9},{9,10},{10,1... | collective-permute-start | bytes 454664 | tf_op jit(solution)/shard_map/ppermute | solution.py:18
  98.7 4.6 %collective-permute-start.17 = (bf16[576,128]{1,0:T(8,128)(2,1)S(1)}, bf16[576,128]{1,0:T(8,128)(2,1)S(1)}, u32[]{:S(2)}, u32[]{:S(2)}) collective-permute-start(bf16[576,128]{1,0:T(8,128)(2,1)S(1)} %shard_map.65), channel_id=1, source_target_pairs={{0,7},{1,0},{2,1},{3,2},{4,3},{5,4},{6,5},{7,6},{8,15},{9,8},{10,9... | collective-permute-start | bytes 442376 | tf_op jit(solution)/shard_map/ppermute | solution.py:18
  103.4 1.8 %collective-permute-done.16.refs_7_ = bf16[592,128]{1,0:T(8,128)(2,1)S(1)} collective-permute-done((bf16[592,128]{1,0:T(8,128)(2,1)S(1)}, bf16[592,128]{1,0:T(8,128)(2,1)S(1)}, u32[]{:S(2)}, u32[]{:S(2)}) %collective-permute-start.16) | collective-permute-done | bytes 151584 | tf_op jit(solution)/shard_map/ppermute | solution.py:18
  105.1 1.5 %shard_map.64 = (f32[128,1024]{1,0:T(8,128)S(1)}, bf16[1024,1024]{1,0:T(8,128)(2,1)S(1)}, bf16[16,1024]{1,0:T(8,128)(2,1)S(1)}) custom-call(bf16[1168,128]{1,0:T(8,128)(2,1)S(1)} %shard_map.62.refs_0_, bf16[1168,128]{1,0:T(8,128)(2,1)S(1)} %collective-permute-done.10.refs_1_, bf16[1168,128]{1,0:T(8,128)(2,1)S(1)} %collective-permute-done.11.refs_2_, ...), custom_call_target="tpu_custom_call" | custom-call | flops 536870912 | bytes 1048576 | tf_op jit(solution)/shard_map/pallas_call | solution.py:43
  106.7 1.9 %shard_map.66 = (f32[128,1024]{1,0:T(8,128)S(1)}, f32[128,1024]{1,0:T(8,128)S(1)}, f32[8,128]{1,0:T(8,128)S(1)}, bf16[1024,1024]{1,0:T(8,128)(2,1)S(1)}) custom-call(bf16[1168,128]{1,0:T(8,128)(2,1)S(1)} %shard_map.62.refs_0_, bf16[1168,128]{1,0:T(8,128)(2,1)S(1)} %collective-permute-done.10.refs_1_, bf16[1168,128]{1,0:T(8,128)(2,1)S(1)} %collective-permute-done.11.refs_2_, ...), custom_call_target="tpu_custom_call" | custom-call | flops 1073741824 | bytes 1048576 | tf_op jit(solution)/shard_map/pallas_call | solution.py:43
  108.6 1.2 shard_map.67.refs_6_
  109.7 1.9 %collective-permute-start.19 = (bf16[144,1024]{1,0:T(8,128)(2,1)S(1)}, bf16[144,1024]{1,0:T(8,128)(2,1)S(1)}, u32[]{:S(2)}, u32[]{:S(2)}) collective-permute-start(bf16[144,1024]{1,0:T(8,128)(2,1)S(1)} %shard_map.67.refs_6_), channel_id=1, source_target_pairs={{0,504},{8,0},{16,8},{24,16},{32,24},{40,32},{48,40},{56,48},{64,5... | collective-permute-start | bytes 884744 | tf_op jit(solution)/shard_map/ppermute | solution.py:18
  111.7 3.4 %shard_map.68.refs_2_ = bf16[272,1024]{1,0:T(8,128)(2,1)S(1)} custom-call(bf16[256,1024]{1,0:T(8,128)(2,1)S(1)} %collective-permute-done.9.refs_0_, bf16[1024,1024]{1,0:T(8,128)(2,1)S(1)} %get-tuple-element.15.refs_1_.refs_4_.refs_2_, bf16[1024,1024]{1,0:T(8,128)(2,1)S(1)} %get-tuple-element.16.refs_2_.refs_5_.refs_3_.refs_4_, ...), custom_call_target="tpu_custom_call" | custom-call | flops 1879048192 | bytes 1048576 | tf_op jit(solution)/shard_map/pallas_call | solution.py:43
  115.1 3.3 %collective-permute-start.18 = (bf16[272,1024]{1,0:T(8,128)(2,1)S(1)}, bf16[272,1024]{1,0:T(8,128)(2,1)S(1)}, u32[]{:S(2)}, u32[]{:S(2)}) collective-permute-start(bf16[272,1024]{1,0:T(8,128)(2,1)S(1)} %shard_map.68.refs_2_), channel_id=1, source_target_pairs={{0,504},{8,0},{16,8},{24,16},{32,24},{40,32},{48,40},{56,48},{64,5... | collective-permute-start | bytes 1671176 | tf_op jit(solution)/shard_map/ppermute | solution.py:18
  118.4 0.5 shard_map.69.refs_6_
  118.9 0.0 copy-start.1
  118.9 1.5 %shard_map.70.refs_5_ = bf16[144,1024]{1,0:T(8,128)(2,1)S(1)} custom-call(bf16[144,1024]{1,0:T(8,128)(2,1)S(1)} %collective-permute-done.19.refs_0_, f32[128,1024]{1,0:T(8,128)S(1)} %get-tuple-element.20.refs_12_.refs_1_, f32[128,1024]{1,0:T(8,128)S(1)} %get-tuple-element.23.refs_2_, f32[8,128]{1,0:T(8,128)S(1)} %get-tuple-element.22.refs_3_, ...), custom_call_target="tpu_custom_call" | custom-call | flops 536870912 | bytes 1048576 | tf_op jit(solution)/shard_map/pallas_call | solution.py:43
  120.4 2.0 %collective-permute-start.20 = (bf16[144,1024]{1,0:T(8,128)(2,1)S(1)}, bf16[144,1024]{1,0:T(8,128)(2,1)S(1)}, u32[]{:S(2)}, u32[]{:S(2)}) collective-permute-start(bf16[144,1024]{1,0:T(8,128)(2,1)S(1)} %shard_map.70.refs_5_), channel_id=1, source_target_pairs={{0,504},{8,0},{16,8},{24,16},{32,24},{40,32},{48,40},{56,48},{64,5... | collective-permute-start | bytes 884744 | tf_op jit(solution)/shard_map/ppermute | solution.py:18
  122.4 3.2 %collective-permute-start.21 = (bf16[128,1024]{1,0:T(8,128)(2,1)S(1)}, bf16[128,1024]{1,0:T(8,128)(2,1)S(1)}, u32[]{:S(2)}, u32[]{:S(2)}) collective-permute-start(bf16[128,1024]{1,0:T(8,128)(2,1)S(1)} %shard_map.69.refs_6_), channel_id=1, source_target_pairs={{0,496},{8,504},{16,0},{24,8},{32,16},{40,24},{48,32},{56,40},{64,... | collective-permute-start | bytes 786440 | tf_op jit(solution)/shard_map/ppermute | solution.py:18
  125.6 1.5 %shard_map.71.refs_5_ = bf16[128,1024]{1,0:T(8,128)(2,1)S(1)} custom-call(bf16[272,1024]{1,0:T(8,128)(2,1)S(1)} %collective-permute-done.18.refs_0_, f32[128,1024]{1,0:T(8,128)S(1)} %get-tuple-element.24.refs_1_, bf16[1024,1024]{1,0:T(8,128)(2,1)S(1)} %get-tuple-element.15.refs_1_.refs_4_.refs_2_, ...), custom_call_target="tpu_custom_call" | custom-call | flops 536870912 | bytes 1048576 | tf_op jit(solution)/shard_map/pallas_call | solution.py:43
  127.1 10.4 %collective-permute-done.21.refs_2_ = bf16[128,1024]{1,0:T(8,128)(2,1)S(1)} collective-permute-done((bf16[128,1024]{1,0:T(8,128)(2,1)S(1)}, bf16[128,1024]{1,0:T(8,128)(2,1)S(1)}, u32[]{:S(2)}, u32[]{:S(2)}) %collective-permute-start.21) | collective-permute-done | bytes 262176 | tf_op jit(solution)/shard_map/ppermute | solution.py:18
  137.5 1.7 %shard_map.72 = (bf16[2,128,1024]{2,1,0:T(8,128)(2,1)}, bf16[2,128]{1,0:T(2,128)(2,1)}, bf16[2,128,1024]{2,1,0:T(8,128)(2,1)}) custom-call(bf16[272,1024]{1,0:T(8,128)(2,1)S(1)} %collective-permute-done.18.refs_0_, bf16[144,1024]{1,0:T(8,128)(2,1)S(1)} %collective-permute-done.20.refs_1_, bf16[128,1024]{1,0:T(8,128)(2,1)S(1)} %collective-permute-done.21.refs_2_, ...), custom_call_target="tpu_custom_call" | custom-call | flops 268435456 | bytes 1048576 | tf_op jit(solution)/shard_map/pallas_call | solution.py:43
  (21 shorter events, 0.1 us)
Async XLA Ops:
  0.6 22.4 %collective-permute-start.3 = (bf16[2,128,1024]{2,1,0:T(8,128)(2,1)}, bf16[2,128,1024]{2,1,0:T(8,128)(2,1)S(1)}, u32[]{:S(2)}, u32[]{:S(2)}) collective-permute-start(bf16[2,128,1024]{2,1,0:T(8,128)(2,1)} %refs_10_.1), channel_id=1, source_target_pairs={{0,7},{1,0},{2,1},{3,2},{4,3},{5,4},{6,5},{7,6},{8,15},{9,8},{10,9... | collective-permute-start | bytes 1572872 | tf_op jit(solution)/shard_map/ppermute | solution.py:18
  11.6 17.0 %collective-permute-start = (bf16[2,128,1024]{2,1,0:T(8,128)(2,1)}, bf16[2,128,1024]{2,1,0:T(8,128)(2,1)S(1)}, u32[]{:S(2)}, u32[]{:S(2)}) collective-permute-start(bf16[2,128,1024]{2,1,0:T(8,128)(2,1)} %refs_10_.1), channel_id=1, source_target_pairs={{0,1},{1,2},{2,3},{3,4},{4,5},{5,6},{6,7},{7,0},{8,9},{9,10},{10,1... | collective-permute-start | bytes 1572872 | tf_op jit(solution)/shard_map/ppermute | solution.py:18
  23.1 15.8 %collective-permute-start.4 = (bf16[2,128,1024]{2,1,0:T(8,128)(2,1)S(1)}, bf16[2,128,1024]{2,1,0:T(8,128)(2,1)S(1)}, u32[]{:S(2)}, u32[]{:S(2)}) collective-permute-start(bf16[2,128,1024]{2,1,0:T(8,128)(2,1)S(1)} %collective-permute-done.3.refs_4_), channel_id=1, source_target_pairs={{0,7},{1,0},{2,1},{3,2},{4,3},{5,4},{6,5},{7,6},{8,15},{9,8},{10,9... | collective-permute-start | bytes 1572872 | tf_op jit(solution)/shard_map/ppermute | solution.py:18
  28.6 15.9 %collective-permute-start.1 = (bf16[2,128,1024]{2,1,0:T(8,128)(2,1)S(1)}, bf16[2,128,1024]{2,1,0:T(8,128)(2,1)S(1)}, u32[]{:S(2)}, u32[]{:S(2)}) collective-permute-start(bf16[2,128,1024]{2,1,0:T(8,128)(2,1)S(1)} %collective-permute-done.refs_1_), channel_id=1, source_target_pairs={{0,1},{1,2},{2,3},{3,4},{4,5},{5,6},{6,7},{7,0},{8,9},{9,10},{10,1... | collective-permute-start | bytes 1572872 | tf_op jit(solution)/shard_map/ppermute | solution.py:18
  38.9 36.9 %collective-permute-start.5 = (bf16[2,128,1024]{2,1,0:T(8,128)(2,1)S(1)}, bf16[2,128,1024]{2,1,0:T(8,128)(2,1)S(1)}, u32[]{:S(2)}, u32[]{:S(2)}) collective-permute-start(bf16[2,128,1024]{2,1,0:T(8,128)(2,1)S(1)} %collective-permute-done.4.refs_5_), channel_id=1, source_target_pairs={{0,7},{1,0},{2,1},{3,2},{4,3},{5,4},{6,5},{7,6},{8,15},{9,8},{10,9... | collective-permute-start | bytes 1572872 | tf_op jit(solution)/shard_map/ppermute | solution.py:18
  44.5 33.2 %collective-permute-start.2 = (bf16[2,128,1024]{2,1,0:T(8,128)(2,1)S(1)}, bf16[2,128,1024]{2,1,0:T(8,128)(2,1)S(1)}, u32[]{:S(2)}, u32[]{:S(2)}) collective-permute-start(bf16[2,128,1024]{2,1,0:T(8,128)(2,1)S(1)} %collective-permute-done.1.refs_2_), channel_id=1, source_target_pairs={{0,1},{1,2},{2,3},{3,4},{4,5},{5,6},{6,7},{7,0},{8,9},{9,10},{10,1... | collective-permute-start | bytes 1572872 | tf_op jit(solution)/shard_map/ppermute | solution.py:18
  46.4 1.0 copy-start
  47.4 0.7 copy-start.4
  48.1 41.9 %copy-start.3 = (bf16[2,128,1024]{2,1,0:T(8,128)(2,1)S(1)}, bf16[2,128,1024]{2,1,0:T(8,128)(2,1)}, u32[]{:S(2)}) copy-start(bf16[2,128,1024]{2,1,0:T(8,128)(2,1)} %refs_10_.1) | copy-start | bytes 1572868
  48.3 17.4 %collective-permute-start.10 = (bf16[1168,128]{1,0:T(8,128)(2,1)S(1)}, bf16[1168,128]{1,0:T(8,128)(2,1)S(1)}, u32[]{:S(2)}, u32[]{:S(2)}) collective-permute-start(bf16[1168,128]{1,0:T(8,128)(2,1)S(1)} %shard_map.62.refs_0_), channel_id=1, source_target_pairs={{0,1},{1,2},{2,3},{3,4},{4,5},{5,6},{6,7},{7,0},{8,9},{9,10},{10,1... | collective-permute-start | bytes 897032 | tf_op jit(solution)/shard_map/ppermute | solution.py:18
  50.2 17.4 %collective-permute-start.13 = (bf16[1168,128]{1,0:T(8,128)(2,1)S(1)}, bf16[1168,128]{1,0:T(8,128)(2,1)S(1)}, u32[]{:S(2)}, u32[]{:S(2)}) collective-permute-start(bf16[1168,128]{1,0:T(8,128)(2,1)S(1)} %shard_map.62.refs_0_), channel_id=1, source_target_pairs={{0,7},{1,0},{2,1},{3,2},{4,3},{5,4},{6,5},{7,6},{8,15},{9,8},{10,9... | collective-permute-start | bytes 897032 | tf_op jit(solution)/shard_map/ppermute | solution.py:18
  65.7 16.0 %collective-permute-start.11 = (bf16[1168,128]{1,0:T(8,128)(2,1)S(1)}, bf16[1168,128]{1,0:T(8,128)(2,1)S(1)}, u32[]{:S(2)}, u32[]{:S(2)}) collective-permute-start(bf16[1168,128]{1,0:T(8,128)(2,1)S(1)} %collective-permute-done.10.refs_1_), channel_id=1, source_target_pairs={{0,1},{1,2},{2,3},{3,4},{4,5},{5,6},{6,7},{7,0},{8,9},{9,10},{10,1... | collective-permute-start | bytes 897032 | tf_op jit(solution)/shard_map/ppermute | solution.py:18
  67.6 16.0 %collective-permute-start.14 = (bf16[1168,128]{1,0:T(8,128)(2,1)S(1)}, bf16[1168,128]{1,0:T(8,128)(2,1)S(1)}, u32[]{:S(2)}, u32[]{:S(2)}) collective-permute-start(bf16[1168,128]{1,0:T(8,128)(2,1)S(1)} %collective-permute-done.13.refs_4_), channel_id=1, source_target_pairs={{0,7},{1,0},{2,1},{3,2},{4,3},{5,4},{6,5},{7,6},{8,15},{9,8},{10,9... | collective-permute-start | bytes 897032 | tf_op jit(solution)/shard_map/ppermute | solution.py:18
  72.7 1.0 copy-start.2
  73.8 15.0 %collective-permute-start.8 = (bf16[128,1024]{1,0:T(8,128)(2,1)S(1)}, bf16[128,1024]{1,0:T(8,128)(2,1)S(1)}, u32[]{:S(2)}, u32[]{:S(2)}) collective-permute-start(bf16[128,1024]{1,0:T(8,128)(2,1)S(1)} %shard_map.60), channel_id=1, source_target_pairs={{0,8},{8,16},{16,24},{24,32},{32,40},{40,48},{48,56},{56,64},{64,7... | collective-permute-start | bytes 786440 | tf_op jit(solution)/shard_map/ppermute | solution.py:18
  75.8 13.0 %collective-permute-start.7 = (bf16[128,1024]{1,0:T(8,128)(2,1)S(1)}, bf16[128,1024]{1,0:T(8,128)(2,1)S(1)}, u32[]{:S(2)}, u32[]{:S(2)}) collective-permute-start(bf16[128,1024]{1,0:T(8,128)(2,1)S(1)} %shard_map.59.refs_2_), channel_id=1, source_target_pairs={{0,7},{1,0},{2,1},{3,2},{4,3},{5,4},{6,5},{7,6},{8,15},{9,8},{10,9... | collective-permute-start | bytes 786440 | tf_op jit(solution)/shard_map/ppermute | solution.py:18
  77.7 12.3 %collective-permute-start.6 = (bf16[128,1024]{1,0:T(8,128)(2,1)S(1)}, bf16[128,1024]{1,0:T(8,128)(2,1)S(1)}, u32[]{:S(2)}, u32[]{:S(2)}) collective-permute-start(bf16[128,1024]{1,0:T(8,128)(2,1)S(1)} %shard_map.58.refs_1_), channel_id=1, source_target_pairs={{0,1},{1,2},{2,3},{3,4},{4,5},{5,6},{6,7},{7,0},{8,9},{9,10},{10,1... | collective-permute-start | bytes 786440 | tf_op jit(solution)/shard_map/ppermute | solution.py:18
  81.7 14.6 %collective-permute-start.12 = (bf16[1168,128]{1,0:T(8,128)(2,1)S(1)}, bf16[1168,128]{1,0:T(8,128)(2,1)S(1)}, u32[]{:S(2)}, u32[]{:S(2)}) collective-permute-start(bf16[1168,128]{1,0:T(8,128)(2,1)S(1)} %collective-permute-done.11.refs_2_), channel_id=1, source_target_pairs={{0,1},{1,2},{2,3},{3,4},{4,5},{5,6},{6,7},{7,0},{8,9},{9,10},{10,1... | collective-permute-start | bytes 897032 | tf_op jit(solution)/shard_map/ppermute | solution.py:18
  83.6 15.1 %collective-permute-start.15 = (bf16[1168,128]{1,0:T(8,128)(2,1)S(1)}, bf16[1168,128]{1,0:T(8,128)(2,1)S(1)}, u32[]{:S(2)}, u32[]{:S(2)}) collective-permute-start(bf16[1168,128]{1,0:T(8,128)(2,1)S(1)} %collective-permute-done.14.refs_5_), channel_id=1, source_target_pairs={{0,7},{1,0},{2,1},{3,2},{4,3},{5,4},{6,5},{7,6},{8,15},{9,8},{10,9... | collective-permute-start | bytes 897032 | tf_op jit(solution)/shard_map/ppermute | solution.py:18
  91.3 17.3 %collective-permute-start.9 = (bf16[256,1024]{1,0:T(8,128)(2,1)S(1)}, bf16[256,1024]{1,0:T(8,128)(2,1)S(1)}, u32[]{:S(2)}, u32[]{:S(2)}) collective-permute-start(bf16[256,1024]{1,0:T(8,128)(2,1)S(1)} %get-tuple-element.14.refs_9_), channel_id=1, source_target_pairs={{0,8},{8,16},{16,24},{24,32},{32,40},{40,48},{48,56},{56,64},{64,7... | collective-permute-start | bytes 1572872 | tf_op jit(solution)/shard_map/ppermute | solution.py:18
  96.3 8.9 %collective-permute-start.16 = (bf16[592,128]{1,0:T(8,128)(2,1)S(1)}, bf16[592,128]{1,0:T(8,128)(2,1)S(1)}, u32[]{:S(2)}, u32[]{:S(2)}) collective-permute-start(bf16[592,128]{1,0:T(8,128)(2,1)S(1)} %shard_map.63), channel_id=1, source_target_pairs={{0,1},{1,2},{2,3},{3,4},{4,5},{5,6},{6,7},{7,0},{8,9},{9,10},{10,1... | collective-permute-start | bytes 454664 | tf_op jit(solution)/shard_map/ppermute | solution.py:18
  98.7 8.0 %collective-permute-start.17 = (bf16[576,128]{1,0:T(8,128)(2,1)S(1)}, bf16[576,128]{1,0:T(8,128)(2,1)S(1)}, u32[]{:S(2)}, u32[]{:S(2)}) collective-permute-start(bf16[576,128]{1,0:T(8,128)(2,1)S(1)} %shard_map.65), channel_id=1, source_target_pairs={{0,7},{1,0},{2,1},{3,2},{4,3},{5,4},{6,5},{7,6},{8,15},{9,8},{10,9... | collective-permute-start | bytes 442376 | tf_op jit(solution)/shard_map/ppermute | solution.py:18
  109.7 9.1 %collective-permute-start.19 = (bf16[144,1024]{1,0:T(8,128)(2,1)S(1)}, bf16[144,1024]{1,0:T(8,128)(2,1)S(1)}, u32[]{:S(2)}, u32[]{:S(2)}) collective-permute-start(bf16[144,1024]{1,0:T(8,128)(2,1)S(1)} %shard_map.67.refs_6_), channel_id=1, source_target_pairs={{0,504},{8,0},{16,8},{24,16},{32,24},{40,32},{48,40},{56,48},{64,5... | collective-permute-start | bytes 884744 | tf_op jit(solution)/shard_map/ppermute | solution.py:18
  115.1 10.5 %collective-permute-start.18 = (bf16[272,1024]{1,0:T(8,128)(2,1)S(1)}, bf16[272,1024]{1,0:T(8,128)(2,1)S(1)}, u32[]{:S(2)}, u32[]{:S(2)}) collective-permute-start(bf16[272,1024]{1,0:T(8,128)(2,1)S(1)} %shard_map.68.refs_2_), channel_id=1, source_target_pairs={{0,504},{8,0},{16,8},{24,16},{32,24},{40,32},{48,40},{56,48},{64,5... | collective-permute-start | bytes 1671176 | tf_op jit(solution)/shard_map/ppermute | solution.py:18
  118.9 6.7 %copy-start.1 = (bf16[2,128,1024]{2,1,0:T(8,128)(2,1)S(1)}, bf16[2,128,1024]{2,1,0:T(8,128)(2,1)}, u32[]{:S(2)}) copy-start(bf16[2,128,1024]{2,1,0:T(8,128)(2,1)} %refs_6_.1) | copy-start | bytes 1572868
  120.4 17.1 %collective-permute-start.20 = (bf16[144,1024]{1,0:T(8,128)(2,1)S(1)}, bf16[144,1024]{1,0:T(8,128)(2,1)S(1)}, u32[]{:S(2)}, u32[]{:S(2)}) collective-permute-start(bf16[144,1024]{1,0:T(8,128)(2,1)S(1)} %shard_map.70.refs_5_), channel_id=1, source_target_pairs={{0,504},{8,0},{16,8},{24,16},{32,24},{40,32},{48,40},{56,48},{64,5... | collective-permute-start | bytes 884744 | tf_op jit(solution)/shard_map/ppermute | solution.py:18
  122.4 15.1 %collective-permute-start.21 = (bf16[128,1024]{1,0:T(8,128)(2,1)S(1)}, bf16[128,1024]{1,0:T(8,128)(2,1)S(1)}, u32[]{:S(2)}, u32[]{:S(2)}) collective-permute-start(bf16[128,1024]{1,0:T(8,128)(2,1)S(1)} %shard_map.69.refs_6_), channel_id=1, source_target_pairs={{0,496},{8,504},{16,0},{24,8},{32,16},{40,24},{48,32},{56,40},{64,... | collective-permute-start | bytes 786440 | tf_op jit(solution)/shard_map/ppermute | solution.py:18
